TPU v7x, 32 devices: a whole 2x2x4 slice. The times are simulated.
32 devices in a mesh: group: 4 (over y, x), bulk: 8 (over z, core).
Axes of the slice: x: 2, y: 2, z: 4, core: 2. Of those that a mesh axis runs over, the one named last changes fastest.
Arguments:
- right_sides: float32 [32, 65536], P(None, ('group', 'bulk')), may hold values from -6 to 6
- points: float32 [3, 65536], P(None, ('group', 'bulk')), may hold values from 0 to 4
- basis: float32 [256, 64, 256], P(('group', 'bulk')), may hold values from -0.375 to 0.375
- transfer: float32 [480, 64, 64], P(('group', 'bulk')), may hold values from -0.5 to 0.5
- skeleton: float32 [480, 3, 64], P(('group', 'bulk')), may hold values from 0 to 2
- near_list: int32 [256, 8], P(('group', 'bulk')), may hold values from 0 to 255, as said below
- near_count: int32 [256], P(('group', 'bulk')), may hold values from 0 to 8
- inter_list: int32 [480, 8], P(('group', 'bulk')), may hold values from 0 to 255, as said below
- inter_count: int32 [480], P(('group', 'bulk')), may hold values from 0 to 8
- upper_transfer: float32 [32, 64, 64], replicated, may hold values from -0.5 to 0.5
- upper_skeleton: float32 [32, 3, 64], replicated, may hold values from 0 to 2
- upper_list: int32 [32, 8], replicated, may hold values from 0 to 31, as said below
- upper_count: int32 [32], replicated, may hold values from 0 to 3, as said below
Outputs:
- product: float32 [32, 65536], P(None, ('group', 'bulk'))
Inputs may be any that keep to these rules, and one draw needn't show every extreme that they name: `near_list`: row t holds distinct leaves other than t at most 4 leaves away; only the first near_count[t] entries count, the rest are in range and are ignored. `inter_list`: A node's row holds distinct other nodes of its level, each of the first inter_count entries at most max(m // 2, 1) places away where m is the level's nodes on one device; only the first inter_count entries count, the rest are in range and are ignored. `upper_list`: row h holds distinct other heap nodes of h's level; at levels with more nodes than there are indices of group, they lie below the same ancestor at the level that has one node per index of group. Only the first upper_count entries count, the rest are in range and are ignored. `upper_count`: entries 0 and 1 are 0.
All inputs are finite; a program needn't handle non-finite values.
Results may differ from a plain program's by a relative error of at most 0.0003.
Values sent between devices are 32-bit elements; how exact they have to be, the bound alone decides.
No kernel may reach another device: no remote copies, remote signals or barrier semaphores. Data moves between devices by JAX's collectives and lax.ppermute only.
A program may use at most 128 MiB of HBM per device.

v0:
```python
import jax
import jax.numpy as jnp
from jax import lax
from jax.sharding import PartitionSpec as P

FULL_PRECISION = lax.Precision.HIGHEST
AMPLITUDE = 0.2
KERNEL_RATE = 2.0
SOFTENING = 0.01
NUGGET = 0.5


def extended_2(cells, sides, width):
    for axis, dim in sides:
        count = lax.axis_size(axis)
        ends = count - 1
        head = lax.slice_in_dim(cells, 0, width, axis=dim)
        tail = lax.slice_in_dim(cells, cells.shape[dim] - width, cells.shape[dim], axis=dim)
        cells = jnp.concatenate(
            [
                lax.ppermute(tail, axis, [(i, (i + 1) % count) for i in range(ends)]),
                cells,
                lax.ppermute(head, axis, [((i + 1) % count, i) for i in range(ends)]),
            ],
            axis=dim,
        )
    return cells


def matern(source_pts, target_pts):
    delta_x = source_pts[..., 0, :, None] - target_pts[..., 0, None, :]
    delta_y = source_pts[..., 1, :, None] - target_pts[..., 1, None, :]
    delta_z = source_pts[..., 2, :, None] - target_pts[..., 2, None, :]
    spread = jnp.sqrt(delta_x * delta_x + delta_y * delta_y + delta_z * delta_z + SOFTENING)
    scaled = KERNEL_RATE * spread
    return AMPLITUDE * (1.0 + scaled) * jnp.exp(-scaled)


def near_terms(own_points, own_rows, far_points, far_rows, weights):
    self_kernel = matern(own_points, own_points)
    result = (
        jnp.einsum("brq,bqp->brp", own_rows, self_kernel, precision=FULL_PRECISION)
        + NUGGET * own_rows
    )
    cross_kernel = matern(far_points, own_points[:, None])
    masked = far_rows * weights[:, :, None, None]
    return result + jnp.einsum("bnrq,bnqp->brp", masked, cross_kernel, precision=FULL_PRECISION)


def couple(lookup, positions, target_skeleton, counts):
    gathered = jnp.take(lookup, positions, axis=0, mode="clip")
    kernel = matern(gathered[:, :, :3], target_skeleton[:, None])
    active = (jnp.arange(positions.shape[1])[None, :] < counts[:, None]).astype(jnp.float32)
    weighted = gathered[:, :, 3:] * active[:, :, None, None]
    return jnp.einsum("nsri,nsij->nrj", weighted, kernel, precision=FULL_PRECISION)


def on_device(
    right_sides,
    points,
    basis,
    transfer,
    skeleton,
    near_list,
    near_count,
    inter_list,
    inter_count,
    upper_transfer,
    upper_skeleton,
    upper_list,
    upper_count,
):
    leaves = basis.shape[0]
    rank_size = basis.shape[1]
    leaf_size = basis.shape[2]
    rhs_count = right_sides.shape[0]
    near_slots = near_list.shape[1]
    slot_count = 2 * leaves - 1
    half_reach = leaves // 2
    devices = lax.axis_size(("group", "bulk"))
    device = lax.axis_index(("group", "bulk"))
    stacked_rows = jnp.concatenate([points, right_sides], axis=0)
    extended = extended_2(stacked_rows, ((("group", "bulk"), 1),), half_reach * leaf_size)
    lookup_rows = extended.reshape(3 + rhs_count, leaves + 2 * half_reach, leaf_size).transpose(
        1, 0, 2
    )
    near_positions = near_list - device * leaves + half_reach
    weights = (jnp.arange(near_slots)[None, :] < near_count[:, None]).astype(jnp.float32)
    block_leaves = min(4, leaves)

    def near_block(first_leaf):
        own_table = lax.dynamic_slice_in_dim(lookup_rows, first_leaf + half_reach, block_leaves, 0)
        source_ids = lax.dynamic_slice_in_dim(near_positions, first_leaf, block_leaves, 0)
        far_table = jnp.take(lookup_rows, source_ids, axis=0, mode="clip")
        block_weights = lax.dynamic_slice_in_dim(weights, first_leaf, block_leaves, 0)
        return near_terms(
            own_table[:, :3],
            own_table[:, 3:],
            far_table[:, :, :3],
            far_table[:, :, 3:],
            block_weights,
        )

    near_part = lax.map(near_block, jnp.arange(0, leaves, block_leaves, dtype=jnp.int32))
    near_part = near_part.reshape(leaves, rhs_count, leaf_size)
    leaf_rows = right_sides.reshape(rhs_count, leaves, leaf_size)
    coefficients = [jnp.einsum("rlp,lkp->lrk", leaf_rows, basis, precision=FULL_PRECISION)]
    level_total = leaves.bit_length()
    for level_index in range(level_total - 1):
        node_count = leaves >> level_index
        offset = 2 * leaves - 2 * node_count
        lifted = jnp.einsum(
            "nrk,nkq->nrq",
            coefficients[-1],
            transfer[offset : offset + node_count],
            precision=FULL_PRECISION,
        )
        coefficients.append(lifted.reshape(node_count // 2, 2, rhs_count, rank_size).sum(axis=1))
    root_transfer = transfer[slot_count - 1]
    root_term = jnp.dot(
        coefficients[-1][0],
        root_transfer,
        precision=FULL_PRECISION,
        preferred_element_type=jnp.float32,
    )
    joined = jnp.concatenate([skeleton, jnp.concatenate(coefficients, axis=0)], axis=1)
    beside_all = extended_2(joined, ((("group", "bulk"), 0),), slot_count)
    local_fields = []
    for level_index in range(level_total):
        node_count = leaves >> level_index
        offset = 2 * leaves - 2 * node_count
        source_ids = inter_list[offset : offset + node_count]
        target_skeleton = skeleton[offset : offset + node_count]
        owner_device = source_ids // node_count
        positions_here = (
            (owner_device - device + 1) * slot_count
            + offset
            + source_ids
            - owner_device * node_count
        )
        local_fields.append(
            couple(
                beside_all,
                positions_here,
                target_skeleton,
                inter_count[offset : offset + node_count],
            )
        )
    tree_depth = devices.bit_length() - 1
    heap_coefs = jnp.zeros((devices, rhs_count, rank_size), jnp.float32)
    all_roots = lax.all_gather(root_term[None], ("group", "bulk"), axis=0, tiled=True)
    level_coef = all_roots.reshape(-1, 2, rhs_count, rank_size).sum(axis=1)
    first_level = tree_depth - 1
    for level_index in range(first_level, 0, -1):
        heap_coefs = lax.dynamic_update_slice_in_dim(heap_coefs, level_coef, 1 << level_index, 0)
        if level_index > 1:
            lifted = jnp.einsum(
                "nrk,nkq->nrq",
                level_coef,
                upper_transfer[1 << level_index : 2 << level_index],
                precision=FULL_PRECISION,
            )
            level_coef = lifted.reshape(-1, 2, rhs_count, rank_size).sum(axis=1)
    ancestors = jnp.stack(
        [
            (devices + device) // (1 << tree_depth - level_index)
            for level_index in range(1, tree_depth)
        ]
    )
    upper_lookup = jnp.concatenate([upper_skeleton, heap_coefs], axis=1)
    path_fields = couple(
        upper_lookup,
        jnp.take(upper_list, ancestors, axis=0),
        jnp.take(upper_skeleton, ancestors, axis=0),
        jnp.take(upper_count, ancestors, axis=0),
    )
    downward = path_fields[0]
    for step_index in range(1, tree_depth - 1):
        child_transfer = jnp.take(upper_transfer, ancestors[step_index], axis=0)
        downward = path_fields[step_index] + jnp.dot(
            downward, child_transfer.T, precision=FULL_PRECISION, preferred_element_type=jnp.float32
        )
    incoming = jnp.dot(
        downward, root_transfer.T, precision=FULL_PRECISION, preferred_element_type=jnp.float32
    )
    local_fields[-1] = local_fields[-1] + incoming[None]
    for level_index in range(level_total - 2, -1, -1):
        node_count = leaves >> level_index
        offset = 2 * leaves - 2 * node_count
        parent = jnp.repeat(local_fields[level_index + 1], 2, axis=0)
        local_fields[level_index] = local_fields[level_index] + jnp.einsum(
            "nrq,nkq->nrk", parent, transfer[offset : offset + node_count], precision=FULL_PRECISION
        )
    far_part = jnp.einsum("lrk,lkp->rlp", local_fields[0], basis, precision=FULL_PRECISION)
    combined = far_part + near_part.transpose(1, 0, 2)
    return combined.reshape(rhs_count, leaves * leaf_size)


def solution(mesh):
    in_specs = (
        P(None, ("group", "bulk")),
        P(None, ("group", "bulk")),
        P(("group", "bulk"), None, None),
        P(("group", "bulk"), None, None),
        P(("group", "bulk"), None, None),
        P(("group", "bulk"), None),
        P(("group", "bulk")),
        P(("group", "bulk"), None),
        P(("group", "bulk")),
        P(),
        P(),
        P(),
        P(),
    )
    out_specs = P(None, ("group", "bulk"))
    return jax.shard_map(
        on_device, mesh=mesh, in_specs=in_specs, out_specs=out_specs, check_vma=False
    )
```

profile of v0, /device:TPU:0, one launch (start us, length us, event | category | flops | bytes accessed | tf_op | source)
XLA Modules:
  0.0 140.8 jit_solution(9403777817733503389)
XLA Ops:
  0.0 1.2 copy-done
  1.2 1.5 %fusion.173 = f32[8,32,64]{2,1,0:T(8,128)S(1)} fusion(f32[8,64,256]{2,1,0:T(8,128)S(1)} %copy-done, f32[4,8,8,256]{3,2,1,0:T(8,128)} %bitcast.226), kind=kOutput, calls=%fused_computation.217 | convolution fusion | flops 50331648 | bytes 851968 | tf_op jit(solution)/shard_map/rlp,lkp->lrk/dot_general | solution.py:107
  2.8 1.3 bitcast_reduce_fusion.2
  4.6 0.8 maximum_maximum_fusion
  5.4 3.1 %collective-permute-start = (f32[15,35,64]{2,1,0:T(8,128)}, f32[15,35,64]{2,1,0:T(8,128)}, u32[]{:S(2)}, u32[]{:S(2)}) collective-permute-start(f32[15,35,64]{2,1,0:T(8,128)} %maximum_maximum_fusion), channel_id=1, source_target_pairs={{0,1},{1,2},{2,3},{3,4},{4,5},{5,6},{6,7},{7,8},{8,9},{9,10},{10,1... | collective-permute-start | bytes 403208 | tf_op jit(solution)/shard_map/ppermute | solution.py:21
  8.5 1.3 collective-permute-start.1
  9.8 0.8 fusion.209
  10.6 5.2 %collective-permute-start.2 = (f32[35,1024]{1,0:T(8,128)}, f32[35,1024]{1,0:T(8,128)}, u32[]{:S(2)}, u32[]{:S(2)}) collective-permute-start(f32[35,1024]{1,0:T(8,128)} %get-tuple-element.142), channel_id=1, source_target_pairs={{0,1},{1,2},{2,3},{3,4},{4,5},{5,6},{6,7},{7,8},{8,9},{9,10},{10,1... | collective-permute-start | bytes 430088 | tf_op jit(solution)/shard_map/ppermute | solution.py:21
  15.7 1.3 collective-permute-start.3
  17.5 0.7 slice.320
  18.2 0.6 slice.310
  18.9 0.6 slice.300
  19.5 0.5 iota_multiply_fusion
  20.2 0.6 gather_fusion.8
  20.8 0.6 gather_fusion.7
  21.5 0.6 gather_fusion.5
  22.3 45.7 %all-gather = f32[1024,64]{1,0:T(8,128)S(1)} all-gather(f32[32,64]{1,0:T(8,128)S(1)} %fusion.237), channel_id=2, replica_groups=mesh['group'=4,'bulk'=8] {'group','bulk'}, dimensions={0}, use_global_device_ids=true | all-gather | bytes 270336 | tf_op jit(solution)/shard_map/all_gather | solution.py:151
  68.1 0.6 bitcast_reduce_fusion
  68.7 0.3 bitcast_reduce_fusion.1
  69.5 1.4 %gather_fusion.6 = f32[32,35,64]{2,1,0:T(8,128)} fusion(f32[32,35,64]{2,1,0:T(8,128)S(1)} %pad_maximum_fusion.1, s32[1024]{0:T(1024)S(1)} %pad_clamp_fusion.1), kind=kCustom, calls=%fused_computation.6 | custom fusion | bytes 573568 | tf_op jit(solution)/shard_map/jit(_take)/gather | solution.py:51
  70.9 1.1 fusion.296
  72.8 3.0 %convolution_bitcast_fusion = f32[4,32,64]{2,1,0:T(8,128)S(1)} fusion(f32[4,8,35,64]{3,2,1,0:T(8,128)} %bitcast.233, f32[4,64]{1,0:T(4,128)S(1)} %get-tuple-element.154, f32[4,8,64]{2,1,0:T(8,128)S(1)} %bitcast.252, f32[4,64]{1,0:T(4,128)S(1)} %get-tuple-element.155, f32[4,8,64]{2,1,0:T(8,128)S(1)} %bitcast.251, f32[4,64]{1,0:T(4,128)S(1)} %get-tuple-element.153, ...), kind=kOutput, calls=%fused_computation.116 | convolution fusion | flops 52232192 | bytes 584832 | tf_op jit(solution)/shard_map/nsri,nsij->nrj/dot_general | solution.py:55
  76.4 0.7 compare_convert_fusion
  77.3 1.1 pad_maximum_fusion
  78.4 0.6 gather_fusion.4
  79.0 0.6 gather_fusion.3
  79.6 0.6 convolution_bitcast_fusion.3
  80.4 1.2 convolution_bitcast_fusion.2
  81.8 0.3 fusion.225
  82.2 0.6 gather_fusion.2
  82.8 1.7 %gather_fusion.1 = f32[64,35,64]{2,1,0:T(8,128)} fusion(f32[45,35,64]{2,1,0:T(8,128)S(1)} %pad_maximum_fusion, s32[1024]{0:T(1024)S(1)} %pad_clamp_fusion.6), kind=kCustom, calls=%fused_computation.1 | custom fusion | bytes 1147136 | tf_op jit(solution)/shard_map/jit(_take)/gather | solution.py:51
  84.5 1.3 fusion.294
  85.8 5.0 %fusion.88 = f32[8,32,64]{2,1,0:T(8,128)S(1)} fusion(f32[8,8,35,64]{3,2,1,0:T(8,128)} %bitcast.230, f32[8,64]{1,0:T(8,128)S(1)} %get-tuple-element.148, f32[8,8,64]{2,1,0:T(8,128)S(1)} %bitcast.249, f32[8,64]{1,0:T(8,128)S(1)} %get-tuple-element.149, f32[8,8,64]{2,1,0:T(8,128)S(1)} %bitcast.248, f32[8,64]{1,0:T(8,128)S(1)} %get-tuple-element.147, ...), kind=kOutput, calls=%fused_computation.115 | convolution fusion | flops 104464384 | bytes 1169664 | tf_op jit(solution)/shard_map/nsri,nsij->nrj/dot_general | solution.py:55
  90.8 2.4 %fusion.91 = f32[4,32,64]{2,1,0:T(8,128)S(1)} fusion(f32[4,32,64]{2,1,0:T(8,128)S(1)} %fusion.225, f32[4,8,35,64]{3,2,1,0:T(8,128)S(1)} %bitcast.235, f32[4,64]{1,0:T(4,128)S(1)} %get-tuple-element.151, f32[4,8,64]{2,1,0:T(8,128)S(1)} %bitcast.255, f32[4,64]{1,0:T(4,128)S(1)} %get-tuple-element.152, f32[4,8,64]{2,1,0:T(8,128)S(1)} %bitcast.254, ...), kind=kOutput, calls=%fused_computation.118 | convolution fusion | flops 52240384 | bytes 679936 | tf_op jit(solution)/shard_map/nsri,nsij->nrj/dot_general | solution.py:55
  93.3 0.5 convolution_add_fusion.2
  93.8 1.0 pad_maximum_fusion.2
  95.1 0.3 copy.28
  95.7 44.0 %while.13 = (s32[]{:T(128)}, f32[2,4,32,256]{3,2,1,0:T(8,128)S(1)}, s32[2]{0:T(128)S(1)}, f32[16,35,256]{2,1,0:T(8,128)S(1)}, s32[8,8]{1,0:T(8,128)S(1)}, /*inde...) while((s32[]{:T(128)}, f32[2,4,32,256]{3,2,1,0:T(8,128)S(1)}, ...), condition=%wide.region_7.9_spmd, body=%wide.region_6.8_spmd.sunk | while | flops 939361280 | bytes 4658465 | solution.py:104
  95.7 0.6 dynamic_slice.32
  99.7 0.6 gather_fusion
  100.4 15.2 %fusion.325 = f32[4,32,256]{2,1,0:T(8,128)S(1)} fusion(f32[4,256]{1,0:T(4,128)S(1)} %get-tuple-element.216, f32[4,8,256]{2,1,0:T(8,128)S(1)} %get-tuple-element.219, f32[4,256]{1,0:T(4,128)S(1)} %get-tuple-element.220, f32[4,8,256]{2,1,0:T(8,128)S(1)} %get-tuple-element.221, f32[4,256]{1,0:T(4,128)S(1)} %bitcast.245, ...), kind=kOutput, calls=%fused_computation.40.clone.1 | convolution fusion | flops 834928640 | bytes 1292288 | tf_op jit(solution)/shard_map/while/body/eval_jaxpr/bnrq,bnqp->brp/dot_general | solution.py:47
  115.7 1.9 %fusion.326 = f32[2,4,32,256]{3,2,1,0:T(8,128)S(1)} fusion(f32[2,4,32,256]{3,2,1,0:T(8,128)S(1)} %get-tuple-element.244, s32[]{:T(128)} %get-tuple-element.243, f32[4,32,256]{2,1,0:T(8,128)S(1)} %fusion.325, f32[4,256]{1,0:T(4,128)S(1)} %get-tuple-element.226, f32[4,256]{1,0:T(4,128)S(1)} %get-tuple-element.227, f32[4,256]{1,0:T(4,128)S(1)} %bitcast.246, ...), kind=kOutput, calls=%fused_computation.39.clone.1 | convolution fusion | flops 104431616 | bytes 550916 | tf_op jit(solution)/shard_map/while/body/eval_jaxpr/brq,bqp->brp/dot_general | solution.py:42
  117.7 0.6 dynamic_slice.32
  121.7 0.6 gather_fusion
  122.4 15.2 %fusion.325 = f32[4,32,256]{2,1,0:T(8,128)S(1)} fusion(f32[4,256]{1,0:T(4,128)S(1)} %get-tuple-element.216, f32[4,8,256]{2,1,0:T(8,128)S(1)} %get-tuple-element.219, f32[4,256]{1,0:T(4,128)S(1)} %get-tuple-element.220, f32[4,8,256]{2,1,0:T(8,128)S(1)} %get-tuple-element.221, f32[4,256]{1,0:T(4,128)S(1)} %bitcast.245, ...), kind=kOutput, calls=%fused_computation.40.clone.1 | convolution fusion | flops 834928640 | bytes 1292288 | tf_op jit(solution)/shard_map/while/body/eval_jaxpr/bnrq,bnqp->brp/dot_general | solution.py:47
  137.8 1.9 %fusion.326 = f32[2,4,32,256]{3,2,1,0:T(8,128)S(1)} fusion(f32[2,4,32,256]{3,2,1,0:T(8,128)S(1)} %get-tuple-element.244, s32[]{:T(128)} %get-tuple-element.243, f32[4,32,256]{2,1,0:T(8,128)S(1)} %fusion.325, f32[4,256]{1,0:T(4,128)S(1)} %get-tuple-element.226, f32[4,256]{1,0:T(4,128)S(1)} %get-tuple-element.227, f32[4,256]{1,0:T(4,128)S(1)} %bitcast.246, ...), kind=kOutput, calls=%fused_computation.39.clone.1 | convolution fusion | flops 104431616 | bytes 550916 | tf_op jit(solution)/shard_map/while/body/eval_jaxpr/brq,bqp->brp/dot_general | solution.py:42
  139.7 0.4 fusion.87
  140.1 0.7 copy.45
  (127 shorter events, 4.8 us)
Async XLA Ops:
  0.0 1.2 copy-start
  0.0 9.8 %copy-start.2 = (f32[32,2048]{1,0:T(8,128)S(1)}, f32[32,2048]{1,0:T(8,128)}, u32[]{:S(2)}) copy-start(f32[32,2048]{1,0:T(8,128)} %param.17) | copy-start | bytes 786436
  0.0 4.1 %copy-start.3 = (f32[15,64,64]{2,1,0:T(8,128)S(1)}, f32[15,64,64]{2,1,0:T(8,128)}, u32[]{:S(2)}) copy-start(f32[15,64,64]{2,1,0:T(8,128)} %param.20) | copy-start | bytes 737284
  0.0 4.6 %copy-start.7 = (f32[15,3,64]{2,0,1:T(8,128)S(1)}, f32[15,3,64]{2,0,1:T(8,128)}, u32[]{:S(2)}) copy-start(f32[15,3,64]{2,0,1:T(8,128)} %param.21) | copy-start | bytes 34564
  0.0 9.8 %copy-start.6 = (f32[3,2048]{1,0:T(4,128)S(1)}, f32[3,2048]{1,0:T(4,128)}, u32[]{:S(2)}) copy-start(f32[3,2048]{1,0:T(4,128)} %param.18) | copy-start | bytes 73732
  2.7 14.5 %copy-start.8 = (s32[15,8]{0,1:T(8,128)S(1)}, s32[15,8]{0,1:T(8,128)}, u32[]{:S(2)}) copy-start(s32[15,8]{0,1:T(8,128)} %param.24) | copy-start | bytes 1444
  2.7 14.8 %copy-start.11 = (s32[15]{0:T(128)S(1)}, s32[15]{0:T(128)}, u32[]{:S(2)}) copy-start(s32[15]{0:T(128)} %param.25) | copy-start | bytes 184
  2.7 17.4 %copy-start.5 = (f32[32,3,64]{2,0,1:T(8,128)S(1)}, f32[32,3,64]{2,0,1:T(8,128)}, u32[]{:S(2)}) copy-start(f32[32,3,64]{2,0,1:T(8,128)} %param.27) | copy-start | bytes 73732
  2.7 18.0 %copy-start.1 = (s32[32]{0:T(128)S(1)}, s32[32]{0:T(128)}, u32[]{:S(2)}) copy-start(s32[32]{0:T(128)} %param.29) | copy-start | bytes 388
  4.1 17.3 %copy-start.9 = (s32[32,8]{0,1:T(8,128)S(1)}, s32[32,8]{0,1:T(8,128)}, u32[]{:S(2)}) copy-start(s32[32,8]{0,1:T(8,128)} %param.28) | copy-start | bytes 3076
  5.4 71.9 %collective-permute-start = (f32[15,35,64]{2,1,0:T(8,128)}, f32[15,35,64]{2,1,0:T(8,128)}, u32[]{:S(2)}, u32[]{:S(2)}) collective-permute-start(f32[15,35,64]{2,1,0:T(8,128)} %maximum_maximum_fusion), channel_id=1, source_target_pairs={{0,1},{1,2},{2,3},{3,4},{4,5},{5,6},{6,7},{7,8},{8,9},{9,10},{10,1... | collective-permute-start | bytes 403208 | tf_op jit(solution)/shard_map/ppermute | solution.py:21
  8.5 68.8 %collective-permute-start.1 = (f32[15,35,64]{2,1,0:T(8,128)}, f32[15,35,64]{2,1,0:T(8,128)}, u32[]{:S(2)}, u32[]{:S(2)}) collective-permute-start(f32[15,35,64]{2,1,0:T(8,128)} %maximum_maximum_fusion), channel_id=1, source_target_pairs={{1,0},{2,1},{3,2},{4,3},{5,4},{6,5},{7,6},{8,7},{9,8},{10,9},{11,1... | collective-permute-start | bytes 403208 | tf_op jit(solution)/shard_map/ppermute | solution.py:23
  10.6 83.2 %collective-permute-start.2 = (f32[35,1024]{1,0:T(8,128)}, f32[35,1024]{1,0:T(8,128)}, u32[]{:S(2)}, u32[]{:S(2)}) collective-permute-start(f32[35,1024]{1,0:T(8,128)} %get-tuple-element.142), channel_id=1, source_target_pairs={{0,1},{1,2},{2,3},{3,4},{4,5},{5,6},{6,7},{7,8},{8,9},{9,10},{10,1... | collective-permute-start | bytes 430088 | tf_op jit(solution)/shard_map/ppermute | solution.py:21
  15.7 78.1 %collective-permute-start.3 = (f32[35,1024]{1,0:T(8,128)}, f32[35,1024]{1,0:T(8,128)}, u32[]{:S(2)}, u32[]{:S(2)}) collective-permute-start(f32[35,1024]{1,0:T(8,128)} %get-tuple-element.143), channel_id=1, source_target_pairs={{1,0},{2,1},{3,2},{4,3},{5,4},{6,5},{7,6},{8,7},{9,8},{10,9},{11,1... | collective-permute-start | bytes 430088 | tf_op jit(solution)/shard_map/ppermute | solution.py:23
  20.7 47.3 %copy-start.4 = (f32[32,64,64]{2,1,0:T(8,128)S(1)}, f32[32,64,64]{2,1,0:T(8,128)}, u32[]{:S(2)}) copy-start(f32[32,64,64]{2,1,0:T(8,128)} %param.26) | copy-start | bytes 1572868
  69.3 3.0 %copy-start.16 = (s32[2]{0:T(128)S(1)}, s32[2]{0:T(128)}, u32[]{:S(2)}) copy-start(s32[2]{0:T(128)} %slice.310) | copy-start | bytes 28
  69.3 3.3 %copy-start.14 = (s32[4]{0:T(128)S(1)}, s32[4]{0:T(128)}, u32[]{:S(2)}) copy-start(s32[4]{0:T(128)} %slice.300) | copy-start | bytes 52
  69.3 3.3 %copy-start.12 = (s32[15]{0:T(128)S(1)}, s32[15]{0:T(128)}, u32[]{:S(2)}) copy-start(s32[15]{0:T(128)} %param.25) | copy-start | bytes 184
  69.4 3.4 %copy-start.13 = (s32[8]{0:T(128)S(1)}, s32[8]{0:T(128)}, u32[]{:S(2)}) copy-start(s32[8]{0:T(128)} %param.23) | copy-start | bytes 100
  72.8 3.6 %copy-start.10 = (s32[8,8]{1,0:T(8,128)S(1)}, s32[8,8]{1,0:T(8,128)}, u32[]{:S(2)}) copy-start(s32[8,8]{1,0:T(8,128)} %param.22) | copy-start | bytes 772
  95.1 0.6 copy-start.15
where the time goes:
time: 142 us; the launch traced here: 141 us
  matrix products  53.3 us (38%)
  blocking collectives  45.7 us (32%)
  local copies, waits for them, and re-layouts  17.5 us (12%)
  starting transfers between devices  10.8 us (8%)
  loops' own time  6.74 us (5%)
  other arithmetic  6.16 us (4%)
    all_gather x1, blocking collectives, on_device(): lax.all_gather(root_term[None], ('group', 'bulk'), axis=0, tiled=True)  45.7 us
    dot_general x2, matrix products, near_terms(): jnp.einsum('bnrq,bnqp->brp', masked, cross_kernel, precision=FULL_PRECISION)  30.5 us
    dot_general x5, matrix products, couple(): jnp.einsum('nsri,nsij->nrj', weighted, kernel, precision=FULL_PRECISION)  12.2 us
    ppermute x2, starting transfers between devices, extended_2(): lax.ppermute(tail, axis, [(i, (i + 1) % count) for i in range(ends)])  8.28 us
    another operation x1, loops' own time, on_device(): lax.map(near_block, jnp.arange(0, leaves, block_leaves, dtype=jnp.int32))  6.74 us
    gather x5, local copies, waits for them, and re-layouts, couple(): gathered = jnp.take(lookup, positions, axis=0, mode='clip')  4.92 us
    dot_general x2, matrix products, near_terms(): jnp.einsum('brq,bqp->brp', own_rows, self_kernel, precision=FULL_PRECISION)  3.87 us
  transfers between devices with their start and end apart: 4, of which 0 were waited for; matrix products, arithmetic and copies ran while one was open for 22% of the time, Pallas kernels for 0%

commit v1 on v0

v1 whole, which is shorter than its diff:
```python
import functools
import math

import jax
import jax.numpy as jnp
from jax import lax
from jax.experimental import pallas as pl
from jax.experimental.pallas import tpu as pltpu
from jax.sharding import PartitionSpec as P

AMPLITUDE = 0.2
KERNEL_RATE = 2.0
SOFTENING = 0.01
NUGGET = 0.5
SCALE = KERNEL_RATE * math.log2(math.e)
FLOOR = SOFTENING * SCALE * SCALE
SHIFT = 1.0 / math.log(2.0)
GAIN = AMPLITUDE * math.log(2.0)
FEATURES = 48
STEP = 4
AXES = ("group", "bulk")

f32 = jnp.float32
bf16 = jnp.bfloat16


def dot(a, b, ca, cb):
    return lax.dot_general(a, b, (((ca,), (cb,)), ((), ())), preferred_element_type=f32)


def split2(x):
    high = x.astype(bf16)
    return high, (x - high.astype(f32)).astype(bf16)


def split3(x):
    a = x.astype(bf16).astype(f32)
    b = (x - a).astype(bf16).astype(f32)
    return a, b, x - a - b


def matmul(a, b, ca=1, cb=0):
    ah, al = split2(a)
    bh, bl = split2(b)
    rows = a.shape[1 - ca]
    if ca == 1:
        both = dot(jnp.concatenate([ah, al], axis=0), bh, ca, cb)
        return both[:rows] + both[rows:] + dot(ah, bl, ca, cb)
    return dot(ah, bh, ca, cb) + dot(al, bh, ca, cb) + dot(ah, bl, ca, cb)


def scaled_points(coords):
    u = coords * SCALE
    return u, jnp.broadcast_to(jnp.sum(u * u, axis=0, keepdims=True), u.shape)


def place(row, vector, first, second, third):
    rest = jnp.where(row == 5, third, 0.0)
    rest = jnp.where(row == 4, second, rest)
    rest = jnp.where(row == 3, first, rest)
    return jnp.where(row < 3, vector, rest)


def source_features(coords):
    u, length = scaled_points(coords)
    row = lax.broadcasted_iota(jnp.int32, u.shape, 0)
    a, b, c = split3(u)
    return jnp.concatenate(
        [place(row, a, *split3(length)), place(row, a, 1.0, 1.0, 1.0), b, b, a, c], axis=0
    )


def target_features(coords):
    u, length = scaled_points(coords)
    row = lax.broadcasted_iota(jnp.int32, u.shape, 0)
    a, b, c = split3(-2.0 * u)
    return jnp.concatenate(
        [place(row, a, 1.0, 1.0, 1.0), place(row, b, *split3(length + FLOOR)), a, b, c, a], axis=0
    )


def kernel_of(square):
    t = square * lax.rsqrt(square)
    return (SHIFT + t) * jnp.exp2(-t)


def halves(nodes):
    return max(nodes // 2, 1)


class Sizes:
    def __init__(self, mesh_group, mesh_bulk, leaves, rank, leaf, rhs, near, slots):
        self.group, self.bulk = mesh_group, mesh_bulk
        self.devices = mesh_group * mesh_bulk
        self.leaves, self.rank, self.leaf, self.rhs = leaves, rank, leaf, rhs
        self.near, self.slots = near, slots
        self.levels = leaves.bit_length()
        self.counts = [leaves >> level for level in range(self.levels)]
        self.offsets = [2 * leaves - 2 * count for count in self.counts]
        self.nodes = 2 * leaves - 1
        self.depth = self.devices.bit_length() - 1
        self.top = mesh_group.bit_length() - 1
        self.half = halves(leaves)
        self.message_c = []
        at = self.half * leaf
        for count in self.counts:
            self.message_c.append(at)
            at += halves(count) * rank
        at = -(-at // 128) * 128
        self.message_terms = at
        self.terms = self.depth - self.top
        at += self.terms * rank
        self.message = -(-at // 128) * 128
        self.ext_counts = [count + 2 * halves(count) for count in self.counts]
        self.ext_offsets = [sum(self.ext_counts[:i]) for i in range(self.levels)]
        self.ext_nodes = sum(self.ext_counts)


def put(ref, rows, at, value):
    ref[rows, at : at + value.shape[1]] = value


def up_kernel(z, info, rhs_ref, pts_ref, basis_ref, transfer_ref, skel_ref, *rest):
    upper = rest[: z.terms - 1]
    near_ref, far_ref, coef_ref, terms_ref = rest[z.terms - 1 :]
    parity = info[0] % 2
    rows = slice(0, z.rhs)
    spare = slice(z.rhs, z.rhs + 8)
    pair = 2 * z.rank
    tables = []
    pieces = []
    for leaf in range(z.leaves):
        at = leaf * z.leaf
        pieces.append(matmul(rhs_ref[:, at : at + z.leaf], basis_ref[leaf], 1, 1))
    for level in range(z.levels):
        tables.append(pieces)
        for i, piece in enumerate(pieces):
            coef_ref[z.offsets[level] + i] = piece
        if level + 1 < z.levels:
            raised = []
            for i in range(z.counts[level + 1]):
                both = jnp.concatenate([pieces[2 * i], pieces[2 * i + 1]], axis=1)
                first = z.offsets[level] + 2 * i
                matrix = transfer_ref[first : first + 2].reshape(pair, z.rank)
                raised.append(matmul(both, matrix))
            pieces = raised
    term = matmul(tables[-1][0], transfer_ref[z.nodes - 1])
    lifted = [term]
    for matrix in upper:
        term = matmul(term, matrix[0])
        lifted.append(term)
    terms_ref[...] = jnp.concatenate(lifted, axis=1)
    width = z.half * z.leaf
    for ref, flip in ((near_ref, 0), (far_ref, 1)):
        last = (parity + 1 + flip) % 2
        at = pl.multiple_of(last * ((z.leaves - z.half) * z.leaf), 128)
        ref[rows, 0:width] = rhs_ref[:, pl.ds(at, width)]
        ref[spare, :] = jnp.zeros((8, z.message), f32)
        ref[z.rhs : z.rhs + 3, 0:width] = pts_ref[:, pl.ds(at, width)]
        for level in range(z.levels):
            count, start = z.counts[level], z.message_c[level]
            shift = count - halves(count)
            for i in range(halves(count)):
                node = z.offsets[level] + i + last * shift
                here = slice(start + i * z.rank, start + (i + 1) * z.rank)
                ref[rows, here] = coef_ref[node]
                ref[z.rhs : z.rhs + 3, here] = skel_ref[node]
        ref[rows, z.message_terms : z.message_terms + z.terms * z.rank] = terms_ref[...]


def near_kernel(z, info, list_ref, count_ref, rhs_ref, pts_ref, a_ref, b_ref, out_ref, src, tgt, val, halo):
    device = info[0]
    parity = device % 2
    width = z.half * z.leaf

    @pl.when(parity == 0)
    def _():
        halo[0] = b_ref[:, 0:width]
        halo[1] = a_ref[:, 0:width]

    @pl.when(parity == 1)
    def _():
        halo[0] = a_ref[:, 0:width]
        halo[1] = b_ref[:, 0:width]

    def fill(first, values, coords):
        high, low = split2(values * GAIN)
        features = source_features(coords)
        for i in range(values.shape[1] // z.leaf):
            here = slice(i * z.leaf, (i + 1) * z.leaf)
            val[first + i, 0 : z.rhs] = high[:, here]
            val[first + i, z.rhs : 2 * z.rhs] = low[:, here]
            src[first + i] = features[:, here].T.astype(bf16)

    coords = jnp.concatenate([pts_ref[...], jnp.zeros((5, pts_ref.shape[1]), f32)], axis=0)
    fill(0, halo[0, 0 : z.rhs], halo[0, z.rhs : z.rhs + 8])
    fill(z.half, rhs_ref[...], coords)
    fill(z.half + z.leaves, halo[1, 0 : z.rhs], halo[1, z.rhs : z.rhs + 8])
    features = target_features(coords).astype(bf16)
    for i in range(z.leaves):
        tgt[i] = features[:, i * z.leaf : (i + 1) * z.leaf]
    last = 2 * z.half + z.leaves - 1

    def term(target, source, weight):
        kernel_high, kernel_low = split2(kernel_of(dot(src[source], tgt[target], 1, 0)))
        values = val[source]
        both = dot(values, kernel_high, 1, 0)
        total = both[: z.rhs] + both[z.rhs :] + dot(values[: z.rhs], kernel_low, 1, 0)
        return total if weight is None else total * weight

    def one(target, carry):
        count = count_ref[target]

        def body(i, total):
            for k in range(STEP):
                slot = i * STEP + k
                source = list_ref[target, jnp.minimum(slot, z.near - 1)] - device * z.leaves + z.half
                source = jnp.clip(source, 0, last)
                total += term(target, source, jnp.where(slot < count, 1.0, 0.0))
            return total

        total = term(target, target + z.half, None)
        halo[0, 0 : z.rhs, 0 : z.leaf] = lax.fori_loop(0, (count + STEP - 1) // STEP, body, total)
        at = pl.multiple_of(target * z.leaf, 128)
        out_ref[:, pl.ds(at, z.leaf)] = halo[0, 0 : z.rhs, 0 : z.leaf] + NUGGET * rhs_ref[:, pl.ds(at, z.leaf)]
        return carry

    lax.fori_loop(0, z.leaves, one, 0)


def pad8(block):
    return jnp.concatenate([block, jnp.zeros((8 - block.shape[0], block.shape[1]), f32)], axis=0)


def gathered_kernel(z, sources, target_rows):
    return split2(kernel_of(dot(target_rows, sources, 1, 0)))


def packed(blocks):
    return blocks[0] if len(blocks) == 1 else jnp.concatenate(blocks, axis=1)


def couple(kernel_high, kernel_low, coefs):
    high, low = split2(coefs)
    rows = coefs.shape[0]
    both = dot(jnp.concatenate([high, low], axis=0), kernel_high, 1, 1)
    return both[:rows] + both[rows:] + dot(high, kernel_low, 1, 1)


def local_kernel(z, info, list_ref, count_ref, coef_ref, skel_ref, a_ref, b_ref, out_ref, table, feats, halo):
    device = info[0]
    parity = device % 2
    start = z.message_c[0]

    @pl.when(parity == 0)
    def _():
        halo[0] = b_ref[...]
        halo[1] = a_ref[...]

    @pl.when(parity == 1)
    def _():
        halo[0] = a_ref[...]
        halo[1] = b_ref[...]

    row_features = []
    for level in range(z.levels):
        count, half, base = z.counts[level], halves(z.counts[level]), z.ext_offsets[level]
        for i in range(half):
            here = slice(z.message_c[level] + i * z.rank, z.message_c[level] + (i + 1) * z.rank)
            for side, first in ((0, base), (1, base + half + count)):
                table[first + i] = halo[side, 0 : z.rhs, here] * GAIN
                feats[first + i] = source_features(halo[side, z.rhs : z.rhs + 8, here])
        for i in range(count):
            node = z.offsets[level] + i
            table[base + half + i] = coef_ref[node] * GAIN
            coords = pad8(skel_ref[node])
            feats[base + half + i] = source_features(coords)
            row_features.append(target_features(coords).T.astype(bf16))
    for level in range(z.levels):
        count, half, base = z.counts[level], halves(z.counts[level]), z.ext_offsets[level]
        for i in range(count):
            node = z.offsets[level] + i
            used = count_ref[node]
            values, points = [], []
            for slot in range(z.slots):
                at = jnp.clip(list_ref[node, slot] - device * count + half, 0, z.ext_counts[level] - 1)
                values.append(table[base + at] * jnp.where(slot < used, 1.0, 0.0))
                points.append(feats[base + at])
            high, low = gathered_kernel(z, packed(points).astype(bf16), row_features[node])
            out_ref[node] = couple(high, low, packed(values))


def final_kernel(z, info, list_ref, count_ref, near_ref, field_ref, basis_ref, transfer_ref, skel_ref, matrix_ref, *rest):
    tables, out_ref = rest[: z.terms], rest[-1]
    device = info[0]
    values = {}
    for i in range(z.terms):
        table = tables[i]
        values[z.depth - 1 - i] = table
    top = values[z.top]
    size = z.group
    own = (z.devices + device) >> (z.depth - z.top)
    level_values = {}
    current = [top[j] for j in range(size)]
    level_values[z.top] = current
    for level in range(z.top, 1, -1):
        anchor = (z.devices + device) >> (z.depth - level)
        moved = [matmul(current[j], matrix_ref[anchor ^ j]) for j in range(len(current))]
        current = [moved[2 * j] + moved[2 * j + 1] for j in range(len(current) // 2)]
        level_values[level - 1] = current
    downward = None
    for level in range(1, z.depth):
        anchor = (z.devices + device) >> (z.depth - level)
        if level <= z.top:
            size = len(level_values[level])
        else:
            size = z.bulk >> (z.depth - level)
        used = count_ref[anchor]
        slots = min(z.slots, size - 1)
        if slots:
            target = target_features(pad8(skel_ref[anchor])).T.astype(bf16)
            coefs, points = [], []
            for slot in range(slots):
                source = list_ref[anchor, slot]
                at = jnp.where(slot < used, source ^ anchor, 0)
                source = jnp.where(slot < used, source, anchor)
                weight = jnp.where(slot < used, GAIN, 0.0)
                if level < z.top:
                    chosen = level_values[level][0] * 0.0
                    for j in range(1, size):
                        chosen += level_values[level][j] * jnp.where(at == j, weight, 0.0)
                else:
                    chosen = values[level][at] * weight
                coefs.append(chosen)
                points.append(source_features(pad8(skel_ref[source])))
            high, low = gathered_kernel(z, packed(points).astype(bf16), target)
            field = couple(high, low, packed(coefs))
        else:
            field = jnp.zeros((z.rhs, z.rank), f32)
        if downward is None:
            downward = field
        else:
            downward = field + matmul(downward, matrix_ref[anchor], 1, 1)
    incoming = matmul(downward, transfer_ref[z.nodes - 1], 1, 1)
    fields = [field_ref[z.nodes - 1] + incoming]
    for level in range(z.levels - 2, -1, -1):
        below = []
        for i in range(z.counts[level]):
            node = z.offsets[level] + i
            below.append(field_ref[node] + matmul(fields[i // 2], transfer_ref[node], 1, 1))
        fields = below
    for leaf in range(z.leaves):
        here = slice(leaf * z.leaf, (leaf + 1) * z.leaf)
        out_ref[:, here] = near_ref[:, here] + matmul(fields[leaf], basis_ref[leaf])


SMEM = pl.BlockSpec(memory_space=pltpu.SMEM)
VMEM = pl.BlockSpec(memory_space=pltpu.VMEM)


def flip(x, axis, bit):
    return lax.ppermute(x, axis, [(i, i ^ bit) for i in range(lax.axis_size(axis))])


def on_device(
    right_sides,
    points,
    basis,
    transfer,
    skeleton,
    near_list,
    near_count,
    inter_list,
    inter_count,
    upper_transfer,
    upper_skeleton,
    upper_list,
    upper_count,
):
    z = Sizes(
        lax.axis_size("group"),
        lax.axis_size("bulk"),
        basis.shape[0],
        basis.shape[1],
        basis.shape[2],
        right_sides.shape[0],
        near_list.shape[1],
        inter_list.shape[1],
    )
    device = lax.axis_index(AXES).astype(jnp.int32)
    info = device.reshape(1)
    message = jax.ShapeDtypeStruct((z.rhs + 8, z.message), f32)

    def ancestor(level):
        return lambda i, info: ((z.devices + info[0]) // (1 << (z.depth - level)), 0, 0)

    def whole(array):
        return pl.BlockSpec(array.shape, lambda i, info, n=array.ndim: (0,) * n)

    raised = [upper_transfer] * (z.terms - 1)
    outs = (
        message,
        message,
        jax.ShapeDtypeStruct((z.nodes, z.rhs, z.rank), f32),
        jax.ShapeDtypeStruct((z.rhs, z.terms * z.rank), f32),
    )
    to_partner, to_other, coefs, terms = pl.pallas_call(
        functools.partial(up_kernel, z),
        name="up",
        out_shape=outs,
        grid_spec=pltpu.PrefetchScalarGridSpec(
            num_scalar_prefetch=1,
            grid=(1,),
            in_specs=[whole(a) for a in (right_sides, points, basis, transfer, skeleton)]
            + [
                pl.BlockSpec((1, z.rank, z.rank), ancestor(level))
                for level in range(z.depth - 1, z.top, -1)
            ],
            out_specs=[whole(a) for a in outs],
        ),
    )(info, right_sides, points, basis, transfer, skeleton, *raised)
    from_partner = flip(to_partner, "bulk", 1)
    pairs = [(i, i + 1) for i in range(1, z.devices - 1, 2)]
    from_other = lax.ppermute(to_other, AXES, pairs + [(b, a) for a, b in pairs])

    near_part = pl.pallas_call(
        functools.partial(near_kernel, z),
        name="near",
        out_shape=jax.ShapeDtypeStruct(right_sides.shape, f32),
        in_specs=[SMEM, SMEM, SMEM, VMEM, VMEM, VMEM, VMEM],
        out_specs=VMEM,
        scratch_shapes=[
            pltpu.VMEM((2 * z.half + z.leaves, z.leaf, FEATURES), bf16),
            pltpu.VMEM((z.leaves, FEATURES, z.leaf), bf16),
            pltpu.VMEM((2 * z.half + z.leaves, 2 * z.rhs, z.leaf), bf16),
            pltpu.VMEM((2, z.rhs + 8, z.half * z.leaf), f32),
        ],
    )(info, near_list, near_count, right_sides, points, from_partner, from_other)

    fields = pl.pallas_call(
        functools.partial(local_kernel, z),
        name="local",
        out_shape=jax.ShapeDtypeStruct((z.nodes, z.rhs, z.rank), f32),
        in_specs=[SMEM, SMEM, SMEM, VMEM, VMEM, VMEM, VMEM],
        out_specs=VMEM,
        scratch_shapes=[
            pltpu.VMEM((z.ext_nodes, z.rhs, z.rank), f32),
            pltpu.VMEM((z.ext_nodes, FEATURES, z.rank), f32),
            pltpu.VMEM((2, z.rhs + 8, z.message), f32),
        ],
    )(info, inter_list, inter_count, coefs, skeleton, from_partner, from_other)

    first = z.message_terms
    terms = terms.reshape(z.rhs, z.terms, z.rank).transpose(1, 0, 2)
    theirs = from_partner[: z.rhs, first : first + z.terms * z.rank]
    theirs = theirs.reshape(z.rhs, z.terms, z.rank).transpose(1, 0, 2)
    whole_levels, partial = [], terms + theirs
    for bit in range(1, z.bulk.bit_length()):
        whole_levels.append(partial[:1])
        partial = partial[1:]
        if bit == z.bulk.bit_length() - 1:
            break
        sizes = [level.shape[0] for level in whole_levels]
        sent = jnp.concatenate(whole_levels + [partial], axis=0)
        received = flip(sent, "bulk", 1 << bit)
        at = 0
        for i, size in enumerate(sizes):
            whole_levels[i] = jnp.concatenate([whole_levels[i], received[at : at + size]], axis=0)
            at += size
        partial = partial + received[at:]
    top = whole_levels[-1]
    for bit in range(z.top):
        top = jnp.concatenate([top, flip(top, "group", 1 << bit)], axis=0)
    whole_levels[-1] = top

    return pl.pallas_call(
        functools.partial(final_kernel, z),
        name="final",
        out_shape=jax.ShapeDtypeStruct(right_sides.shape, f32),
        in_specs=[SMEM, SMEM, SMEM] + [VMEM] * (6 + z.terms),
        out_specs=VMEM,
    )(
        info,
        upper_list,
        upper_count,
        near_part,
        fields,
        basis,
        transfer,
        upper_skeleton,
        upper_transfer,
        *whole_levels,
    )


def solution(mesh):
    in_specs = (
        P(None, AXES),
        P(None, AXES),
        P(AXES, None, None),
        P(AXES, None, None),
        P(AXES, None, None),
        P(AXES, None),
        P(AXES),
        P(AXES, None),
        P(AXES),
        P(),
        P(),
        P(),
        P(),
    )
    return jax.shard_map(
        on_device, mesh=mesh, in_specs=in_specs, out_specs=P(None, AXES), check_vma=False
    )
```

time: 142 us -> 53.6 us (0.38); the launches traced: 141 us -> 54.2 us
  matrix products: 53.3 us -> 0 us
  blocking collectives: 45.7 us -> 0 us
  Pallas kernels: 0 us -> 21 us
  local copies, waits for them, and re-layouts: 17.5 us -> 4.21 us
  starting transfers between devices: 10.8 us -> 20.5 us
  loops' own time: 6.74 us -> 0 us
  waiting for transfers between devices: 0.01 us -> 5.68 us
  other arithmetic: 6.16 us -> 2.67 us
    dot_general x25 -> x0, matrix products: 53.3 us -> none  [the longest x2 30.5 us: near_terms(): jnp.einsum('bnrq,bnqp->brp', masked, cross_kernel, precision=FULL_PRECISION)]
    all_gather x1 -> x0, blocking collectives: 45.7 us -> none  [on_device(): lax.all_gather(root_term[None], ('group', 'bulk'), axis=0, tiled=True)]
    pallas_call x0 -> x4, Pallas kernels: none -> 21 us  [the longest x1 9.05 us: on_device(): pl.pallas_call(functools.partial(near_kernel, z), name='near', out_shape=...]
    ppermute x4 -> x6, starting transfers between devices: 10.8 us -> 20.5 us  [the longest x5 19.9 us: flip(): lax.ppermute(x, axis, [(i, i ^ bit) for i in range(lax.axis_size(axis))])]
    gather x10 -> x0, local copies, waits for them, and re-layouts: 7.95 us -> none  [the longest x5 4.92 us: couple(): gathered = jnp.take(lookup, positions, axis=0, mode='clip')]
    another operation x1 -> x0, loops' own time: 6.74 us -> none  [on_device(): lax.map(near_block, jnp.arange(0, leaves, block_leaves, dtype=jnp.int32))]
    ppermute x4 -> x6, waiting for transfers between devices: 0.01 us -> 5.68 us  [the longest x5 5.68 us: flip(): lax.ppermute(x, axis, [(i, i ^ bit) for i in range(lax.axis_size(axis))])]
    slice x14 -> x3, local copies, waits for them, and re-layouts: 4.51 us -> 0.01 us  [the longest x2 0.01 us: on_device(): received[at:at + size]]
  transfers between devices with their start and end apart: 4 -> 6, of which waited for: 0 -> 4; matrix products, arithmetic and copies ran while one was open for 22% -> 6% of each run, Pallas kernels for 0% -> 25%
where the time goes in v1:
time: 53.6 us; the launch traced here: 54.2 us
  Pallas kernels  21 us (39%)
  starting transfers between devices  20.5 us (38%)
  waiting for transfers between devices  5.68 us (11%)
  local copies, waits for them, and re-layouts  4.21 us (8%)
  other arithmetic  2.67 us (5%)
    ppermute x5, starting transfers between devices, flip(): lax.ppermute(x, axis, [(i, i ^ bit) for i in range(lax.axis_size(axis))])  19.9 us
    pallas_call x1, Pallas kernels, on_device(): pl.pallas_call(functools.partial(near_kernel, z), name='near', out_shape=...  9.05 us
    ppermute x5, waiting for transfers between devices, flip(): lax.ppermute(x, axis, [(i, i ^ bit) for i in range(lax.axis_size(axis))])  5.68 us
    pallas_call x1, Pallas kernels, on_device(): pl.pallas_call(functools.partial(local_kernel, z), name='local', out_shap...  4.46 us
    unnamed x16, local copies, waits for them, and re-layouts  4.11 us
    pallas_call x1, Pallas kernels, on_device(): pl.pallas_call(functools.partial(final_kernel, z), name='final', out_shap...  4.05 us
    pallas_call x1, Pallas kernels, on_device(): pl.pallas_call(functools.partial(up_kernel, z), name='up', out_shape=outs...  3.48 us
    concatenate x2, other arithmetic, on_device(): jnp.concatenate([whole_levels[i], received[at:at + size]], axis=0)  1.24 us
  transfers between devices with their start and end apart: 6, of which 4 were waited for; matrix products, arithmetic and copies ran while one was open for 6% of the time, Pallas kernels for 25%

profile of v1, /device:TPU:0, one launch (start us, length us, event | category | flops | bytes accessed | tf_op | source)
XLA Modules:
  0.0 54.2 jit_solution(10354205065492349388)
XLA Ops:
  0.0 1.4 %copy.19.skel_ref = f32[15,3,64]{2,1,0:T(4,128)} copy(f32[15,3,64]{2,0,1:T(8,128)} %param.17) | data formatting | bytes 23040 | tf_op args[4]
  1.4 3.5 %up.1 = (f32[40,1792]{1,0:T(8,128)}, f32[40,1792]{1,0:T(8,128)}, f32[15,32,64]{2,1,0:T(8,128)}, f32[32,192]{1,0:T(8,128)}) custom-call(s32[1]{0:T(128)} %bitcast.info, f32[32,2048]{1,0:T(8,128)} %rhs_ref.3, f32[3,2048]{1,0:T(4,128)} %pts_ref.3, f32[8,64,256]{2,1,0:T(8,128)} %basis_ref.3, f32[15,64,64]{2,1,0:T(8,128)} %transfer_ref.3, ...), custom_call_target="tpu_custom_call" | custom-call | tf_op jit(solution)/shard_map/up/pallas_call | solution.py:407
  4.8 0.0 copy-start.5
  4.8 0.5 collective-permute-start
  5.3 1.4 %collective-permute-done.a_ref = f32[40,1792]{1,0:T(8,128)S(1)} collective-permute-done((f32[40,1792]{1,0:T(8,128)}, f32[40,1792]{1,0:T(8,128)S(1)}, u32[]{:S(2)}, u32[]{:S(2)}) %collective-permute-start) | collective-permute-done | bytes 286752 | tf_op jit(solution)/shard_map/ppermute | solution.py:362
  6.7 0.0 copy-start
  6.7 0.8 %slice_add_fusion.1 = f32[32,192]{1,0:T(8,128)S(1)} fusion(f32[32,192]{1,0:T(8,128)} %get-tuple-element.12, f32[40,1792]{1,0:T(8,128)S(1)} %collective-permute-done.a_ref), kind=kLoop, calls=%fused_computation.6 | loop fusion | flops 6144 | bytes 73728 | tf_op jit(solution)/shard_map/add | solution.py:457
  7.5 0.1 add.20
  7.6 3.0 %collective-permute-start.2 = (f32[3,32,64]{2,1,0:T(8,128)S(1)}, f32[3,32,64]{2,1,0:T(8,128)S(1)}, u32[]{:S(2)}, u32[]{:S(2)}) collective-permute-start(f32[3,32,64]{2,1,0:T(8,128)S(1)} %bitcast.4), channel_id=1, source_target_pairs={{0,2},{1,3},{2,0},{3,1},{4,6},{5,7},{6,4},{7,5},{8,10},{9,11},{10,... | collective-permute-start | bytes 73736 | tf_op jit(solution)/shard_map/ppermute | solution.py:362
  10.6 0.0 copy-done.5
  10.6 0.7 %collective-permute-start.1 = (f32[40,1792]{1,0:T(8,128)S(1)}, f32[40,1792]{1,0:T(8,128)S(1)}, u32[]{:S(2)}, u32[]{:S(2)}) collective-permute-start(f32[40,1792]{1,0:T(8,128)S(1)} %copy-done.5), channel_id=1, source_target_pairs={{1,2},{3,4},{5,6},{7,8},{9,10},{11,12},{13,14},{15,16},{17,18},{19... | collective-permute-start | bytes 860168 | tf_op jit(solution)/shard_map/ppermute | solution.py:424
  11.3 1.4 %collective-permute-done.2 = f32[3,32,64]{2,1,0:T(8,128)S(1)} collective-permute-done((f32[3,32,64]{2,1,0:T(8,128)S(1)}, f32[3,32,64]{2,1,0:T(8,128)S(1)}, u32[]{:S(2)}, u32[]{:S(2)}) %collective-permute-start.2) | collective-permute-done | bytes 24608 | tf_op jit(solution)/shard_map/ppermute | solution.py:362
  12.7 0.0 copy-start.3
  12.7 0.0 copy-start.2
  12.7 0.0 copy-done
  12.7 3.1 %collective-permute-start.3 = (f32[4,32,64]{2,1,0:T(8,128)S(1)}, f32[4,32,64]{2,1,0:T(8,128)S(1)}, u32[]{:S(2)}, u32[]{:S(2)}) collective-permute-start(f32[4,32,64]{2,1,0:T(8,128)S(1)} %pad_maximum_fusion), channel_id=1, source_target_pairs={{0,4},{1,5},{2,6},{3,7},{4,0},{5,1},{6,2},{7,3},{8,12},{9,13},{10,... | collective-permute-start | bytes 98312 | tf_op jit(solution)/shard_map/ppermute | solution.py:362
  15.8 0.0 copy-done.3
  15.8 0.7 %copy.20.list_ref = s32[15,8]{1,0:T(8,128)} copy(s32[15,8]{0,1:T(8,128)S(1)} %copy-done.3) | data formatting | bytes 960 | tf_op args[7]
  16.5 0.0 copy-done.2
  16.5 0.0 copy-start.4
  16.5 0.7 %copy.24.skel_ref = f32[32,3,64]{2,1,0:T(4,128)} copy(f32[32,3,64]{2,0,1:T(8,128)S(1)} %copy-done.2) | data formatting | bytes 49152 | tf_op args[10]
  17.2 0.0 copy-done.4
  17.2 0.7 %copy.23.list_ref = s32[32,8]{1,0:T(8,128)} copy(s32[32,8]{0,1:T(8,128)S(1)} %copy-done.4) | data formatting | bytes 2048 | tf_op args[11]
  17.9 0.0 collective-permute-done.1.b_ref
  17.9 0.0 copy-start.1
  17.9 0.7 %copy-done.1 = f32[40,1792]{1,0:T(8,128)} copy-done((f32[40,1792]{1,0:T(8,128)}, f32[40,1792]{1,0:T(8,128)S(1)}, u32[]{:S(2)}) %copy-start.1) | copy-done | bytes 286744
  18.6 9.1 %near.1.near_ref = f32[32,2048]{1,0:T(8,128)} custom-call(s32[1]{0:T(128)} %bitcast.info, s32[8,8]{1,0:T(8,128)} %list_ref.3, s32[8]{0:T(128)} %count_ref.3, f32[32,2048]{1,0:T(8,128)} %rhs_ref.3, f32[3,2048]{1,0:T(4,128)} %pts_ref.3, f32[40,1792]{1,0:T(8,128)} %copy-done, f32[40,1792]{1,0:T(8,128)} %copy-done.1), custom_call_target="tpu_custom_call" | custom-call | tf_op jit(solution)/shard_map/near/pallas_call | solution.py:426
  27.6 4.5 %local.1.field_ref = f32[15,32,64]{2,1,0:T(8,128)} custom-call(s32[1]{0:T(128)} %bitcast.info, s32[15,8]{1,0:T(8,128)} %copy.20.list_ref, s32[15]{0:T(128)} %count_ref.4, f32[15,32,64]{2,1,0:T(8,128)} %get-tuple-element.11.coef_ref, f32[15,3,64]{2,1,0:T(4,128)} %copy.19.skel_ref, f32[40,1792]{1,0:T(8,128)} %copy-done, f32[40,1792]{1,0:T(8,128)} %copy-done.1), custom_call_target="tpu_custom_call" | custom-call | tf_op jit(solution)/shard_map/local/pallas_call | solution.py:440
  32.1 0.0 collective-permute-done.3
  32.1 11.8 %collective-permute-start.4 = (f32[1,32,64]{2,1,0:T(8,128)S(1)}, f32[1,32,64]{2,1,0:T(8,128)S(1)}, u32[]{:S(2)}, u32[]{:S(2)}) collective-permute-start(f32[1,32,64]{2,1,0:T(8,128)S(1)} %get-tuple-element.13), channel_id=1, source_target_pairs={{0,8},{8,0},{16,24},{24,16},{1,9},{9,1},{17,25},{25,17},{2,10},{10... | collective-permute-start | bytes 24584 | tf_op jit(solution)/shard_map/ppermute | solution.py:362
  43.9 0.6 %pad_maximum_fusion.1.rest_0_ = f32[4,32,64]{2,1,0:T(8,128)} fusion(f32[2,32,64]{2,1,0:T(8,128)S(1)} %slice.47, f32[1,32,64]{2,1,0:T(8,128)S(1)} %slice.44, f32[1,32,64]{2,1,0:T(8,128)S(1)} %slice.43), kind=kLoop, calls=%fused_computation.1 | loop fusion | flops 16384 | bytes 65536 | tf_op jit(solution)/shard_map/concatenate | solution.py:468
  44.5 1.1 %collective-permute-done.4 = f32[1,32,64]{2,1,0:T(8,128)S(1)} collective-permute-done((f32[1,32,64]{2,1,0:T(8,128)S(1)}, f32[1,32,64]{2,1,0:T(8,128)S(1)}, u32[]{:S(2)}, u32[]{:S(2)}) %collective-permute-start.4) | collective-permute-done | bytes 8224 | tf_op jit(solution)/shard_map/ppermute | solution.py:362
  45.6 1.5 %collective-permute-start.5 = (f32[2,32,64]{2,1,0:T(8,128)S(1)}, f32[2,32,64]{2,1,0:T(8,128)S(1)}, u32[]{:S(2)}, u32[]{:S(2)}) collective-permute-start(f32[2,32,64]{2,1,0:T(8,128)S(1)} %pad_maximum_fusion.5), channel_id=1, source_target_pairs={{0,16},{8,24},{16,0},{24,8},{1,17},{9,25},{17,1},{25,9},{2,18},{10... | collective-permute-start | bytes 49160 | tf_op jit(solution)/shard_map/ppermute | solution.py:362
  47.1 0.6 %pad_maximum_fusion.4.rest_1_ = f32[2,32,64]{2,1,0:T(8,128)} fusion(f32[1,32,64]{2,1,0:T(8,128)S(1)} %get-tuple-element.14, f32[1,32,64]{2,1,0:T(8,128)S(1)} %get-tuple-element.15), kind=kLoop, calls=%fused_computation.7 | loop fusion | flops 4096 | bytes 32768 | tf_op jit(solution)/shard_map/concatenate | solution.py:468
  47.7 1.8 %collective-permute-done.5 = f32[2,32,64]{2,1,0:T(8,128)S(1)} collective-permute-done((f32[2,32,64]{2,1,0:T(8,128)S(1)}, f32[2,32,64]{2,1,0:T(8,128)S(1)}, u32[]{:S(2)}, u32[]{:S(2)}) %collective-permute-start.5) | collective-permute-done | bytes 16416 | tf_op jit(solution)/shard_map/ppermute | solution.py:362
  49.5 0.6 %pad_maximum_fusion.3.rest_2_ = f32[4,32,64]{2,1,0:T(8,128)} fusion(f32[2,32,64]{2,1,0:T(8,128)S(1)} %collective-permute-done.5, f32[1,32,64]{2,1,0:T(8,128)S(1)} %collective-permute-done.4, f32[1,32,64]{2,1,0:T(8,128)S(1)} %get-tuple-element.13), kind=kLoop, calls=%fused_computation.3 | loop fusion | flops 16384 | bytes 65536 | tf_op jit(solution)/shard_map/concatenate | solution.py:473
  50.2 4.1 %final.1 = f32[32,2048]{1,0:T(8,128)} custom-call(s32[1]{0:T(128)} %bitcast.info, s32[32,8]{1,0:T(8,128)} %copy.23.list_ref, s32[32]{0:T(128)} %count_ref.5, f32[32,2048]{1,0:T(8,128)} %near.1.near_ref, f32[15,32,64]{2,1,0:T(8,128)} %local.1.field_ref, f32[8,64,256]{2,1,0:T(8,128)} %basis_ref.3, f32[15,64,64]{2,1,0:T(8,128)} %transfer_ref.3, ...), custom_call_target="tpu_custom_call" | custom-call | tf_op jit(solution)/shard_map/final/pallas_call | solution.py:476
  (8 shorter events, 0.0 us)
Async XLA Ops:
  4.8 5.8 %copy-start.5 = (f32[40,1792]{1,0:T(8,128)S(1)}, f32[40,1792]{1,0:T(8,128)}, u32[]{:S(2)}) copy-start(f32[40,1792]{1,0:T(8,128)} %get-tuple-element.10) | copy-start | bytes 860164
  4.8 1.9 %collective-permute-start = (f32[40,1792]{1,0:T(8,128)}, f32[40,1792]{1,0:T(8,128)S(1)}, u32[]{:S(2)}, u32[]{:S(2)}) collective-permute-start(f32[40,1792]{1,0:T(8,128)} %get-tuple-element.9), channel_id=1, source_target_pairs={{0,1},{1,0},{2,3},{3,2},{4,5},{5,4},{6,7},{7,6},{8,9},{9,8},{10,11... | collective-permute-start | bytes 860168 | tf_op jit(solution)/shard_map/ppermute | solution.py:362
  6.7 6.0 %copy-start = (f32[40,1792]{1,0:T(8,128)}, f32[40,1792]{1,0:T(8,128)S(1)}, u32[]{:S(2)}) copy-start(f32[40,1792]{1,0:T(8,128)S(1)} %collective-permute-done.a_ref) | copy-start | bytes 860164
  7.6 5.1 %collective-permute-start.2 = (f32[3,32,64]{2,1,0:T(8,128)S(1)}, f32[3,32,64]{2,1,0:T(8,128)S(1)}, u32[]{:S(2)}, u32[]{:S(2)}) collective-permute-start(f32[3,32,64]{2,1,0:T(8,128)S(1)} %bitcast.4), channel_id=1, source_target_pairs={{0,2},{1,3},{2,0},{3,1},{4,6},{5,7},{6,4},{7,5},{8,10},{9,11},{10,... | collective-permute-start | bytes 73736 | tf_op jit(solution)/shard_map/ppermute | solution.py:362
  10.6 7.3 %collective-permute-start.1 = (f32[40,1792]{1,0:T(8,128)S(1)}, f32[40,1792]{1,0:T(8,128)S(1)}, u32[]{:S(2)}, u32[]{:S(2)}) collective-permute-start(f32[40,1792]{1,0:T(8,128)S(1)} %copy-done.5), channel_id=1, source_target_pairs={{1,2},{3,4},{5,6},{7,8},{9,10},{11,12},{13,14},{15,16},{17,18},{19... | collective-permute-start | bytes 860168 | tf_op jit(solution)/shard_map/ppermute | solution.py:424
  12.7 3.2 %copy-start.3 = (s32[15,8]{0,1:T(8,128)S(1)}, s32[15,8]{0,1:T(8,128)}, u32[]{:S(2)}) copy-start(s32[15,8]{0,1:T(8,128)} %param.20) | copy-start | bytes 1444
  12.7 3.8 %copy-start.2 = (f32[32,3,64]{2,0,1:T(8,128)S(1)}, f32[32,3,64]{2,0,1:T(8,128)}, u32[]{:S(2)}) copy-start(f32[32,3,64]{2,0,1:T(8,128)} %param.23) | copy-start | bytes 73732
  12.7 19.4 %collective-permute-start.3 = (f32[4,32,64]{2,1,0:T(8,128)S(1)}, f32[4,32,64]{2,1,0:T(8,128)S(1)}, u32[]{:S(2)}, u32[]{:S(2)}) collective-permute-start(f32[4,32,64]{2,1,0:T(8,128)S(1)} %pad_maximum_fusion), channel_id=1, source_target_pairs={{0,4},{1,5},{2,6},{3,7},{4,0},{5,1},{6,2},{7,3},{8,12},{9,13},{10,... | collective-permute-start | bytes 98312 | tf_op jit(solution)/shard_map/ppermute | solution.py:362
  16.5 0.7 %copy-start.4 = (s32[32,8]{0,1:T(8,128)S(1)}, s32[32,8]{0,1:T(8,128)}, u32[]{:S(2)}) copy-start(s32[32,8]{0,1:T(8,128)} %param.24) | copy-start | bytes 3076
  17.9 0.7 %copy-start.1 = (f32[40,1792]{1,0:T(8,128)}, f32[40,1792]{1,0:T(8,128)S(1)}, u32[]{:S(2)}) copy-start(f32[40,1792]{1,0:T(8,128)S(1)} %collective-permute-done.1.b_ref) | copy-start | bytes 860164
  32.1 13.5 %collective-permute-start.4 = (f32[1,32,64]{2,1,0:T(8,128)S(1)}, f32[1,32,64]{2,1,0:T(8,128)S(1)}, u32[]{:S(2)}, u32[]{:S(2)}) collective-permute-start(f32[1,32,64]{2,1,0:T(8,128)S(1)} %get-tuple-element.13), channel_id=1, source_target_pairs={{0,8},{8,0},{16,24},{24,16},{1,9},{9,1},{17,25},{25,17},{2,10},{10... | collective-permute-start | bytes 24584 | tf_op jit(solution)/shard_map/ppermute | solution.py:362
  45.6 3.9 %collective-permute-start.5 = (f32[2,32,64]{2,1,0:T(8,128)S(1)}, f32[2,32,64]{2,1,0:T(8,128)S(1)}, u32[]{:S(2)}, u32[]{:S(2)}) collective-permute-start(f32[2,32,64]{2,1,0:T(8,128)S(1)} %pad_maximum_fusion.5), channel_id=1, source_target_pairs={{0,16},{8,24},{16,0},{24,8},{1,17},{9,25},{17,1},{25,9},{2,18},{10... | collective-permute-start | bytes 49160 | tf_op jit(solution)/shard_map/ppermute | solution.py:362

commit v2 on v1

v2 whole, which is shorter than its diff:
```python
import functools
import math

import jax
import jax.numpy as jnp
from jax import lax
from jax.experimental import pallas as pl
from jax.experimental.pallas import tpu as pltpu
from jax.sharding import PartitionSpec as P

AMPLITUDE = 0.2
KERNEL_RATE = 2.0
SOFTENING = 0.01
NUGGET = 0.5
SCALE = KERNEL_RATE * math.log2(math.e)
FLOOR = SOFTENING * SCALE * SCALE
SHIFT = 1.0 / math.log(2.0)
GAIN = AMPLITUDE * math.log(2.0)
FEATURES = 48
STEP = 4
NEAR_SHARES = (5, 10, 13)
AXES = ("group", "bulk")

f32 = jnp.float32
bf16 = jnp.bfloat16


def dot(a, b, ca, cb):
    return lax.dot_general(a, b, (((ca,), (cb,)), ((), ())), preferred_element_type=f32)


def split2(x):
    high = x.astype(bf16)
    return high, (x - high.astype(f32)).astype(bf16)


def split3(x):
    a = x.astype(bf16).astype(f32)
    b = (x - a).astype(bf16).astype(f32)
    return a, b, x - a - b


def matmul(a, b, ca=1, cb=0):
    ah, al = split2(a)
    bh, bl = split2(b)
    rows = a.shape[1 - ca]
    if ca == 1:
        both = dot(jnp.concatenate([ah, al], axis=0), bh, ca, cb)
        return both[:rows] + both[rows:] + dot(ah, bl, ca, cb)
    return dot(ah, bh, ca, cb) + dot(al, bh, ca, cb) + dot(ah, bl, ca, cb)


def scaled_points(coords):
    u = coords * SCALE
    return u, jnp.broadcast_to(jnp.sum(u * u, axis=0, keepdims=True), u.shape)


def place(row, vector, first, second, third):
    rest = jnp.where(row == 5, third, 0.0)
    rest = jnp.where(row == 4, second, rest)
    rest = jnp.where(row == 3, first, rest)
    return jnp.where(row < 3, vector, rest)


def source_features(coords):
    u, length = scaled_points(coords)
    row = lax.broadcasted_iota(jnp.int32, u.shape, 0)
    a, b, c = split3(u)
    return jnp.concatenate(
        [place(row, a, *split3(length)), place(row, a, 1.0, 1.0, 1.0), b, b, a, c], axis=0
    )


def target_features(coords):
    u, length = scaled_points(coords)
    row = lax.broadcasted_iota(jnp.int32, u.shape, 0)
    a, b, c = split3(-2.0 * u)
    return jnp.concatenate(
        [place(row, a, 1.0, 1.0, 1.0), place(row, b, *split3(length + FLOOR)), a, b, c, a], axis=0
    )


def kernel_of(square):
    t = square * lax.rsqrt(square)
    return (SHIFT + t) * jnp.exp2(-t)


def halves(nodes):
    return max(nodes // 2, 1)


class Sizes:
    def __init__(self, mesh_group, mesh_bulk, leaves, rank, leaf, rhs, near, slots):
        self.group, self.bulk = mesh_group, mesh_bulk
        self.devices = mesh_group * mesh_bulk
        self.leaves, self.rank, self.leaf, self.rhs = leaves, rank, leaf, rhs
        self.near, self.slots = near, slots
        self.levels = leaves.bit_length()
        self.counts = [leaves >> level for level in range(self.levels)]
        self.offsets = [2 * leaves - 2 * count for count in self.counts]
        self.nodes = 2 * leaves - 1
        self.depth = self.devices.bit_length() - 1
        self.top = mesh_group.bit_length() - 1
        self.half = halves(leaves)
        self.message_c = []
        at = self.half * leaf
        for count in self.counts:
            self.message_c.append(at)
            at += halves(count) * rank
        self.message_term = -(-at // 128) * 128
        self.message = self.message_term + -(-rank // 128) * 128
        self.packed = -(-self.nodes * rank // 128) * 128
        self.ext_counts = [count + 2 * halves(count) for count in self.counts]
        self.ext_offsets = [sum(self.ext_counts[:i]) for i in range(self.levels)]
        self.ext_nodes = sum(self.ext_counts)
        self.upper_levels = list(range(1, self.depth))

    def level_size(self, level):
        return self.bulk >> (self.depth - level) if level > self.top else 1 << level

    def level_slots(self, level):
        return min(self.slots, self.level_size(level) - 1)

    def anchor(self, device, level):
        return (self.devices + device) >> (self.depth - level)


def up_kernel(
    z, info_ref, near_list, near_count, inter_list, inter_count, upper_list, upper_count,
    rhs_ref, pts_ref, basis_ref, transfer_ref, skel_ref,
    near_msg, far_msg, own_ref, term_ref, items_ref, halo_ref, bounds_ref, slots_ref, upper_ref,
):
    device = info_ref[0]
    parity = device % 2
    pair = 2 * z.rank
    rows, spare = slice(0, z.rhs), slice(z.rhs, z.rhs + 8)
    coords = slice(z.rhs, z.rhs + 3)
    own_ref[spare, :] = jnp.zeros((8, z.packed), f32)
    for node in range(z.nodes):
        own_ref[coords, node * z.rank : (node + 1) * z.rank] = skel_ref[:, node, :]
    pieces = []
    for leaf in range(z.leaves):
        at = leaf * z.leaf
        pieces.append(matmul(rhs_ref[:, at : at + z.leaf], basis_ref[leaf], 1, 1))
    for level in range(z.levels):
        first = z.offsets[level]
        if len(pieces) == 1:
            own_ref[rows, first * z.rank : (first + 1) * z.rank] = pieces[0]
            break
        raised = []
        for i in range(len(pieces) // 2):
            both = jnp.concatenate([pieces[2 * i], pieces[2 * i + 1]], axis=1)
            node = first + 2 * i
            own_ref[rows, node * z.rank : node * z.rank + pair] = both
            raised.append(matmul(both, transfer_ref[node : node + 2].reshape(pair, z.rank)))
        pieces = raised
    term = matmul(pieces[0], transfer_ref[z.nodes - 1])
    term_ref[...] = term
    width = z.half * z.leaf
    for ref, other in ((near_msg, 0), (far_msg, 1)):
        last = (parity + 1 + other) % 2
        at = pl.multiple_of(last * ((z.leaves - z.half) * z.leaf), 128)
        ref[spare, :] = jnp.zeros((8, z.message), f32)
        ref[rows, 0:width] = rhs_ref[:, pl.ds(at, width)]
        ref[coords, 0:width] = pts_ref[:, pl.ds(at, width)]
        for level in range(z.levels):
            size = halves(z.counts[level]) * z.rank
            first = z.offsets[level] * z.rank
            shift = (z.counts[level] - halves(z.counts[level])) * z.rank
            here = slice(z.message_c[level], z.message_c[level] + size)
            low = own_ref[:, first : first + size]
            if shift:
                low = jnp.where(last == 1, own_ref[:, first + shift : first + shift + size], low)
            ref[:, here] = low
        ref[rows, z.message_term : z.message_term + z.rank] = term

    here = z.leaves
    for leaf in range(z.leaves):
        items_ref[leaf] = leaf * (z.leaves + 1)
    away = 0
    for leaf in range(z.leaves):
        count = near_count[leaf]
        for slot in range(z.near):
            source = near_list[leaf, slot] - device * z.leaves
            used = jnp.where(slot < count, 1, 0)
            inside = jnp.where((source >= 0) & (source < z.leaves), used, 0)
            items_ref[here] = leaf * z.leaves + jnp.clip(source, 0, z.leaves - 1)
            place_in_halo = jnp.where(source < 0, source + z.half, source - z.leaves + z.half)
            halo_ref[away] = leaf * 2 * z.half + jnp.clip(place_in_halo, 0, 2 * z.half - 1)
            here = here + inside
            away = away + used - inside
    bounds_ref[0] = here
    bounds_ref[1] = away
    bounds_ref[2] = device
    for level in range(z.levels):
        count, half, base = z.counts[level], halves(z.counts[level]), z.ext_offsets[level]
        for i in range(count):
            node = z.offsets[level] + i
            for slot in range(z.slots):
                at = inter_list[slot, node] - device * count + half
                slots_ref[node * z.slots + slot] = base + jnp.clip(at, 0, z.ext_counts[level] - 1)
            bounds_ref[3 + node] = inter_count[node]
    for k, level in enumerate(z.upper_levels):
        anchor = z.anchor(device, level)
        used = upper_count[anchor]
        for slot in range(z.level_slots(level)):
            upper_ref[k * z.slots + slot] = jnp.where(slot < used, upper_list[slot, anchor], -1)


def pair_kernel(z, bounds_ref, term_ref, a_ref, matrix_ref, out_ref):
    device = bounds_ref[2]
    term = term_ref[...] + a_ref[0 : z.rhs, z.message_term : z.message_term + z.rank]
    out_ref[0] = term
    for i, level in enumerate(range(z.depth - 1, z.top, -1)):
        term = matmul(term, matrix_ref[z.anchor(device, level)])
        out_ref[i + 1] = term


def pad8(block):
    return jnp.concatenate([block, jnp.zeros((8 - block.shape[0], block.shape[1]), f32)], axis=0)


def fill_sources(z, src, val, first, values, coords):
    high, low = split2(values * GAIN)
    features = source_features(coords)
    for i in range(values.shape[1] // z.leaf):
        here = slice(i * z.leaf, (i + 1) * z.leaf)
        val[first + i, 0 : z.rhs] = high[:, here]
        val[first + i, z.rhs : 2 * z.rhs] = low[:, here]
        src[first + i] = features[:, here].T.astype(bf16)


def own_kernel(z, rhs_ref, pts_ref, src, tgt, val, acc):
    coords = pad8(pts_ref[...])
    fill_sources(z, src, val, 0, rhs_ref[...], coords)
    features = target_features(coords).astype(bf16)
    for i in range(z.leaves):
        here = slice(i * z.leaf, (i + 1) * z.leaf)
        tgt[i] = features[:, here]
        acc[i] = NUGGET * rhs_ref[:, here]


def halo_kernel(z, bounds_ref, a_ref, b_ref, src, val):
    width = z.half * z.leaf
    parity = bounds_ref[2] % 2
    left = jnp.where(parity == 0, b_ref[:, 0:width], a_ref[:, 0:width])
    right = jnp.where(parity == 0, a_ref[:, 0:width], b_ref[:, 0:width])
    fill_sources(z, src, val, 0, left[0 : z.rhs], left[z.rhs : z.rhs + 8])
    fill_sources(z, src, val, z.half, right[0 : z.rhs], right[z.rhs : z.rhs + 8])


def run_items(z, list_ref, per_target, first, end, src, tgt, val, acc):
    def group(at, size):
        for k in range(size):
            item = list_ref[at + k]
            target, source = item // per_target, item % per_target
            kernel_high, kernel_low = split2(kernel_of(dot(src[source], tgt[target], 1, 0)))
            values = val[source]
            both = dot(values, kernel_high, 1, 0)
            low = dot(values[: z.rhs], kernel_low, 1, 0)
            acc[target] += both[: z.rhs] + both[z.rhs :] + low

    count = end - first
    groups = count // STEP

    def body(i, carry):
        group(first + i * STEP, STEP)
        return carry

    lax.fori_loop(0, groups, body, 0)
    at = first + groups * STEP
    size = STEP // 2
    while size:
        rest = count & size

        @pl.when(rest != 0)
        def _(at=at, size=size):
            group(at, size)

        at = at + rest
        size //= 2


def near_bounds(bounds_ref):
    here, away = bounds_ref[0], bounds_ref[1]
    total = here + away
    first = jnp.minimum(here, (total * NEAR_SHARES[0] // 16) // STEP * STEP)
    second = jnp.minimum(here, (total * NEAR_SHARES[1] // 16) // STEP * STEP)
    third = jnp.clip((total * NEAR_SHARES[2] // 16) - here, 0, away)
    return here, away, first, second, third


def near_kernel(z, part, items_ref, halo_ref, bounds_ref, tgt, src, val, *rest):
    here, away, first, second, third = near_bounds(bounds_ref)
    _, acc = rest[-2:]
    begin, end = ((0, first), (first, second), (second, here), (here, here))[part]
    if part < 3:
        run_items(z, items_ref, z.leaves, begin, end, src, tgt, val, acc)
    if part >= 2:
        begin, end = ((0, third), (third, away))[part - 2]
        run_items(z, halo_ref, 2 * z.half, begin, end, rest[0], tgt, rest[1], acc)


def packed(blocks):
    return blocks[0] if len(blocks) == 1 else jnp.concatenate(blocks, axis=1)


def couple(kernel_high, kernel_low, high, low):
    rows = high.shape[0]
    both = dot(jnp.concatenate([high, low], axis=0), kernel_high, 1, 1)
    return both[:rows] + both[rows:] + dot(high, kernel_low, 1, 1)


def local_kernel(z, bounds_ref, slots_ref, own_ref, a_ref, b_ref, out_ref, feats, vals, rows_ref):
    parity = bounds_ref[2] % 2
    rank = z.rank
    start, width = z.message_c[0], z.message_term - z.message_c[0]
    a, b = a_ref[:, start : start + width], b_ref[:, start : start + width]
    sides = [jnp.where(parity == 0, b, a), jnp.where(parity == 0, a, b)]
    own = own_ref[...]
    blank_features = jnp.zeros((FEATURES, rank), bf16)
    blank_values = jnp.zeros((2 * z.rhs, rank), bf16)

    def store(at, features, values):
        feats[0, at] = jnp.concatenate([features, blank_features], axis=1)
        feats[1, at] = jnp.concatenate([blank_features, features], axis=1)
        vals[0, at] = jnp.concatenate([values, blank_values], axis=1)
        vals[1, at] = jnp.concatenate([blank_values, values], axis=1)

    def prepared(block):
        high, low = split2(block[: z.rhs] * GAIN)
        return (
            source_features(block[z.rhs :]).astype(bf16),
            jnp.concatenate([high, low], axis=0),
        )

    side_tables = [prepared(side) for side in sides]
    own_features, own_values = prepared(own)
    vals[0, z.ext_nodes] = jnp.zeros((2 * z.rhs, 2 * rank), bf16)
    vals[1, z.ext_nodes] = jnp.zeros((2 * z.rhs, 2 * rank), bf16)
    for level in range(z.levels):
        count, half, base = z.counts[level], halves(z.counts[level]), z.ext_offsets[level]
        for i in range(half):
            at = z.message_c[level] - start + i * rank
            for (features, values), first in zip(side_tables, (base, base + half + count)):
                store(first + i, features[:, at : at + rank], values[:, at : at + rank])
        for i in range(count):
            at = (z.offsets[level] + i) * rank
            store(base + half + i, own_features[:, at : at + rank], own_values[:, at : at + rank])
    target = target_features(own[z.rhs :])
    for at in range(0, z.packed, 2 * rank):
        turned = target[:, at : at + 2 * rank].T.astype(bf16)
        rows_ref[at : at + 2 * rank] = turned
    for node in range(z.nodes):
        used = bounds_ref[3 + node]
        points, values = [], []
        for slot in range(0, z.slots, 2):
            at = [slots_ref[node * z.slots + slot + k] for k in range(2)]
            points.append(feats[0, at[0]] + feats[1, at[1]])
            at = [jnp.where(slot + k < used, at[k], z.ext_nodes) for k in range(2)]
            values.append(vals[0, at[0]] + vals[1, at[1]])
        rows = rows_ref[node * rank : (node + 1) * rank]
        high, low = split2(kernel_of(dot(rows, packed(points), 1, 0)))
        values = packed(values)
        both = dot(values, high, 1, 1)
        out_ref[node] = both[: z.rhs] + both[z.rhs :] + dot(values[: z.rhs], low, 1, 1)


def upper_kernels(z, k, level, device, upper_ref, skel_ref):
    anchor = z.anchor(device, level)
    target = target_features(pad8(skel_ref[:, anchor, :])).T.astype(bf16)
    points = []
    for slot in range(z.level_slots(level)):
        source = upper_ref[k * z.slots + slot]
        points.append(pad8(skel_ref[:, jnp.where(source < 0, anchor, source), :]))
    return split2(kernel_of(dot(target, source_features(packed(points)).astype(bf16), 1, 0)))


def upper_sources(z, k, level, device, upper_ref, table):
    anchor = z.anchor(device, level)
    coefs = []
    for slot in range(z.level_slots(level)):
        source = upper_ref[k * z.slots + slot]
        coefs.append(table(jnp.where(source < 0, 0, source ^ anchor)) * jnp.where(source < 0, 0.0, GAIN))
    return split2(packed(coefs))


def upper_widths(z):
    return [z.level_slots(level) * z.rank for level in z.upper_levels if level <= z.top and z.level_slots(level)]


def top_kernel(z, bounds_ref, upper_ref, skel_ref, *outs):
    device = bounds_ref[2]
    at = 0
    for k, level in enumerate(z.upper_levels):
        if level <= z.top and z.level_slots(level):
            outs[at][...], outs[at + 1][...] = upper_kernels(z, k, level, device, upper_ref, skel_ref)
            at += 2


def mid_kernel(z, bounds_ref, upper_ref, fields_ref, basis_ref, transfer_ref, skel_ref, matrix_ref, *rest):
    tables = rest[: z.depth - 1 - z.top]
    _, acc, weights = rest[-3:]
    device = bounds_ref[2]
    rank, rhs = z.rank, z.rhs
    row = lax.broadcasted_iota(jnp.int32, (rhs + rank, rank), 0)
    column = lax.broadcasted_iota(jnp.int32, (rhs + rank, rank), 1)
    path = jnp.where(row - rhs == column, 1.0, 0.0)
    none = jnp.zeros((rank, rank), f32)
    for k, level in enumerate(z.upper_levels):
        if level <= z.top:
            continue
        table = tables[z.depth - 1 - level]
        path = matmul(path, matrix_ref[z.anchor(device, level)], 1, 1)
        if z.level_slots(level):
            kernel_high, kernel_low = upper_kernels(z, k, level, device, upper_ref, skel_ref)
            high, low = upper_sources(z, k, level, device, upper_ref, lambda at: table[at])
            field = couple(kernel_high, kernel_low, high, low)
            path = path + jnp.concatenate([field, none], axis=0)
    path = matmul(path, transfer_ref[z.nodes - 1], 1, 1)
    paths = [path + jnp.concatenate([fields_ref[z.nodes - 1], none], axis=0)]
    for level in range(z.levels - 2, -1, -1):
        below = []
        for i, path in enumerate(paths):
            node = z.offsets[level] + 2 * i
            both = matmul(path, transfer_ref[node : node + 2].reshape(2 * rank, rank), 1, 1)
            for child in range(2):
                lower = both[:, child * rank : (child + 1) * rank]
                below.append(lower + jnp.concatenate([fields_ref[node + child], none], axis=0))
        paths = below
    for leaf in range(z.leaves):
        values = matmul(paths[leaf], basis_ref[leaf])
        acc[leaf] += values[:rhs]
        high, low = split2(values[rhs:])
        weights[0, leaf] = high
        weights[1, leaf] = low


def final_kernel(z, bounds_ref, upper_ref, acc, weights, matrix_ref, *rest):
    out_ref, rest = rest[-1], rest[:-1]
    pieces, kernels = rest[: z.top + 1], rest[z.top + 1 :]
    device = bounds_ref[2]
    current = [piece[j] for piece in pieces for j in range(piece.shape[0])]
    values = {z.top: current}
    for level in range(z.top, 1, -1):
        anchor = z.anchor(device, level)
        moved = [matmul(current[j], matrix_ref[anchor ^ j]) for j in range(len(current))]
        current = [moved[2 * j] + moved[2 * j + 1] for j in range(len(current) // 2)]
        values[level - 1] = current
    downward, at = None, 0
    for k, level in enumerate(z.upper_levels):
        if level > z.top:
            continue
        if z.level_slots(level):

            def table(place, level=level):
                chosen = jnp.zeros((z.rhs, z.rank), f32)
                for j in range(1, len(values[level])):
                    chosen = jnp.where(place == j, values[level][j], chosen)
                return chosen

            high, low = upper_sources(z, k, level, device, upper_ref, table)
            field = couple(kernels[at][...], kernels[at + 1][...], high, low)
            at += 2
        else:
            field = jnp.zeros((z.rhs, z.rank), f32)
        if downward is None:
            downward = field
        else:
            downward = field + matmul(downward, matrix_ref[z.anchor(device, level)], 1, 1)
    high, low = split2(downward)
    stacked = jnp.concatenate([high, low], axis=0)
    for leaf in range(z.leaves):
        both = dot(stacked, weights[0, leaf], 1, 0)
        value = both[: z.rhs] + both[z.rhs :] + dot(high, weights[1, leaf], 1, 0)
        out_ref[:, leaf * z.leaf : (leaf + 1) * z.leaf] = acc[leaf] + value


SMEM = pl.BlockSpec(memory_space=pltpu.SMEM)
VMEM = pl.BlockSpec(memory_space=pltpu.VMEM)


def on_chip(x):
    return pltpu.with_memory_space_constraint(x, pltpu.VMEM)


def scalars(x):
    return pltpu.with_memory_space_constraint(x, pltpu.SMEM)


def call(body, outs, smem, vmem, scratch=(), aliases=None, cost=1.0, in_hbm=False, out_hbm=False):
    many = isinstance(outs, (list, tuple))
    listed = list(outs) if many else [outs]
    specs = [SMEM if o.dtype == jnp.int32 else VMEM for o in listed]
    shapes = [
        jax.ShapeDtypeStruct(o.shape, o.dtype)
        if out_hbm
        else (pltpu.SMEM if o.dtype == jnp.int32 else pltpu.VMEM)(o.shape, o.dtype)
        for o in listed
    ]
    if not in_hbm:
        smem, vmem = map(scalars, smem), map(on_chip, vmem)
    smem, vmem = list(smem), list(vmem)
    return pl.pallas_call(
        body,
        out_shape=shapes if many else shapes[0],
        in_specs=[SMEM] * len(smem) + [VMEM] * len(vmem),
        out_specs=specs if many else specs[0],
        scratch_shapes=list(scratch),
        input_output_aliases=aliases or {},
        compiler_params=pltpu.CompilerParams(vmem_limit_bytes=16 << 20),
        cost_estimate=pl.CostEstimate(
            flops=int(cost * 1e8), bytes_accessed=int(cost * 3e6), transcendentals=0
        ),
    )(*smem, *vmem)


def flip(x, axis, bit):
    return lax.ppermute(x, axis, [(i, i ^ bit) for i in range(lax.axis_size(axis))])


def shape(*dims, dtype=f32):
    return jax.ShapeDtypeStruct(dims, dtype)


def on_device(
    right_sides,
    points,
    basis,
    transfer,
    skeleton,
    near_list,
    near_count,
    inter_list,
    inter_count,
    upper_transfer,
    upper_skeleton,
    upper_list,
    upper_count,
):
    z = Sizes(
        lax.axis_size("group"),
        lax.axis_size("bulk"),
        basis.shape[0],
        basis.shape[1],
        basis.shape[2],
        right_sides.shape[0],
        near_list.shape[1],
        inter_list.shape[1],
    )
    part = functools.partial
    integers = part(shape, dtype=jnp.int32)
    halfs = part(shape, dtype=bf16)
    info = lax.axis_index(AXES).astype(jnp.int32).reshape(1)
    skeleton, upper_skeleton = skeleton.transpose(1, 0, 2), upper_skeleton.transpose(1, 0, 2)
    message = shape(z.rhs + 8, z.message)

    to_partner, to_other, own, term, items, halo_items, bounds, slots, upper = call(
        part(up_kernel, z),
        [
            message,
            message,
            shape(z.rhs + 8, z.packed),
            shape(z.rhs, z.rank),
            integers(z.leaves * (z.near + 1) + 1),
            integers(z.leaves * z.near + 1),
            integers(3 + z.nodes),
            integers(z.nodes * z.slots),
            integers(len(z.upper_levels) * z.slots),
        ],
        [info, near_list, near_count, inter_list.T, inter_count, upper_list.T, upper_count],
        [right_sides, points, basis, transfer, skeleton],
        cost=2.0,
        in_hbm=True,
    )
    from_partner = flip(to_partner, "bulk", 1)
    sources = (2 * z.rhs, z.leaf)
    src, tgt, val, acc = call(
        part(own_kernel, z),
        [
            halfs(z.leaves, z.leaf, FEATURES),
            halfs(z.leaves, FEATURES, z.leaf),
            halfs(z.leaves, *sources),
            shape(z.leaves, z.rhs, z.leaf),
        ],
        [],
        [right_sides, points],
        cost=0.7,
    )
    terms = call(
        part(pair_kernel, z),
        shape(z.depth - z.top, z.rhs, z.rank),
        [bounds],
        [term, from_partner, upper_transfer],
        cost=0.3,
    )
    pairs = [(i, i + 1) for i in range(1, z.devices - 1, 2)]
    from_other = lax.ppermute(to_other, AXES, pairs + [(b, a) for a, b in pairs])

    whole_levels, partial = [], terms
    for bit in range(1, z.bulk.bit_length()):
        whole_levels.append([partial[:1]])
        partial = partial[1:]
        if bit == z.bulk.bit_length() - 1:
            break
        sizes = [sum(p.shape[0] for p in level) for level in whole_levels]
        sent = jnp.concatenate([p for level in whole_levels for p in level] + [partial], axis=0)
        received = flip(sent, "bulk", 1 << bit)
        at = 0
        for level, size in zip(whole_levels, sizes):
            level.append(received[at : at + size])
            at += size
        partial = partial + received[at:]
    top = whole_levels.pop()
    whole_levels = [jnp.concatenate(level, axis=0) for level in whole_levels]
    for bit in range(z.top):
        top.append(flip(jnp.concatenate(top, axis=0), "group", 1 << bit))

    def near(index, acc, more=()):
        arrays = [tgt, src, val, *more, acc]
        return call(
            part(near_kernel, z, index),
            shape(z.leaves, z.rhs, z.leaf),
            [items, halo_items, bounds],
            arrays,
            aliases={2 + len(arrays): 0},
            cost=2.0,
        )

    acc = near(0, acc)
    acc = near(1, acc)
    halo_tables = call(
        part(halo_kernel, z),
        [halfs(2 * z.half, z.leaf, FEATURES), halfs(2 * z.half, *sources)],
        [bounds],
        [from_partner, from_other],
        cost=0.5,
    )
    acc = near(2, acc, halo_tables)
    acc = near(3, acc, halo_tables)
    fields = call(
        part(local_kernel, z),
        shape(z.nodes, z.rhs, z.rank),
        [bounds, slots],
        [own, from_partner, from_other],
        scratch=[
            pltpu.VMEM((2, z.ext_nodes, FEATURES, 2 * z.rank), bf16),
            pltpu.VMEM((2, z.ext_nodes + 1, 2 * z.rhs, 2 * z.rank), bf16),
            pltpu.VMEM((z.packed, FEATURES), bf16),
        ],
        cost=1.5,
    )
    kernels = call(
        part(top_kernel, z),
        [halfs(z.rank, width) for width in upper_widths(z) for _ in range(2)],
        [bounds, upper],
        [upper_skeleton],
        cost=0.3,
    )
    acc, weights = call(
        part(mid_kernel, z),
        [shape(z.leaves, z.rhs, z.leaf), halfs(2, z.leaves, z.rank, z.leaf)],
        [bounds, upper],
        [fields, basis, transfer, upper_skeleton, upper_transfer, *whole_levels, acc],
        aliases={7 + len(whole_levels): 0},
        cost=1.0,
    )
    return call(
        part(final_kernel, z),
        shape(*right_sides.shape),
        [bounds, upper],
        [acc, weights, upper_transfer, *top, *kernels],
        cost=1.0,
        out_hbm=True,
    )


def solution(mesh):
    in_specs = (
        P(None, AXES),
        P(None, AXES),
        P(AXES, None, None),
        P(AXES, None, None),
        P(AXES, None, None),
        P(AXES, None),
        P(AXES),
        P(AXES, None),
        P(AXES),
        P(),
        P(),
        P(),
        P(),
    )
    return jax.shard_map(
        on_device, mesh=mesh, in_specs=in_specs, out_specs=P(None, AXES), check_vma=False
    )
```

time: 53.6 us -> 39.5 us (0.74); the launches traced: 54.2 us -> 39 us
  Pallas kernels: 21 us -> 14.8 us
  starting transfers between devices: 20.5 us -> 15.6 us
  other arithmetic: 2.67 us -> 0.04 us
  waiting for transfers between devices: 5.68 us -> 3.09 us
  local copies, waits for them, and re-layouts: 4.21 us -> 5.27 us
    pallas_call x4 -> x12, Pallas kernels: 21 us -> 14.8 us  [call(): pl.pallas_call(body, out_shape=shapes if many else shapes[0], in_specs=[S...]
    ppermute x5, starting transfers between devices: 19.9 us -> 14.9 us  [flip(): lax.ppermute(x, axis, [(i, i ^ bit) for i in range(lax.axis_size(axis))])]
    ppermute x5, waiting for transfers between devices: 5.68 us -> 3.08 us  [flip(): lax.ppermute(x, axis, [(i, i ^ bit) for i in range(lax.axis_size(axis))])]
    concatenate x5 -> x4, other arithmetic: 1.89 us -> 0.03 us  [the longest x2 0.02 us: on_device(): whole_levels = [jnp.concatenate(level, axis=0) for level in whole_levels]]
    unnamed x16 -> x32, local copies, waits for them, and re-layouts: 4.11 us -> 5.26 us
    add x1 -> x0, other arithmetic: 0.76 us -> none  [on_device(): whole_levels, partial = ([], terms + theirs)]
  transfers between devices with their start and end apart: 6 -> 6, of which waited for: 4 -> 3; matrix products, arithmetic and copies ran while one was open for 6% -> 0% of each run, Pallas kernels for 25% -> 28%
where the time goes in v2:
time: 39.5 us; the launch traced here: 39 us
  starting transfers between devices  15.6 us (39%)
  Pallas kernels  14.8 us (37%)
  local copies, waits for them, and re-layouts  5.27 us (13%)
  waiting for transfers between devices  3.09 us (8%)
    ppermute x5, starting transfers between devices, flip(): lax.ppermute(x, axis, [(i, i ^ bit) for i in range(lax.axis_size(axis))])  14.9 us
    pallas_call x12, Pallas kernels, call(): pl.pallas_call(body, out_shape=shapes if many else shapes[0], in_specs=[S...  14.8 us
    unnamed x32, local copies, waits for them, and re-layouts  5.26 us
    ppermute x5, waiting for transfers between devices, flip(): lax.ppermute(x, axis, [(i, i ^ bit) for i in range(lax.axis_size(axis))])  3.08 us
  transfers between devices with their start and end apart: 6, of which 3 were waited for; matrix products, arithmetic and copies ran while one was open for 0% of the time, Pallas kernels for 28%

profile of v2, /device:TPU:0, one launch (start us, length us, event | category | flops | bytes accessed | tf_op | source)
XLA Modules:
  0.0 39.0 jit_solution(17227121626174504305)
XLA Ops:
  0.0 0.0 copy-start.15
  0.0 0.0 copy-start.12
  0.0 0.0 copy-start.11
  0.0 0.0 copy-start.10
  0.0 0.0 copy-start.14
  0.0 0.6 %copy-done.15 = s32[32]{0:T(128)S(1)} copy-done((s32[32]{0:T(128)S(1)}, s32[32]{0:T(128)}, u32[]{:S(2)}) %copy-start.15) | copy-done | bytes 152
  0.7 0.0 copy-done.12
  0.7 0.0 copy-done.11
  0.7 0.0 copy-done.10
  0.7 0.0 copy-done.13
  0.7 0.0 copy-done.14
  0.7 0.0 copy-start.1
  0.7 1.0 %copy-done.1 = f32[8,64,256]{2,1,0:T(8,128)S(1)} copy-done((f32[8,64,256]{2,1,0:T(8,128)S(1)}, f32[8,64,256]{2,1,0:T(8,128)}, u32[]{:S(2)}) %copy-start.1) | copy-done | bytes 524312
  1.8 0.0 copy-start.3
  1.8 1.0 %copy-done.3 = f32[15,64,64]{2,1,0:T(8,128)S(1)} copy-done((f32[15,64,64]{2,1,0:T(8,128)S(1)}, f32[15,64,64]{2,1,0:T(8,128)}, u32[]{:S(2)}) %copy-start.3) | copy-done | bytes 245784
  2.8 0.9 %copy-done.5 = f32[32,2048]{1,0:T(8,128)S(1)} copy-done((f32[32,2048]{1,0:T(8,128)S(1)}, f32[32,2048]{1,0:T(8,128)}, u32[]{:S(2)}) %copy-start.5) | copy-done | bytes 262168
  3.8 0.8 %copy-done.7 = f32[3,2048]{1,0:T(4,128)S(1)} copy-done((f32[3,2048]{1,0:T(4,128)S(1)}, f32[3,2048]{1,0:T(4,128)}, u32[]{:S(2)}) %copy-start.7) | copy-done | bytes 24600
  4.5 0.7 %copy-done.9 = f32[15,3,64]{2,0,1:T(8,128)S(1)} copy-done((f32[15,3,64]{2,0,1:T(8,128)S(1)}, f32[15,3,64]{2,0,1:T(8,128)}, u32[]{:S(2)}) %copy-start.9) | copy-done | bytes 11544
  5.3 2.6 %shard_map.127 = (f32[40,1664]{1,0:T(8,128)S(1)}, f32[40,1664]{1,0:T(8,128)S(1)}, f32[40,1024]{1,0:T(8,128)S(1)}, f32[32,64]{1,0:T(8,128)S(1)}, s32[73]{0:T(128)...) custom-call(s32[1]{0:T(128)} %bitcast.info_ref, s32[8,8]{1,0:T(8,128)S(1)} %copy-done.10, ...), custom_call_target="tpu_custom_call" | custom-call | flops 200000000 | bytes 6000000 | tf_op jit(solution)/shard_map/pallas_call | solution.py:504
  7.8 0.6 %collective-permute-start = (f32[40,1664]{1,0:T(8,128)S(1)}, f32[40,1664]{1,0:T(8,128)S(1)}, u32[]{:S(2)}, u32[]{:S(2)}) collective-permute-start(f32[40,1664]{1,0:T(8,128)S(1)} %get-tuple-element.30), channel_id=1, source_target_pairs={{0,1},{1,0},{2,3},{3,2},{4,5},{5,4},{6,7},{7,6},{8,9},{9,8},{10,11... | collective-permute-start | bytes 798728 | tf_op jit(solution)/shard_map/ppermute | solution.py:519
  8.4 0.7 %collective-permute-start.1 = (f32[40,1664]{1,0:T(8,128)S(1)}, f32[40,1664]{1,0:T(8,128)S(1)}, u32[]{:S(2)}, u32[]{:S(2)}) collective-permute-start(f32[40,1664]{1,0:T(8,128)S(1)} %get-tuple-element.31), channel_id=1, source_target_pairs={{1,2},{3,4},{5,6},{7,8},{9,10},{11,12},{13,14},{15,16},{17,18},{19... | collective-permute-start | bytes 798728 | tf_op jit(solution)/shard_map/ppermute | solution.py:598
  9.1 0.0 copy-done.6
  9.1 0.3 shard_map.130
  9.4 1.2 %shard_map.132.rest_0_ = f32[8,32,256]{2,1,0:T(8,128)S(1)} custom-call(s32[73]{0:T(128)S(4)} %get-tuple-element.33.items_ref, s32[65]{0:T(128)S(4)} %get-tuple-element.34.halo_ref, s32[18]{0:T(128)S(4)} %get-tuple-element.26.bounds_ref, bf16[8,48,256]{2,1,0:T(8,128)(2,1)S(1)} %get-tuple-element.35.tgt, ...), custom_call_target="tpu_custom_call", output_to_operand_aliasing={{}: (6, {})} | custom-call | flops 200000000 | bytes 6000000 | tf_op jit(solution)/shard_map/pallas_call | solution.py:504
  10.7 1.3 %shard_map.133.rest_2_ = f32[8,32,256]{2,1,0:T(8,128)S(1)} custom-call(s32[73]{0:T(128)S(4)} %get-tuple-element.33.items_ref, s32[65]{0:T(128)S(4)} %get-tuple-element.34.halo_ref, s32[18]{0:T(128)S(4)} %get-tuple-element.26.bounds_ref, bf16[8,48,256]{2,1,0:T(8,128)(2,1)S(1)} %get-tuple-element.35.tgt, ...), custom_call_target="tpu_custom_call", output_to_operand_aliasing={{}: (6, {})} | custom-call | flops 200000000 | bytes 6000000 | tf_op jit(solution)/shard_map/pallas_call | solution.py:504
  11.9 0.0 collective-permute-done.a_ref
  11.9 0.0 copy-done
  12.0 0.0 copy-start.8
  12.0 0.3 shard_map.129
  12.2 3.2 %collective-permute-start.2 = (f32[3,32,64]{2,1,0:T(8,128)S(1)}, f32[3,32,64]{2,1,0:T(8,128)S(1)}, u32[]{:S(2)}, u32[]{:S(2)}) collective-permute-start(f32[3,32,64]{2,1,0:T(8,128)S(1)} %shard_map.129), channel_id=1, source_target_pairs={{0,2},{1,3},{2,0},{3,1},{4,6},{5,7},{6,4},{7,5},{8,10},{9,11},{10,... | collective-permute-start | bytes 73736 | tf_op jit(solution)/shard_map/ppermute | solution.py:519
  15.5 0.0 copy-done.8
  15.5 0.3 shard_map.137
  15.7 0.0 collective-permute-done.1.b_ref
  15.8 0.3 shard_map.131
  16.1 2.2 %shard_map.134.rest_2_ = f32[8,32,256]{2,1,0:T(8,128)S(1)} custom-call(s32[73]{0:T(128)S(4)} %get-tuple-element.33.items_ref, s32[65]{0:T(128)S(4)} %get-tuple-element.34.halo_ref, s32[18]{0:T(128)S(4)} %get-tuple-element.26.bounds_ref, bf16[8,48,256]{2,1,0:T(8,128)(2,1)S(1)} %get-tuple-element.35.tgt, ...), custom_call_target="tpu_custom_call", output_to_operand_aliasing={{}: (8, {})} | custom-call | flops 200000000 | bytes 6000000 | tf_op jit(solution)/shard_map/pallas_call | solution.py:504
  18.3 0.3 collective-permute-done.2
  18.6 5.7 %collective-permute-start.3 = (f32[4,32,64]{2,1,0:T(8,128)S(1)}, f32[4,32,64]{2,1,0:T(8,128)S(1)}, u32[]{:S(2)}, u32[]{:S(2)}) collective-permute-start(f32[4,32,64]{2,1,0:T(8,128)S(1)} %pad_maximum_fusion), channel_id=1, source_target_pairs={{0,4},{1,5},{2,6},{3,7},{4,0},{5,1},{6,2},{7,3},{8,12},{9,13},{10,... | collective-permute-start | bytes 98312 | tf_op jit(solution)/shard_map/ppermute | solution.py:519
  24.3 2.7 %shard_map.128.fields_ref = f32[15,32,64]{2,1,0:T(8,128)S(1)} custom-call(s32[18]{0:T(128)S(4)} %get-tuple-element.26.bounds_ref, s32[120]{0:T(128)S(4)} %get-tuple-element.28.slots_ref, f32[40,1024]{1,0:T(8,128)S(1)} %get-tuple-element.29.own_ref, f32[40,1664]{1,0:T(8,128)S(1)} %collective-permute-done.a_ref, f32[40,1664]{1,0:T(8,128)S(1)} %collective-permute-done.1.b_ref), custom_call_target="tpu_custom_call" | custom-call | flops 150000000 | bytes 4500000 | tf_op jit(solution)/shard_map/pallas_call | solution.py:504
  27.0 0.5 %shard_map.135.rest_2_ = f32[8,32,256]{2,1,0:T(8,128)S(1)} custom-call(s32[73]{0:T(128)S(4)} %get-tuple-element.33.items_ref, s32[65]{0:T(128)S(4)} %get-tuple-element.34.halo_ref, s32[18]{0:T(128)S(4)} %get-tuple-element.26.bounds_ref, bf16[8,48,256]{2,1,0:T(8,128)(2,1)S(1)} %get-tuple-element.35.tgt, ...), custom_call_target="tpu_custom_call", output_to_operand_aliasing={{}: (8, {})} | custom-call | flops 200000000 | bytes 6000000 | tf_op jit(solution)/shard_map/pallas_call | solution.py:504
  27.5 1.1 %collective-permute-done.3 = f32[4,32,64]{2,1,0:T(8,128)S(1)} collective-permute-done((f32[4,32,64]{2,1,0:T(8,128)S(1)}, f32[4,32,64]{2,1,0:T(8,128)S(1)}, u32[]{:S(2)}, u32[]{:S(2)}) %collective-permute-start.3) | collective-permute-done | bytes 32800 | tf_op jit(solution)/shard_map/ppermute | solution.py:519
  28.6 2.4 %collective-permute-start.4 = (f32[1,32,64]{2,1,0:T(8,128)S(1)}, f32[1,32,64]{2,1,0:T(8,128)S(1)}, u32[]{:S(2)}, u32[]{:S(2)}) collective-permute-start(f32[1,32,64]{2,1,0:T(8,128)S(1)} %get-tuple-element.47.rest_0_), channel_id=1, source_target_pairs={{0,8},{8,0},{16,24},{24,16},{1,9},{9,1},{17,25},{25,17},{2,10},{10... | collective-permute-start | bytes 24584 | tf_op jit(solution)/shard_map/ppermute | solution.py:519
  31.0 1.7 %collective-permute-done.4.rest_1_ = f32[1,32,64]{2,1,0:T(8,128)S(1)} collective-permute-done((f32[1,32,64]{2,1,0:T(8,128)S(1)}, f32[1,32,64]{2,1,0:T(8,128)S(1)}, u32[]{:S(2)}, u32[]{:S(2)}) %collective-permute-start.4) | collective-permute-done | bytes 8224 | tf_op jit(solution)/shard_map/ppermute | solution.py:519
  32.7 3.0 %collective-permute-start.5 = (f32[2,32,64]{2,1,0:T(8,128)S(1)}, f32[2,32,64]{2,1,0:T(8,128)S(1)}, u32[]{:S(2)}, u32[]{:S(2)}) collective-permute-start(f32[2,32,64]{2,1,0:T(8,128)S(1)} %pad_maximum_fusion.4), channel_id=1, source_target_pairs={{0,16},{8,24},{16,0},{24,8},{1,17},{9,25},{17,1},{25,9},{2,18},{10... | collective-permute-start | bytes 49160 | tf_op jit(solution)/shard_map/ppermute | solution.py:519
  35.7 0.0 copy-done.2
  35.7 0.0 copy-done.4
  35.7 1.9 %shard_map.136 = (f32[8,32,256]{2,1,0:T(8,128)S(1)}, bf16[2,8,64,256]{3,2,1,0:T(8,128)(2,1)S(1)}) custom-call(s32[18]{0:T(128)S(4)} %get-tuple-element.26.bounds_ref, s32[32]{0:T(128)S(4)} %get-tuple-element.27.upper_ref, f32[15,32,64]{2,1,0:T(8,128)S(1)} %shard_map.128.fields_ref, f32[8,64,256]{2,1,0:T(8,128)S(1)} %copy-done.2, ...), custom_call_target="tpu_custom_call", output_to_operand_aliasing={{0}: (9, {})} | custom-call | flops 100000000 | bytes 3000000 | tf_op jit(solution)/shard_map/pallas_call | solution.py:504
  37.6 0.0 collective-permute-done.5.rest_2_
  37.6 1.4 %shard_map.138 = f32[32,2048]{1,0:T(8,128)} custom-call(s32[18]{0:T(128)S(4)} %get-tuple-element.26.bounds_ref, s32[32]{0:T(128)S(4)} %get-tuple-element.27.upper_ref, f32[8,32,256]{2,1,0:T(8,128)S(1)} %get-tuple-element.41.acc, bf16[2,8,64,256]{3,2,1,0:T(8,128)(2,1)S(1)} %get-tuple-element.42.weights, f32[32,64,64]{2,1,0:T(8,128)S(1)} %copy-done, ...), custom_call_target="tpu_custom_call" | custom-call | flops 100000000 | bytes 3000000 | tf_op jit(solution)/shard_map/pallas_call | solution.py:504
  (17 shorter events, 0.1 us)
Async XLA Ops:
  0.0 0.7 %copy-start.15 = (s32[32]{0:T(128)S(1)}, s32[32]{0:T(128)}, u32[]{:S(2)}) copy-start(s32[32]{0:T(128)} %upper_count.1) | copy-start | bytes 388
  0.0 0.7 %copy-start.12 = (s32[32,8]{0,1:T(8,128)S(1)}, s32[32,8]{0,1:T(8,128)}, u32[]{:S(2)}) copy-start(s32[32,8]{0,1:T(8,128)} %param.24) | copy-start | bytes 3076
  0.0 0.7 %copy-start.11 = (s32[15,8]{0,1:T(8,128)S(1)}, s32[15,8]{0,1:T(8,128)}, u32[]{:S(2)}) copy-start(s32[15,8]{0,1:T(8,128)} %param.20) | copy-start | bytes 1444
  0.0 0.7 %copy-start.10 = (s32[8,8]{1,0:T(8,128)S(1)}, s32[8,8]{1,0:T(8,128)}, u32[]{:S(2)}) copy-start(s32[8,8]{1,0:T(8,128)} %near_list.1) | copy-start | bytes 772
  0.0 0.7 %copy-start.13 = (s32[8]{0:T(128)S(1)}, s32[8]{0:T(128)}, u32[]{:S(2)}) copy-start(s32[8]{0:T(128)} %near_count.1) | copy-start | bytes 100
  0.0 0.7 %copy-start.14 = (s32[15]{0:T(128)S(1)}, s32[15]{0:T(128)}, u32[]{:S(2)}) copy-start(s32[15]{0:T(128)} %inter_count.1) | copy-start | bytes 184
  0.7 1.0 %copy-start.1 = (f32[8,64,256]{2,1,0:T(8,128)S(1)}, f32[8,64,256]{2,1,0:T(8,128)}, u32[]{:S(2)}) copy-start(f32[8,64,256]{2,1,0:T(8,128)} %basis_ref.3) | copy-start | bytes 1572868
  1.8 1.0 %copy-start.3 = (f32[15,64,64]{2,1,0:T(8,128)S(1)}, f32[15,64,64]{2,1,0:T(8,128)}, u32[]{:S(2)}) copy-start(f32[15,64,64]{2,1,0:T(8,128)} %transfer_ref.3) | copy-start | bytes 737284
  2.8 0.9 %copy-start.5 = (f32[32,2048]{1,0:T(8,128)S(1)}, f32[32,2048]{1,0:T(8,128)}, u32[]{:S(2)}) copy-start(f32[32,2048]{1,0:T(8,128)} %rhs_ref.3) | copy-start | bytes 786436
  3.8 0.8 %copy-start.7 = (f32[3,2048]{1,0:T(4,128)S(1)}, f32[3,2048]{1,0:T(4,128)}, u32[]{:S(2)}) copy-start(f32[3,2048]{1,0:T(4,128)} %pts_ref.3) | copy-start | bytes 73732
  4.5 0.7 %copy-start.9 = (f32[15,3,64]{2,0,1:T(8,128)S(1)}, f32[15,3,64]{2,0,1:T(8,128)}, u32[]{:S(2)}) copy-start(f32[15,3,64]{2,0,1:T(8,128)} %param.17) | copy-start | bytes 34564
  5.3 3.8 %copy-start.6 = (f32[32,2048]{1,0:T(8,128)S(1)}, f32[32,2048]{1,0:T(8,128)}, u32[]{:S(2)}) copy-start(f32[32,2048]{1,0:T(8,128)} %rhs_ref.3) | copy-start | bytes 786436
  7.8 4.1 %collective-permute-start = (f32[40,1664]{1,0:T(8,128)S(1)}, f32[40,1664]{1,0:T(8,128)S(1)}, u32[]{:S(2)}, u32[]{:S(2)}) collective-permute-start(f32[40,1664]{1,0:T(8,128)S(1)} %get-tuple-element.30), channel_id=1, source_target_pairs={{0,1},{1,0},{2,3},{3,2},{4,5},{5,4},{6,7},{7,6},{8,9},{9,8},{10,11... | collective-permute-start | bytes 798728 | tf_op jit(solution)/shard_map/ppermute | solution.py:519
  8.4 7.3 %collective-permute-start.1 = (f32[40,1664]{1,0:T(8,128)S(1)}, f32[40,1664]{1,0:T(8,128)S(1)}, u32[]{:S(2)}, u32[]{:S(2)}) collective-permute-start(f32[40,1664]{1,0:T(8,128)S(1)} %get-tuple-element.31), channel_id=1, source_target_pairs={{1,2},{3,4},{5,6},{7,8},{9,10},{11,12},{13,14},{15,16},{17,18},{19... | collective-permute-start | bytes 798728 | tf_op jit(solution)/shard_map/ppermute | solution.py:598
  10.6 1.3 %copy-start = (f32[32,64,64]{2,1,0:T(8,128)S(1)}, f32[32,64,64]{2,1,0:T(8,128)}, u32[]{:S(2)}) copy-start(f32[32,64,64]{2,1,0:T(8,128)} %matrix_ref.5) | copy-start | bytes 1572868
  12.0 3.5 %copy-start.8 = (f32[32,3,64]{2,0,1:T(8,128)S(1)}, f32[32,3,64]{2,0,1:T(8,128)}, u32[]{:S(2)}) copy-start(f32[32,3,64]{2,0,1:T(8,128)} %param.23) | copy-start | bytes 73732
  12.2 6.3 %collective-permute-start.2 = (f32[3,32,64]{2,1,0:T(8,128)S(1)}, f32[3,32,64]{2,1,0:T(8,128)S(1)}, u32[]{:S(2)}, u32[]{:S(2)}) collective-permute-start(f32[3,32,64]{2,1,0:T(8,128)S(1)} %shard_map.129), channel_id=1, source_target_pairs={{0,2},{1,3},{2,0},{3,1},{4,6},{5,7},{6,4},{7,5},{8,10},{9,11},{10,... | collective-permute-start | bytes 73736 | tf_op jit(solution)/shard_map/ppermute | solution.py:519
  18.6 10.0 %collective-permute-start.3 = (f32[4,32,64]{2,1,0:T(8,128)S(1)}, f32[4,32,64]{2,1,0:T(8,128)S(1)}, u32[]{:S(2)}, u32[]{:S(2)}) collective-permute-start(f32[4,32,64]{2,1,0:T(8,128)S(1)} %pad_maximum_fusion), channel_id=1, source_target_pairs={{0,4},{1,5},{2,6},{3,7},{4,0},{5,1},{6,2},{7,3},{8,12},{9,13},{10,... | collective-permute-start | bytes 98312 | tf_op jit(solution)/shard_map/ppermute | solution.py:519
  27.0 8.7 %copy-start.2 = (f32[8,64,256]{2,1,0:T(8,128)S(1)}, f32[8,64,256]{2,1,0:T(8,128)}, u32[]{:S(2)}) copy-start(f32[8,64,256]{2,1,0:T(8,128)} %basis_ref.3) | copy-start | bytes 1572868
  27.0 8.7 %copy-start.4 = (f32[15,64,64]{2,1,0:T(8,128)S(1)}, f32[15,64,64]{2,1,0:T(8,128)}, u32[]{:S(2)}) copy-start(f32[15,64,64]{2,1,0:T(8,128)} %transfer_ref.3) | copy-start | bytes 737284
  28.6 4.1 %collective-permute-start.4 = (f32[1,32,64]{2,1,0:T(8,128)S(1)}, f32[1,32,64]{2,1,0:T(8,128)S(1)}, u32[]{:S(2)}, u32[]{:S(2)}) collective-permute-start(f32[1,32,64]{2,1,0:T(8,128)S(1)} %get-tuple-element.47.rest_0_), channel_id=1, source_target_pairs={{0,8},{8,0},{16,24},{24,16},{1,9},{9,1},{17,25},{25,17},{2,10},{10... | collective-permute-start | bytes 24584 | tf_op jit(solution)/shard_map/ppermute | solution.py:519
  32.7 4.9 %collective-permute-start.5 = (f32[2,32,64]{2,1,0:T(8,128)S(1)}, f32[2,32,64]{2,1,0:T(8,128)S(1)}, u32[]{:S(2)}, u32[]{:S(2)}) collective-permute-start(f32[2,32,64]{2,1,0:T(8,128)S(1)} %pad_maximum_fusion.4), channel_id=1, source_target_pairs={{0,16},{8,24},{16,0},{24,8},{1,17},{9,25},{17,1},{25,9},{2,18},{10... | collective-permute-start | bytes 49160 | tf_op jit(solution)/shard_map/ppermute | solution.py:519

commit v3 on v2

--- a/solution.py
+++ b/solution.py
@@ -7,6 +7,7 @@
 from jax.experimental import pallas as pl
 from jax.experimental.pallas import tpu as pltpu
 from jax.sharding import PartitionSpec as P
+
 
 AMPLITUDE = 0.2
 KERNEL_RATE = 2.0
@@ -18,7 +19,7 @@
 GAIN = AMPLITUDE * math.log(2.0)
 FEATURES = 48
 STEP = 4
-NEAR_SHARES = (5, 10, 13)
+NEAR_SHARES = (5, 10)
 AXES = ("group", "bulk")
 
 f32 = jnp.float32
@@ -102,6 +103,7 @@
         self.depth = self.devices.bit_length() - 1
         self.top = mesh_group.bit_length() - 1
         self.half = halves(leaves)
+        assert 2 * self.half == leaves and leaves & (leaves - 1) == 0
         self.message_c = []
         at = self.half * leaf
         for count in self.counts:
@@ -111,8 +113,6 @@
         self.message = self.message_term + -(-rank // 128) * 128
         self.packed = -(-self.nodes * rank // 128) * 128
         self.ext_counts = [count + 2 * halves(count) for count in self.counts]
-        self.ext_offsets = [sum(self.ext_counts[:i]) for i in range(self.levels)]
-        self.ext_nodes = sum(self.ext_counts)
         self.upper_levels = list(range(1, self.depth))
 
     def level_size(self, level):
@@ -126,12 +126,59 @@
 
 
 def up_kernel(
-    z, info_ref, near_list, near_count, inter_list, inter_count, upper_list, upper_count,
-    rhs_ref, pts_ref, basis_ref, transfer_ref, skel_ref,
-    near_msg, far_msg, own_ref, term_ref, items_ref, halo_ref, bounds_ref, slots_ref, upper_ref,
+    z, info_ref, near_list_in, near_count_in, upper_list_in, upper_count_in,
+    rhs_in, pts_in, basis_in, transfer_in, skel_in, inter_list_in, inter_count_in, upper_skel_in,
+    near_msg, far_msg, own_ref, term_ref, items_ref, halo_ref, bounds_ref, upper_ref,
+    rhs_ref, pts_ref, basis_ref, transfer_ref, inter_list_ref, inter_count_ref, upper_skel_ref,
+    skel_ref, near_list, near_count, upper_list, upper_count, sems,
 ):
+    moves = (
+        (near_list_in, near_list),
+        (near_count_in, near_count),
+        (upper_list_in, upper_list),
+        (upper_count_in, upper_count),
+        (rhs_in, rhs_ref),
+        (basis_in, basis_ref),
+        (transfer_in, transfer_ref),
+        (skel_in, skel_ref),
+        (pts_in, pts_ref),
+        (inter_list_in, inter_list_ref),
+        (inter_count_in, inter_count_ref),
+        (upper_skel_in, upper_skel_ref),
+    )
+    copies = [pltpu.make_async_copy(*move, sems.at[i]) for i, move in enumerate(moves)]
+    for copy in copies:
+        copy.start()
+    for copy in copies[:4]:
+        copy.wait()
     device = info_ref[0]
     parity = device % 2
+    for leaf in range(z.leaves):
+        items_ref[leaf] = leaf * (z.leaves + 1)
+    here = jnp.int32(z.leaves)
+    away = jnp.int32(0)
+    base = device * z.leaves
+    for leaf in range(z.leaves):
+        count = near_count[leaf]
+        for slot in range(z.near):
+            source = near_list[leaf, slot] - base
+            used = (slot < count).astype(jnp.int32)
+            inside = jnp.where(source // z.leaves == 0, used, 0)
+            items_ref[here] = source + leaf * z.leaves
+            halo_ref[away] = jnp.bitwise_and(source + z.half, 2 * z.half - 1) + leaf * 2 * z.half
+            here = here + inside
+            away = away + used - inside
+    bounds_ref[0] = here
+    bounds_ref[1] = away
+    bounds_ref[2] = device
+    for k, level in enumerate(z.upper_levels):
+        anchor = z.anchor(device, level)
+        used = upper_count[anchor]
+        for slot in range(z.level_slots(level)):
+            upper_ref[k * z.slots + slot] = jnp.where(slot < used, upper_list[slot, anchor], -1)
+
+    for copy in copies[4:]:
+        copy.wait()
     pair = 2 * z.rank
     rows, spare = slice(0, z.rhs), slice(z.rhs, z.rhs + 8)
     coords = slice(z.rhs, z.rhs + 3)
@@ -174,38 +221,6 @@
             ref[:, here] = low
         ref[rows, z.message_term : z.message_term + z.rank] = term
 
-    here = z.leaves
-    for leaf in range(z.leaves):
-        items_ref[leaf] = leaf * (z.leaves + 1)
-    away = 0
-    for leaf in range(z.leaves):
-        count = near_count[leaf]
-        for slot in range(z.near):
-            source = near_list[leaf, slot] - device * z.leaves
-            used = jnp.where(slot < count, 1, 0)
-            inside = jnp.where((source >= 0) & (source < z.leaves), used, 0)
-            items_ref[here] = leaf * z.leaves + jnp.clip(source, 0, z.leaves - 1)
-            place_in_halo = jnp.where(source < 0, source + z.half, source - z.leaves + z.half)
-            halo_ref[away] = leaf * 2 * z.half + jnp.clip(place_in_halo, 0, 2 * z.half - 1)
-            here = here + inside
-            away = away + used - inside
-    bounds_ref[0] = here
-    bounds_ref[1] = away
-    bounds_ref[2] = device
-    for level in range(z.levels):
-        count, half, base = z.counts[level], halves(z.counts[level]), z.ext_offsets[level]
-        for i in range(count):
-            node = z.offsets[level] + i
-            for slot in range(z.slots):
-                at = inter_list[slot, node] - device * count + half
-                slots_ref[node * z.slots + slot] = base + jnp.clip(at, 0, z.ext_counts[level] - 1)
-            bounds_ref[3 + node] = inter_count[node]
-    for k, level in enumerate(z.upper_levels):
-        anchor = z.anchor(device, level)
-        used = upper_count[anchor]
-        for slot in range(z.level_slots(level)):
-            upper_ref[k * z.slots + slot] = jnp.where(slot < used, upper_list[slot, anchor], -1)
-
 
 def pair_kernel(z, bounds_ref, term_ref, a_ref, matrix_ref, out_ref):
     device = bounds_ref[2]
@@ -281,24 +296,14 @@
         size //= 2
 
 
-def near_bounds(bounds_ref):
+def near_kernel(z, part, items_ref, halo_ref, bounds_ref, tgt, src, val, *rest):
     here, away = bounds_ref[0], bounds_ref[1]
-    total = here + away
-    first = jnp.minimum(here, (total * NEAR_SHARES[0] // 16) // STEP * STEP)
-    second = jnp.minimum(here, (total * NEAR_SHARES[1] // 16) // STEP * STEP)
-    third = jnp.clip((total * NEAR_SHARES[2] // 16) - here, 0, away)
-    return here, away, first, second, third
-
-
-def near_kernel(z, part, items_ref, halo_ref, bounds_ref, tgt, src, val, *rest):
-    here, away, first, second, third = near_bounds(bounds_ref)
-    _, acc = rest[-2:]
-    begin, end = ((0, first), (first, second), (second, here), (here, here))[part]
-    if part < 3:
-        run_items(z, items_ref, z.leaves, begin, end, src, tgt, val, acc)
-    if part >= 2:
-        begin, end = ((0, third), (third, away))[part - 2]
-        run_items(z, halo_ref, 2 * z.half, begin, end, rest[0], tgt, rest[1], acc)
+    cuts = [jnp.minimum(here, (here + away) * share // 16 // STEP * STEP) for share in NEAR_SHARES]
+    begin, end = ((0, cuts[0]), (cuts[0], cuts[1]), (cuts[1], here))[part]
+    acc = rest[-1]
+    run_items(z, items_ref, z.leaves, begin, end, src, tgt, val, acc)
+    if part == 2:
+        run_items(z, halo_ref, 2 * z.half, 0, away, rest[0], tgt, rest[1], acc)
 
 
 def packed(blocks):
@@ -311,59 +316,56 @@
     return both[:rows] + both[rows:] + dot(high, kernel_low, 1, 1)
 
 
-def local_kernel(z, bounds_ref, slots_ref, own_ref, a_ref, b_ref, out_ref, feats, vals, rows_ref):
-    parity = bounds_ref[2] % 2
+def local_kernel(z, bounds_ref, list_ref, count_ref, own_ref, a_ref, b_ref, out_ref):
+    device = bounds_ref[2]
+    parity = device % 2
     rank = z.rank
     start, width = z.message_c[0], z.message_term - z.message_c[0]
     a, b = a_ref[:, start : start + width], b_ref[:, start : start + width]
     sides = [jnp.where(parity == 0, b, a), jnp.where(parity == 0, a, b)]
     own = own_ref[...]
-    blank_features = jnp.zeros((FEATURES, rank), bf16)
-    blank_values = jnp.zeros((2 * z.rhs, rank), bf16)
-
-    def store(at, features, values):
-        feats[0, at] = jnp.concatenate([features, blank_features], axis=1)
-        feats[1, at] = jnp.concatenate([blank_features, features], axis=1)
-        vals[0, at] = jnp.concatenate([values, blank_values], axis=1)
-        vals[1, at] = jnp.concatenate([blank_values, values], axis=1)
 
     def prepared(block):
         high, low = split2(block[: z.rhs] * GAIN)
-        return (
-            source_features(block[z.rhs :]).astype(bf16),
-            jnp.concatenate([high, low], axis=0),
-        )
-
-    side_tables = [prepared(side) for side in sides]
-    own_features, own_values = prepared(own)
-    vals[0, z.ext_nodes] = jnp.zeros((2 * z.rhs, 2 * rank), bf16)
-    vals[1, z.ext_nodes] = jnp.zeros((2 * z.rhs, 2 * rank), bf16)
+        features = source_features(block[z.rhs :]).astype(bf16)
+        return features, jnp.concatenate([high, low], axis=0)
+
+    left, right = [prepared(side) for side in sides]
+    middle = prepared(own)
+    target = target_features(own[z.rhs :])
+    slot = lax.broadcasted_iota(jnp.int32, (z.slots, z.nodes), 0)
+    sources = jnp.where(slot < count_ref[...], list_ref[...], -1).T
     for level in range(z.levels):
-        count, half, base = z.counts[level], halves(z.counts[level]), z.ext_offsets[level]
-        for i in range(half):
-            at = z.message_c[level] - start + i * rank
-            for (features, values), first in zip(side_tables, (base, base + half + count)):
-                store(first + i, features[:, at : at + rank], values[:, at : at + rank])
-        for i in range(count):
-            at = (z.offsets[level] + i) * rank
-            store(base + half + i, own_features[:, at : at + rank], own_values[:, at : at + rank])
-    target = target_features(own[z.rhs :])
-    for at in range(0, z.packed, 2 * rank):
-        turned = target[:, at : at + 2 * rank].T.astype(bf16)
-        rows_ref[at : at + 2 * rank] = turned
-    for node in range(z.nodes):
-        used = bounds_ref[3 + node]
-        points, values = [], []
-        for slot in range(0, z.slots, 2):
-            at = [slots_ref[node * z.slots + slot + k] for k in range(2)]
-            points.append(feats[0, at[0]] + feats[1, at[1]])
-            at = [jnp.where(slot + k < used, at[k], z.ext_nodes) for k in range(2)]
-            values.append(vals[0, at[0]] + vals[1, at[1]])
-        rows = rows_ref[node * rank : (node + 1) * rank]
-        high, low = split2(kernel_of(dot(rows, packed(points), 1, 0)))
-        values = packed(values)
-        both = dot(values, high, 1, 1)
-        out_ref[node] = both[: z.rhs] + both[z.rhs :] + dot(values[: z.rhs], low, 1, 1)
+        count, half, first = z.counts[level], halves(z.counts[level]), z.offsets[level]
+        at = z.message_c[level] - start
+        features, values = [
+            jnp.concatenate(
+                [
+                    left[k][:, at : at + half * rank],
+                    middle[k][:, first * rank : (first + count) * rank],
+                    right[k][:, at : at + half * rank],
+                ],
+                axis=1,
+            )
+            for k in range(2)
+        ]
+        total = z.ext_counts[level]
+        here = lax.broadcasted_iota(jnp.int32, (count, total * rank), 1) // rank + device * count - half
+        mask = jnp.zeros((count, total * rank), f32)
+        for k in range(z.slots):
+            mask = jnp.where(sources[first : first + count, k : k + 1] == here, 1.0, mask)
+        mask = mask.astype(bf16)
+        step = min(2, count)
+        for i in range(0, count, step):
+            low, high = i * rank, (i + step + 2 * half) * rank
+            rows = target[:, (first + i) * rank : (first + i + step) * rank].T.astype(bf16)
+            kernel_high, kernel_low = split2(kernel_of(dot(rows, features[:, low:high], 1, 0)))
+            for k in range(step):
+                chosen = values[:, low:high] * mask[i + k : i + k + 1, low:high]
+                part = slice(k * rank, (k + 1) * rank)
+                both = dot(chosen, kernel_high[part], 1, 1)
+                low_part = dot(chosen[: z.rhs], kernel_low[part], 1, 1)
+                out_ref[first + i + k] = both[: z.rhs] + both[z.rhs :] + low_part
 
 
 def upper_kernels(z, k, level, device, upper_ref, skel_ref):
@@ -480,31 +482,30 @@
 VMEM = pl.BlockSpec(memory_space=pltpu.VMEM)
 
 
-def on_chip(x):
-    return pltpu.with_memory_space_constraint(x, pltpu.VMEM)
-
-
-def scalars(x):
-    return pltpu.with_memory_space_constraint(x, pltpu.SMEM)
-
-
-def call(body, outs, smem, vmem, scratch=(), aliases=None, cost=1.0, in_hbm=False, out_hbm=False):
+class Vector:
+    def __init__(self, array):
+        self.shape, self.dtype = array.shape, array.dtype
+
+
+def call(body, outs, smem, vmem, scratch=(), aliases=None, cost=1.0, load=False, out_hbm=False):
     many = isinstance(outs, (list, tuple))
     listed = list(outs) if many else [outs]
-    specs = [SMEM if o.dtype == jnp.int32 else VMEM for o in listed]
+    places = [
+        pltpu.SMEM if o.dtype == jnp.int32 and not isinstance(o, Vector) else pltpu.VMEM for o in listed
+    ]
+    specs = [pl.BlockSpec(memory_space=place) for place in places]
     shapes = [
-        jax.ShapeDtypeStruct(o.shape, o.dtype)
-        if out_hbm
-        else (pltpu.SMEM if o.dtype == jnp.int32 else pltpu.VMEM)(o.shape, o.dtype)
-        for o in listed
+        jax.ShapeDtypeStruct(o.shape, o.dtype) if out_hbm else place(o.shape, o.dtype)
+        for o, place in zip(listed, places)
     ]
-    if not in_hbm:
-        smem, vmem = map(scalars, smem), map(on_chip, vmem)
-    smem, vmem = list(smem), list(vmem)
+    source = pltpu.HBM if load else pltpu.VMEM
+    if not load:
+        smem = [pltpu.with_memory_space_constraint(x, pltpu.SMEM) for x in smem]
+    vmem = [pltpu.with_memory_space_constraint(x, source) for x in vmem]
     return pl.pallas_call(
         body,
         out_shape=shapes if many else shapes[0],
-        in_specs=[SMEM] * len(smem) + [VMEM] * len(vmem),
+        in_specs=[SMEM] * len(smem) + [pl.BlockSpec(memory_space=source)] * len(vmem),
         out_specs=specs if many else specs[0],
         scratch_shapes=list(scratch),
         input_output_aliases=aliases or {},
@@ -553,9 +554,10 @@
     halfs = part(shape, dtype=bf16)
     info = lax.axis_index(AXES).astype(jnp.int32).reshape(1)
     skeleton, upper_skeleton = skeleton.transpose(1, 0, 2), upper_skeleton.transpose(1, 0, 2)
+    inter_list, inter_count, upper_list = inter_list.T, inter_count.reshape(1, -1), upper_list.T
     message = shape(z.rhs + 8, z.message)
 
-    to_partner, to_other, own, term, items, halo_items, bounds, slots, upper = call(
+    to_partner, to_other, own, term, items, halo_items, bounds, upper, *kept = call(
         part(up_kernel, z),
         [
             message,
@@ -564,15 +566,26 @@
             shape(z.rhs, z.rank),
             integers(z.leaves * (z.near + 1) + 1),
             integers(z.leaves * z.near + 1),
-            integers(3 + z.nodes),
-            integers(z.nodes * z.slots),
+            integers(3),
             integers(len(z.upper_levels) * z.slots),
+            *[shape(*a.shape, dtype=a.dtype) for a in (right_sides, points, basis, transfer)],
+            *[Vector(a) for a in (inter_list, inter_count)],
+            shape(*upper_skeleton.shape),
         ],
-        [info, near_list, near_count, inter_list.T, inter_count, upper_list.T, upper_count],
-        [right_sides, points, basis, transfer, skeleton],
+        [info],
+        [near_list, near_count, upper_list, upper_count, right_sides, points, basis, transfer, skeleton, inter_list, inter_count, upper_skeleton],
+        scratch=[
+            pltpu.VMEM(skeleton.shape, f32),
+            pltpu.SMEM(near_list.shape, jnp.int32),
+            pltpu.SMEM(near_count.shape, jnp.int32),
+            pltpu.SMEM(upper_list.shape, jnp.int32),
+            pltpu.SMEM(upper_count.shape, jnp.int32),
+            pltpu.SemaphoreType.DMA((12,)),
+        ],
         cost=2.0,
-        in_hbm=True,
-    )
+        load=True,
+    )
+    right_sides, points, basis, transfer, inter_list, inter_count, upper_skeleton = kept
     from_partner = flip(to_partner, "bulk", 1)
     sources = (2 * z.rhs, z.leaf)
     src, tgt, val, acc = call(
@@ -637,17 +650,11 @@
         cost=0.5,
     )
     acc = near(2, acc, halo_tables)
-    acc = near(3, acc, halo_tables)
     fields = call(
         part(local_kernel, z),
         shape(z.nodes, z.rhs, z.rank),
-        [bounds, slots],
-        [own, from_partner, from_other],
-        scratch=[
-            pltpu.VMEM((2, z.ext_nodes, FEATURES, 2 * z.rank), bf16),
-            pltpu.VMEM((2, z.ext_nodes + 1, 2 * z.rhs, 2 * z.rank), bf16),
-            pltpu.VMEM((z.packed, FEATURES), bf16),
-        ],
+        [bounds],
+        [inter_list, inter_count, own, from_partner, from_other],
         cost=1.5,
     )
     kernels = call(

time: 39.5 us -> 33.1 us (0.84)
  local copies, waits for them, and re-layouts: 5.27 us -> 0.03 us
  starting transfers between devices: 15.6 us -> 11.8 us
  waiting for transfers between devices: 3.09 us -> 6.62 us
  Pallas kernels: 14.8 us -> 14.3 us
    unnamed x32 -> x2, local copies, waits for them, and re-layouts: 5.26 us -> 0.01 us
    ppermute x5, starting transfers between devices: 14.9 us -> 11.2 us  [flip(): lax.ppermute(x, axis, [(i, i ^ bit) for i in range(lax.axis_size(axis))])]
    ppermute x5, waiting for transfers between devices: 3.08 us -> 6.62 us  [flip(): lax.ppermute(x, axis, [(i, i ^ bit) for i in range(lax.axis_size(axis))])]
    pallas_call x12 -> x11, Pallas kernels: 14.8 us -> 14.3 us  [call(): pl.pallas_call(body, out_shape=shapes if many else shapes[0], in_specs=[S...]
  transfers between devices with their start and end apart: 6 -> 6, of which waited for: 3 -> 3; matrix products, arithmetic and copies ran while one was open for 0% -> 0% of each run, Pallas kernels for 28% -> 31%
where the time goes in v3:
time: 33.1 us; the launch traced here: 32.9 us
  Pallas kernels  14.3 us (43%)
  starting transfers between devices  11.8 us (36%)
  waiting for transfers between devices  6.62 us (20%)
    pallas_call x11, Pallas kernels, call(): pl.pallas_call(body, out_shape=shapes if many else shapes[0], in_specs=[S...  14.3 us
    ppermute x5, starting transfers between devices, flip(): lax.ppermute(x, axis, [(i, i ^ bit) for i in range(lax.axis_size(axis))])  11.2 us
    ppermute x5, waiting for transfers between devices, flip(): lax.ppermute(x, axis, [(i, i ^ bit) for i in range(lax.axis_size(axis))])  6.62 us
    ppermute x1, starting transfers between devices, on_device(): lax.ppermute(to_other, AXES, pairs + [(b, a) for a, b in pairs])  0.67 us
  transfers between devices with their start and end apart: 6, of which 3 were waited for; matrix products, arithmetic and copies ran while one was open for 0% of the time, Pallas kernels for 31%

profile of v3, /device:TPU:0, one launch (start us, length us, event | category | flops | bytes accessed | tf_op | source)
XLA Modules:
  0.0 32.9 jit_solution(1025794085460395360)
XLA Ops:
  0.0 2.6 %shard_map.127 = (f32[40,1664]{1,0:T(8,128)S(1)}, f32[40,1664]{1,0:T(8,128)S(1)}, f32[40,1024]{1,0:T(8,128)S(1)}, f32[32,64]{1,0:T(8,128)S(1)}, s32[73]{0:T(128)...) custom-call(s32[1]{0:T(128)} %bitcast.info_ref, ...), custom_call_target="tpu_custom_call" | custom-call | flops 200000000 | bytes 6000000 | tf_op jit(solution)/shard_map/pallas_call | solution.py:505
  2.6 0.0 copy-start
  2.6 0.6 %collective-permute-start = (f32[40,1664]{1,0:T(8,128)S(1)}, f32[40,1664]{1,0:T(8,128)S(1)}, u32[]{:S(2)}, u32[]{:S(2)}) collective-permute-start(f32[40,1664]{1,0:T(8,128)S(1)} %get-tuple-element.37), channel_id=1, source_target_pairs={{0,1},{1,0},{2,3},{3,2},{4,5},{5,4},{6,7},{7,6},{8,9},{9,8},{10,11... | collective-permute-start | bytes 798728 | tf_op jit(solution)/shard_map/ppermute | solution.py:520
  3.2 0.7 %collective-permute-start.1 = (f32[40,1664]{1,0:T(8,128)S(1)}, f32[40,1664]{1,0:T(8,128)S(1)}, u32[]{:S(2)}, u32[]{:S(2)}) collective-permute-start(f32[40,1664]{1,0:T(8,128)S(1)} %get-tuple-element.38), channel_id=1, source_target_pairs={{1,2},{3,4},{5,6},{7,8},{9,10},{11,12},{13,14},{15,16},{17,18},{19... | collective-permute-start | bytes 798728 | tf_op jit(solution)/shard_map/ppermute | solution.py:611
  3.9 0.3 shard_map.130
  4.2 1.3 %shard_map.132.rest_0_ = f32[8,32,256]{2,1,0:T(8,128)S(1)} custom-call(s32[73]{0:T(128)S(4)} %get-tuple-element.43.items_ref, s32[65]{0:T(128)S(4)} %get-tuple-element.44.halo_ref, s32[3]{0:T(128)S(4)} %get-tuple-element.32.bounds_ref, bf16[8,48,256]{2,1,0:T(8,128)(2,1)S(1)} %get-tuple-element.47.tgt, ...), custom_call_target="tpu_custom_call", output_to_operand_aliasing={{}: (6, {})} | custom-call | flops 200000000 | bytes 6000000 | tf_op jit(solution)/shard_map/pallas_call | solution.py:505
  5.4 0.0 collective-permute-done.a_ref
  5.4 0.0 copy-done
  5.5 0.3 shard_map.129
  5.7 3.4 %collective-permute-start.2 = (f32[3,32,64]{2,1,0:T(8,128)S(1)}, f32[3,32,64]{2,1,0:T(8,128)S(1)}, u32[]{:S(2)}, u32[]{:S(2)}) collective-permute-start(f32[3,32,64]{2,1,0:T(8,128)S(1)} %shard_map.129), channel_id=1, source_target_pairs={{0,2},{1,3},{2,0},{3,1},{4,6},{5,7},{6,4},{7,5},{8,10},{9,11},{10,... | collective-permute-start | bytes 73736 | tf_op jit(solution)/shard_map/ppermute | solution.py:520
  9.1 0.3 shard_map.136
  9.3 1.3 %shard_map.133.rest_2_ = f32[8,32,256]{2,1,0:T(8,128)S(1)} custom-call(s32[73]{0:T(128)S(4)} %get-tuple-element.43.items_ref, s32[65]{0:T(128)S(4)} %get-tuple-element.44.halo_ref, s32[3]{0:T(128)S(4)} %get-tuple-element.32.bounds_ref, bf16[8,48,256]{2,1,0:T(8,128)(2,1)S(1)} %get-tuple-element.47.tgt, ...), custom_call_target="tpu_custom_call", output_to_operand_aliasing={{}: (6, {})} | custom-call | flops 200000000 | bytes 6000000 | tf_op jit(solution)/shard_map/pallas_call | solution.py:505
  10.6 0.0 collective-permute-done.1.b_ref
  10.6 0.3 shard_map.131
  10.9 3.6 %collective-permute-done.2 = f32[3,32,64]{2,1,0:T(8,128)S(1)} collective-permute-done((f32[3,32,64]{2,1,0:T(8,128)S(1)}, f32[3,32,64]{2,1,0:T(8,128)S(1)}, u32[]{:S(2)}, u32[]{:S(2)}) %collective-permute-start.2) | collective-permute-done | bytes 24608 | tf_op jit(solution)/shard_map/ppermute | solution.py:520
  14.6 4.4 %collective-permute-start.3 = (f32[4,32,64]{2,1,0:T(8,128)S(1)}, f32[4,32,64]{2,1,0:T(8,128)S(1)}, u32[]{:S(2)}, u32[]{:S(2)}) collective-permute-start(f32[4,32,64]{2,1,0:T(8,128)S(1)} %pad_maximum_fusion), channel_id=1, source_target_pairs={{0,4},{1,5},{2,6},{3,7},{4,0},{5,1},{6,2},{7,3},{8,12},{9,13},{10,... | collective-permute-start | bytes 98312 | tf_op jit(solution)/shard_map/ppermute | solution.py:520
  19.0 2.1 %shard_map.128.fields_ref = f32[15,32,64]{2,1,0:T(8,128)S(1)} custom-call(s32[3]{0:T(128)S(4)} %get-tuple-element.32.bounds_ref, s32[8,15]{1,0:T(8,128)S(1)} %get-tuple-element.34.list_ref, s32[1,15]{1,0:T(1,128)S(1)} %get-tuple-element.35.count_ref, f32[40,1024]{1,0:T(8,128)S(1)} %get-tuple-element.36.own_ref, f32[40,1664]{1,0:T(8,128)S(1)} %collective-permute-done.a_ref, ...), custom_call_target="tpu_custom_call" | custom-call | flops 150000000 | bytes 4500000 | tf_op jit(solution)/shard_map/pallas_call | solution.py:505
  21.1 2.7 %shard_map.134.rest_2_ = f32[8,32,256]{2,1,0:T(8,128)S(1)} custom-call(s32[73]{0:T(128)S(4)} %get-tuple-element.43.items_ref, s32[65]{0:T(128)S(4)} %get-tuple-element.44.halo_ref, s32[3]{0:T(128)S(4)} %get-tuple-element.32.bounds_ref, bf16[8,48,256]{2,1,0:T(8,128)(2,1)S(1)} %get-tuple-element.47.tgt, ...), custom_call_target="tpu_custom_call", output_to_operand_aliasing={{}: (8, {})} | custom-call | flops 200000000 | bytes 6000000 | tf_op jit(solution)/shard_map/pallas_call | solution.py:505
  23.8 0.0 collective-permute-done.3
  23.9 1.2 %collective-permute-start.4 = (f32[1,32,64]{2,1,0:T(8,128)S(1)}, f32[1,32,64]{2,1,0:T(8,128)S(1)}, u32[]{:S(2)}, u32[]{:S(2)}) collective-permute-start(f32[1,32,64]{2,1,0:T(8,128)S(1)} %get-tuple-element.59.rest_0_), channel_id=1, source_target_pairs={{0,8},{8,0},{16,24},{24,16},{1,9},{9,1},{17,25},{25,17},{2,10},{10... | collective-permute-start | bytes 24584 | tf_op jit(solution)/shard_map/ppermute | solution.py:520
  25.0 2.6 %collective-permute-done.4.rest_1_ = f32[1,32,64]{2,1,0:T(8,128)S(1)} collective-permute-done((f32[1,32,64]{2,1,0:T(8,128)S(1)}, f32[1,32,64]{2,1,0:T(8,128)S(1)}, u32[]{:S(2)}, u32[]{:S(2)}) %collective-permute-start.4) | collective-permute-done | bytes 8224 | tf_op jit(solution)/shard_map/ppermute | solution.py:520
  27.7 1.7 %collective-permute-start.5 = (f32[2,32,64]{2,1,0:T(8,128)S(1)}, f32[2,32,64]{2,1,0:T(8,128)S(1)}, u32[]{:S(2)}, u32[]{:S(2)}) collective-permute-start(f32[2,32,64]{2,1,0:T(8,128)S(1)} %pad_maximum_fusion.4), channel_id=1, source_target_pairs={{0,16},{8,24},{16,0},{24,8},{1,17},{9,25},{17,1},{25,9},{2,18},{10... | collective-permute-start | bytes 49160 | tf_op jit(solution)/shard_map/ppermute | solution.py:520
  29.4 1.9 %shard_map.135 = (f32[8,32,256]{2,1,0:T(8,128)S(1)}, bf16[2,8,64,256]{3,2,1,0:T(8,128)(2,1)S(1)}) custom-call(s32[3]{0:T(128)S(4)} %get-tuple-element.32.bounds_ref, s32[32]{0:T(128)S(4)} %get-tuple-element.33.upper_ref, f32[15,32,64]{2,1,0:T(8,128)S(1)} %shard_map.128.fields_ref, ...), custom_call_target="tpu_custom_call", output_to_operand_aliasing={{0}: (9, {})} | custom-call | flops 100000000 | bytes 3000000 | tf_op jit(solution)/shard_map/pallas_call | solution.py:505
  31.2 0.4 %collective-permute-done.5.rest_2_ = f32[2,32,64]{2,1,0:T(8,128)S(1)} collective-permute-done((f32[2,32,64]{2,1,0:T(8,128)S(1)}, f32[2,32,64]{2,1,0:T(8,128)S(1)}, u32[]{:S(2)}, u32[]{:S(2)}) %collective-permute-start.5) | collective-permute-done | bytes 16416 | tf_op jit(solution)/shard_map/ppermute | solution.py:520
  31.6 1.4 %shard_map.137 = f32[32,2048]{1,0:T(8,128)} custom-call(s32[3]{0:T(128)S(4)} %get-tuple-element.32.bounds_ref, s32[32]{0:T(128)S(4)} %get-tuple-element.33.upper_ref, f32[8,32,256]{2,1,0:T(8,128)S(1)} %get-tuple-element.53.acc, bf16[2,8,64,256]{3,2,1,0:T(8,128)(2,1)S(1)} %get-tuple-element.54.weights, f32[32,64,64]{2,1,0:T(8,128)S(1)} %copy-done, ...), custom_call_target="tpu_custom_call" | custom-call | flops 100000000 | bytes 3000000 | tf_op jit(solution)/shard_map/pallas_call | solution.py:505
  (9 shorter events, 0.1 us)
Async XLA Ops:
  2.6 2.8 %copy-start = (f32[32,64,64]{2,1,0:T(8,128)S(1)}, f32[32,64,64]{2,1,0:T(8,128)}, u32[]{:S(2)}) copy-start(f32[32,64,64]{2,1,0:T(8,128)} %matrix_ref.5) | copy-start | bytes 1572868
  2.6 2.8 %collective-permute-start = (f32[40,1664]{1,0:T(8,128)S(1)}, f32[40,1664]{1,0:T(8,128)S(1)}, u32[]{:S(2)}, u32[]{:S(2)}) collective-permute-start(f32[40,1664]{1,0:T(8,128)S(1)} %get-tuple-element.37), channel_id=1, source_target_pairs={{0,1},{1,0},{2,3},{3,2},{4,5},{5,4},{6,7},{7,6},{8,9},{9,8},{10,11... | collective-permute-start | bytes 798728 | tf_op jit(solution)/shard_map/ppermute | solution.py:520
  3.2 7.5 %collective-permute-start.1 = (f32[40,1664]{1,0:T(8,128)S(1)}, f32[40,1664]{1,0:T(8,128)S(1)}, u32[]{:S(2)}, u32[]{:S(2)}) collective-permute-start(f32[40,1664]{1,0:T(8,128)S(1)} %get-tuple-element.38), channel_id=1, source_target_pairs={{1,2},{3,4},{5,6},{7,8},{9,10},{11,12},{13,14},{15,16},{17,18},{19... | collective-permute-start | bytes 798728 | tf_op jit(solution)/shard_map/ppermute | solution.py:611
  5.7 8.8 %collective-permute-start.2 = (f32[3,32,64]{2,1,0:T(8,128)S(1)}, f32[3,32,64]{2,1,0:T(8,128)S(1)}, u32[]{:S(2)}, u32[]{:S(2)}) collective-permute-start(f32[3,32,64]{2,1,0:T(8,128)S(1)} %shard_map.129), channel_id=1, source_target_pairs={{0,2},{1,3},{2,0},{3,1},{4,6},{5,7},{6,4},{7,5},{8,10},{9,11},{10,... | collective-permute-start | bytes 73736 | tf_op jit(solution)/shard_map/ppermute | solution.py:520
  14.6 9.3 %collective-permute-start.3 = (f32[4,32,64]{2,1,0:T(8,128)S(1)}, f32[4,32,64]{2,1,0:T(8,128)S(1)}, u32[]{:S(2)}, u32[]{:S(2)}) collective-permute-start(f32[4,32,64]{2,1,0:T(8,128)S(1)} %pad_maximum_fusion), channel_id=1, source_target_pairs={{0,4},{1,5},{2,6},{3,7},{4,0},{5,1},{6,2},{7,3},{8,12},{9,13},{10,... | collective-permute-start | bytes 98312 | tf_op jit(solution)/shard_map/ppermute | solution.py:520
  23.9 3.8 %collective-permute-start.4 = (f32[1,32,64]{2,1,0:T(8,128)S(1)}, f32[1,32,64]{2,1,0:T(8,128)S(1)}, u32[]{:S(2)}, u32[]{:S(2)}) collective-permute-start(f32[1,32,64]{2,1,0:T(8,128)S(1)} %get-tuple-element.59.rest_0_), channel_id=1, source_target_pairs={{0,8},{8,0},{16,24},{24,16},{1,9},{9,1},{17,25},{25,17},{2,10},{10... | collective-permute-start | bytes 24584 | tf_op jit(solution)/shard_map/ppermute | solution.py:520
  27.7 3.9 %collective-permute-start.5 = (f32[2,32,64]{2,1,0:T(8,128)S(1)}, f32[2,32,64]{2,1,0:T(8,128)S(1)}, u32[]{:S(2)}, u32[]{:S(2)}) collective-permute-start(f32[2,32,64]{2,1,0:T(8,128)S(1)} %pad_maximum_fusion.4), channel_id=1, source_target_pairs={{0,16},{8,24},{16,0},{24,8},{1,17},{9,25},{17,1},{25,9},{2,18},{10... | collective-permute-start | bytes 49160 | tf_op jit(solution)/shard_map/ppermute | solution.py:520

commit v4 on v3

v4 whole, which is shorter than its diff:
```python
import functools
import math

import jax
import jax.numpy as jnp
from jax import lax
from jax.experimental import pallas as pl
from jax.experimental.pallas import tpu as pltpu
from jax.sharding import PartitionSpec as P


AMPLITUDE = 0.2
KERNEL_RATE = 2.0
SOFTENING = 0.01
NUGGET = 0.5
SCALE = KERNEL_RATE * math.log2(math.e)
FLOOR = SOFTENING * SCALE * SCALE
SHIFT = 1.0 / math.log(2.0)
GAIN = AMPLITUDE * math.log(2.0)
FEATURES = 48
STEP = 8
NEAR_CUTS = (8, 24, 40)
AXES = ("group", "bulk")

f32 = jnp.float32
bf16 = jnp.bfloat16


def dot(a, b, ca, cb):
    return lax.dot_general(a, b, (((ca,), (cb,)), ((), ())), preferred_element_type=f32)


def split2(x):
    high = x.astype(bf16)
    return high, (x - high.astype(f32)).astype(bf16)


def split3(x):
    a = x.astype(bf16).astype(f32)
    b = (x - a).astype(bf16).astype(f32)
    return a, b, x - a - b


def matmul(a, b, ca=1, cb=0):
    ah, al = split2(a)
    bh, bl = split2(b)
    rows = a.shape[1 - ca]
    if ca == 1:
        both = dot(jnp.concatenate([ah, al], axis=0), bh, ca, cb)
        return both[:rows] + both[rows:] + dot(ah, bl, ca, cb)
    return dot(ah, bh, ca, cb) + dot(al, bh, ca, cb) + dot(ah, bl, ca, cb)


def scaled_points(coords):
    u = coords * SCALE
    return u, jnp.broadcast_to(jnp.sum(u * u, axis=0, keepdims=True), u.shape)


def place(row, vector, first, second, third):
    rest = jnp.where(row == 5, third, 0.0)
    rest = jnp.where(row == 4, second, rest)
    rest = jnp.where(row == 3, first, rest)
    return jnp.where(row < 3, vector, rest)


def source_features(coords):
    u, length = scaled_points(coords)
    row = lax.broadcasted_iota(jnp.int32, u.shape, 0)
    a, b, c = split3(u)
    return jnp.concatenate(
        [place(row, a, *split3(length)), place(row, a, 1.0, 1.0, 1.0), b, b, a, c], axis=0
    )


def target_features(coords):
    u, length = scaled_points(coords)
    row = lax.broadcasted_iota(jnp.int32, u.shape, 0)
    a, b, c = split3(-2.0 * u)
    return jnp.concatenate(
        [place(row, a, 1.0, 1.0, 1.0), place(row, b, *split3(length + FLOOR)), a, b, c, a], axis=0
    )


def kernel_of(square):
    t = square * lax.rsqrt(square)
    return (SHIFT + t) * jnp.exp2(-t)


def halves(nodes):
    return max(nodes // 2, 1)


class Sizes:
    def __init__(self, mesh_group, mesh_bulk, leaves, rank, leaf, rhs, near, slots):
        self.group, self.bulk = mesh_group, mesh_bulk
        self.devices = mesh_group * mesh_bulk
        self.leaves, self.rank, self.leaf, self.rhs = leaves, rank, leaf, rhs
        self.near, self.slots = near, slots
        self.levels = leaves.bit_length()
        self.counts = [leaves >> level for level in range(self.levels)]
        self.offsets = [2 * leaves - 2 * count for count in self.counts]
        self.nodes = 2 * leaves - 1
        self.depth = self.devices.bit_length() - 1
        self.top = mesh_group.bit_length() - 1
        self.half = halves(leaves)
        assert 2 * self.half == leaves and leaves & (leaves - 1) == 0
        self.message_c = []
        at = self.half * leaf
        for count in self.counts:
            self.message_c.append(at)
            at += halves(count) * rank
        self.message_term = -(-at // 128) * 128
        self.packed = -(-self.nodes * rank // 128) * 128
        self.ext_counts = [count + 2 * halves(count) for count in self.counts]
        self.upper_levels = list(range(1, self.depth))

    def level_size(self, level):
        return self.bulk >> (self.depth - level) if level > self.top else 1 << level

    def level_slots(self, level):
        return min(self.slots, self.level_size(level) - 1)

    @property
    def shared(self):
        return max(2 * self.group - 4, 0)

    def matrix(self, level):
        return self.shared + level - self.top - 1

    def place(self, device, level):
        return self.matrix(level) if level > self.top else self.anchor(device, level) - 4

    def anchor(self, device, level):
        return (self.devices + device) >> (self.depth - level)


def up_kernel(
    z, near_list_in, near_count_in, upper_list_in, upper_count_in,
    rhs_in, pts_in, basis_in, transfer_in, skel_in, inter_list_in, inter_count_in, upper_skel_in, matrix_in,
    near_msg, far_msg, own_ref, term_ref, where_ref, near_list, near_count, upper_list, upper_count,
    rhs_ref, pts_ref, basis_ref, transfer_ref, inter_list_ref, inter_count_ref, upper_skel_ref, matrix_ref,
    skel_ref, sems,
):
    device = lax.axis_index(AXES[0]) * z.bulk + lax.axis_index(AXES[1])
    moves = [
        (rhs_in, rhs_ref),
        (basis_in, basis_ref),
        (transfer_in, transfer_ref),
        (skel_in, skel_ref),
        (pts_in, pts_ref),
        (near_list_in, near_list),
        (near_count_in, near_count),
        (upper_list_in, upper_list),
        (upper_count_in, upper_count),
        (inter_list_in, inter_list_ref),
        (inter_count_in, inter_count_ref),
        (upper_skel_in, upper_skel_ref),
        (matrix_in.at[4 : 2 * z.group], matrix_ref.at[0 : z.shared]),
    ]
    for level in range(z.top + 1, z.depth):
        moves.append((matrix_in.at[z.anchor(device, level)], matrix_ref.at[z.matrix(level)]))
    copies = [pltpu.make_async_copy(*move, sems.at[i]) for i, move in enumerate(moves)]
    for copy in copies:
        copy.start()
    where_ref[0] = device
    parity = device % 2
    for copy in copies[:2]:
        copy.wait()
    pair = 2 * z.rank
    rows, spare = slice(0, z.rhs), slice(z.rhs, z.rhs + 8)
    coords = slice(z.rhs, z.rhs + 3)
    pieces = []
    for leaf in range(z.leaves):
        at = leaf * z.leaf
        pieces.append(matmul(rhs_ref[:, at : at + z.leaf], basis_ref[leaf], 1, 1))
    for copy in copies[2:]:
        copy.wait()
    own_ref[spare, :] = jnp.zeros((8, z.packed), f32)
    for node in range(z.nodes):
        own_ref[coords, node * z.rank : (node + 1) * z.rank] = skel_ref[:, node, :]
    for level in range(z.levels):
        first = z.offsets[level]
        if len(pieces) == 1:
            own_ref[rows, first * z.rank : (first + 1) * z.rank] = pieces[0]
            break
        raised = []
        for i in range(len(pieces) // 2):
            both = jnp.concatenate([pieces[2 * i], pieces[2 * i + 1]], axis=1)
            node = first + 2 * i
            own_ref[rows, node * z.rank : node * z.rank + pair] = both
            raised.append(matmul(both, transfer_ref[node : node + 2].reshape(pair, z.rank)))
        pieces = raised
    term = matmul(pieces[0], transfer_ref[z.nodes - 1])
    term_ref[...] = term
    width = z.half * z.leaf
    for ref, other in ((near_msg, 0), (far_msg, 1)):
        last = (parity + 1 + other) % 2
        at = pl.multiple_of(last * ((z.leaves - z.half) * z.leaf), 128)
        ref[spare, :] = jnp.zeros((8, ref.shape[1]), f32)
        ref[rows, 0:width] = rhs_ref[:, pl.ds(at, width)]
        ref[coords, 0:width] = pts_ref[:, pl.ds(at, width)]
        for level in range(z.levels):
            size = halves(z.counts[level]) * z.rank
            first = z.offsets[level] * z.rank
            shift = (z.counts[level] - halves(z.counts[level])) * z.rank
            here = slice(z.message_c[level], z.message_c[level] + size)
            low = own_ref[:, first : first + size]
            if shift:
                low = jnp.where(last == 1, own_ref[:, first + shift : first + shift + size], low)
            ref[:, here] = low


def lists_kernel(z, where_ref, near_list, near_count, upper_list, upper_count, items_ref, halo_ref, bounds_ref, upper_ref):
    device = where_ref[0]
    for leaf in range(z.leaves):
        items_ref[leaf] = leaf * (z.leaves + 1)
    here = jnp.int32(z.leaves)
    away = jnp.int32(0)
    base = device * z.leaves
    bits = z.leaves.bit_length() - 1
    for leaf in range(z.leaves):
        count = near_count[leaf]
        for slot in range(z.near):
            source = near_list[leaf, slot] - base
            used = (slot < count).astype(jnp.int32)
            inside = jnp.where(lax.shift_right_arithmetic(source, bits) == 0, used, 0)
            items_ref[here] = source + leaf * z.leaves
            halo_ref[away] = jnp.bitwise_and(source + z.half, 2 * z.half - 1) + leaf * 2 * z.half
            here = here + inside
            away = away + used - inside
    bounds_ref[0] = here
    bounds_ref[1] = away
    bounds_ref[2] = device
    for k, level in enumerate(z.upper_levels):
        anchor = z.anchor(device, level)
        used = upper_count[anchor]
        for slot in range(z.level_slots(level)):
            upper_ref[k * z.slots + slot] = jnp.where(slot < used, upper_list[slot, anchor], -1)


def pair_kernel(z, where_ref, term_ref, a_ref, matrix_ref, out_ref):
    term = term_ref[...] + a_ref[...]
    out_ref[0] = term
    for i, level in enumerate(range(z.depth - 1, z.top, -1)):
        term = matmul(term, matrix_ref[z.matrix(level)])
        out_ref[i + 1] = term


def pad8(block):
    return jnp.concatenate([block, jnp.zeros((8 - block.shape[0], block.shape[1]), f32)], axis=0)


def fill_sources(z, src, val, first, values, coords):
    high, low = split2(values * GAIN)
    features = source_features(coords)
    for i in range(values.shape[1] // z.leaf):
        here = slice(i * z.leaf, (i + 1) * z.leaf)
        val[first + i, 0 : z.rhs] = high[:, here]
        val[first + i, z.rhs : 2 * z.rhs] = low[:, here]
        src[first + i] = features[:, here].T.astype(bf16)


def own_kernel(z, rhs_ref, pts_ref, src, tgt, val, acc):
    coords = pad8(pts_ref[...])
    fill_sources(z, src, val, 0, rhs_ref[...], coords)
    features = target_features(coords).astype(bf16)
    for i in range(z.leaves):
        here = slice(i * z.leaf, (i + 1) * z.leaf)
        tgt[i] = features[:, here]
        acc[i] = NUGGET * rhs_ref[:, here]


def halo_kernel(z, bounds_ref, a_ref, b_ref, src, val):
    width = z.half * z.leaf
    parity = bounds_ref[2] % 2
    left = jnp.where(parity == 0, b_ref[:, 0:width], a_ref[:, 0:width])
    right = jnp.where(parity == 0, a_ref[:, 0:width], b_ref[:, 0:width])
    fill_sources(z, src, val, 0, left[0 : z.rhs], left[z.rhs : z.rhs + 8])
    fill_sources(z, src, val, z.half, right[0 : z.rhs], right[z.rhs : z.rhs + 8])


def run_items(z, list_ref, per_target, first, end, src, tgt, val, acc):
    bits = per_target.bit_length() - 1

    def load(at, size):
        items = [list_ref[at + k] for k in range(size)]
        targets = [lax.shift_right_logical(item, bits) for item in items]
        return targets, [jnp.bitwise_and(item, per_target - 1) for item in items]

    def group(targets, sources):
        for target, source in zip(targets, sources):
            kernel_high, kernel_low = split2(kernel_of(dot(src[source], tgt[target], 1, 0)))
            values = val[source]
            both = dot(values, kernel_high, 1, 0)
            low = dot(values[: z.rhs], kernel_low, 1, 0)
            acc[target] += both[: z.rhs] + both[z.rhs :] + low

    count = end - first
    groups = lax.shift_right_logical(count, STEP.bit_length() - 1)

    def body(i, ready):
        later = load(first + (i + 1) * STEP, STEP)
        group(*ready)
        return later

    lax.fori_loop(0, groups, body, load(first, STEP))
    at = first + groups * STEP
    size = STEP // 2
    while size:
        rest = jnp.bitwise_and(count, size)

        @pl.when(rest != 0)
        def _(at=at, size=size):
            group(*load(at, size))

        at = at + rest
        size //= 2


def near_kernel(z, part, items_ref, halo_ref, bounds_ref, tgt, src, val, *rest):
    here, away = bounds_ref[0], bounds_ref[1]
    cuts = [0] + [jnp.minimum(here, cut) for cut in NEAR_CUTS] + [here]
    begin, end = cuts[part], cuts[part + 1]
    acc = rest[-1]
    run_items(z, items_ref, z.leaves, begin, end, src, tgt, val, acc)
    if part == len(NEAR_CUTS):
        run_items(z, halo_ref, 2 * z.half, 0, away, rest[0], tgt, rest[1], acc)


def packed(blocks):
    return blocks[0] if len(blocks) == 1 else jnp.concatenate(blocks, axis=1)


def couple(kernel_high, kernel_low, high, low):
    rows = high.shape[0]
    both = dot(jnp.concatenate([high, low], axis=0), kernel_high, 1, 1)
    return both[:rows] + both[rows:] + dot(high, kernel_low, 1, 1)


def local_kernel(z, bounds_ref, list_ref, count_ref, own_ref, a_ref, b_ref, out_ref):
    device = bounds_ref[2]
    parity = device % 2
    rank = z.rank
    start, width = z.message_c[0], z.message_term - z.message_c[0]
    a, b = a_ref[:, start : start + width], b_ref[:, start : start + width]
    sides = [jnp.where(parity == 0, b, a), jnp.where(parity == 0, a, b)]
    own = own_ref[...]

    def prepared(block):
        high, low = split2(block[: z.rhs] * GAIN)
        return source_features(block[z.rhs :]), jnp.concatenate([high, low], axis=0)

    left, right = [prepared(side) for side in sides]
    middle = prepared(own)
    target = target_features(own[z.rhs :]).astype(bf16)
    slot = lax.broadcasted_iota(jnp.int32, (z.slots, z.nodes), 0)
    sources = jnp.where(slot < count_ref[...], list_ref[...], -1)
    for level in range(z.levels):
        count, half, first = z.counts[level], halves(z.counts[level]), z.offsets[level]
        at = z.message_c[level] - start
        features, values = [
            jnp.concatenate(
                [
                    left[k][:, at : at + half * rank],
                    middle[k][:, first * rank : (first + count) * rank],
                    right[k][:, at : at + half * rank],
                ],
                axis=1,
            )
            for k in range(2)
        ]
        features = features.T.astype(bf16)
        total = z.ext_counts[level]
        named = jnp.concatenate(
            [
                jnp.broadcast_to(sources[:, first + i : first + i + 1], (z.slots, rank))
                for i in range(count)
            ],
            axis=1,
        )
        here = lax.broadcasted_iota(jnp.int32, (total, count * rank), 0) + device * count - half
        mask = jnp.zeros(here.shape, f32)
        for k in range(z.slots):
            mask = jnp.where(named[k : k + 1] == here, 1.0, mask)
        step = min(4, count)
        for i in range(0, count, step):
            nodes = slice(i, i + step + 2 * half)
            lanes = slice(i * rank, (i + step) * rank)
            rows = slice(i * rank, (i + step + 2 * half) * rank)
            there = slice((first + i) * rank, (first + i + step) * rank)
            matrix = kernel_of(dot(features[rows], target[:, there], 1, 0))
            matrix = matrix.reshape(step + 2 * half, rank, step * rank) * mask[nodes, None, lanes]
            matrix_high, matrix_low = split2(matrix.reshape(-1, step * rank))
            chosen = values[:, rows]
            both = dot(chosen, matrix_high, 1, 0)
            low = dot(chosen[: z.rhs], matrix_low, 1, 0)
            out_ref[:, there] = both[: z.rhs] + both[z.rhs :] + low


def upper_kernels(z, k, level, device, upper_ref, skel_ref):
    anchor = z.anchor(device, level)
    target = target_features(pad8(skel_ref[:, anchor, :])).T.astype(bf16)
    points = []
    for slot in range(z.level_slots(level)):
        source = upper_ref[k * z.slots + slot]
        points.append(pad8(skel_ref[:, jnp.where(source < 0, anchor, source), :]))
    return kernel_of(dot(target, source_features(packed(points)).astype(bf16), 1, 0))


def upper_sources(z, k, level, device, upper_ref, table):
    anchor = z.anchor(device, level)
    coefs = []
    for slot in range(z.level_slots(level)):
        source = upper_ref[k * z.slots + slot]
        coefs.append(table(jnp.where(source < 0, 0, source ^ anchor)) * jnp.where(source < 0, 0.0, GAIN))
    return packed(coefs)


def upper_width(z):
    return sum(z.level_slots(level) for level in z.upper_levels) * z.rank


def top_kernel(z, bounds_ref, upper_ref, skel_ref, matrix_ref, high_ref, low_ref):
    device = bounds_ref[2]
    chain = None
    for k, level in enumerate(z.upper_levels):
        if chain is not None:
            chain = matmul(matrix_ref[z.place(device, level)], chain)
        if z.level_slots(level):
            kernels = upper_kernels(z, k, level, device, upper_ref, skel_ref)
            chain = kernels if chain is None else jnp.concatenate([chain, kernels], axis=1)
    high_ref[...], low_ref[...] = split2(chain)


def mid_kernel(z, fields_ref, basis_ref, transfer_ref, acc_in, acc, weights):
    rank, rhs = z.rank, z.rhs
    row = lax.broadcasted_iota(jnp.int32, (rhs + rank, rank), 0)
    column = lax.broadcasted_iota(jnp.int32, (rhs + rank, rank), 1)
    path = jnp.where(row - rhs == column, 1.0, 0.0)
    none = jnp.zeros((rank, rank), f32)
    path = matmul(path, transfer_ref[z.nodes - 1], 1, 1)
    paths = [path + jnp.concatenate([fields_ref[:, (z.nodes - 1) * rank : z.nodes * rank], none], axis=0)]
    none = jnp.zeros((rank, 2 * rank), f32)
    for level in range(z.levels - 2, -1, -1):
        below = []
        for i, path in enumerate(paths):
            node = z.offsets[level] + 2 * i
            both = matmul(path, transfer_ref[node : node + 2].reshape(2 * rank, rank), 1, 1)
            both += jnp.concatenate([fields_ref[:, node * rank : (node + 2) * rank], none], axis=0)
            below += [both[:, :rank], both[:, rank:]]
        paths = below
    for leaf in range(z.leaves):
        values = matmul(paths[leaf], basis_ref[leaf])
        acc[leaf] += values[:rhs]
        high, low = split2(values[rhs:])
        weights[0, leaf] = high
        weights[1, leaf] = low


def final_kernel(z, bounds_ref, upper_ref, acc, weights, matrix_ref, *rest):
    rest, (out_ref, done_ref, sems) = rest[:-3], rest[-3:]
    tables, (chain_high, chain_low) = rest[:-2], rest[-2:]
    device = bounds_ref[2]
    current = [tables[-1][j] for j in range(z.group)]
    values = {z.top: current}
    for level in range(z.top, 1, -1):
        anchor = z.anchor(device, level)
        moved = [matmul(current[j], matrix_ref[(anchor ^ j) - 4]) for j in range(len(current))]
        current = [moved[2 * j] + moved[2 * j + 1] for j in range(len(current) // 2)]
        values[level - 1] = current
    coefs = []
    for k, level in enumerate(z.upper_levels):
        if z.level_slots(level):

            def table(place, level=level):
                if level >= z.top:
                    return tables[z.depth - 1 - level][place]
                chosen = jnp.zeros((z.rhs, z.rank), f32)
                for j in range(1, len(values[level])):
                    chosen = jnp.where(place == j, values[level][j], chosen)
                return chosen

            coefs.append(upper_sources(z, k, level, device, upper_ref, table))
    downward = couple(chain_high[...], chain_low[...], *split2(packed(coefs)))
    high, low = split2(downward)
    stacked = jnp.concatenate([high, low], axis=0)
    copies = []
    for leaf in range(z.leaves):
        both = dot(stacked, weights[0, leaf], 1, 0)
        value = both[: z.rhs] + both[z.rhs :] + dot(high, weights[1, leaf], 1, 0)
        done_ref[leaf] = acc[leaf] + value
        here = out_ref.at[:, leaf * z.leaf : (leaf + 1) * z.leaf]
        copies.append(pltpu.make_async_copy(done_ref.at[leaf], here, sems.at[leaf]))
        copies[-1].start()
    for copy in copies:
        copy.wait()


SMEM = pl.BlockSpec(memory_space=pltpu.SMEM)
VMEM = pl.BlockSpec(memory_space=pltpu.VMEM)


class Vector:
    def __init__(self, array):
        self.shape, self.dtype = array.shape, array.dtype


def call(body, outs, smem, vmem, scratch=(), aliases=None, cost=1.0, load=False, out_hbm=False):
    many = isinstance(outs, (list, tuple))
    listed = list(outs) if many else [outs]
    places = [
        pltpu.SMEM if o.dtype == jnp.int32 and not isinstance(o, Vector) else pltpu.VMEM for o in listed
    ]
    specs = [pl.BlockSpec(memory_space=pltpu.HBM if out_hbm else place) for place in places]
    shapes = [
        jax.ShapeDtypeStruct(o.shape, o.dtype) if out_hbm else place(o.shape, o.dtype)
        for o, place in zip(listed, places)
    ]
    source = pltpu.HBM if load else pltpu.VMEM
    if not load:
        smem = [pltpu.with_memory_space_constraint(x, pltpu.SMEM) for x in smem]
    vmem = [pltpu.with_memory_space_constraint(x, source) for x in vmem]
    return pl.pallas_call(
        body,
        out_shape=shapes if many else shapes[0],
        in_specs=[SMEM] * len(smem) + [pl.BlockSpec(memory_space=source)] * len(vmem),
        out_specs=specs if many else specs[0],
        scratch_shapes=list(scratch),
        input_output_aliases=aliases or {},
        compiler_params=pltpu.CompilerParams(vmem_limit_bytes=16 << 20),
        cost_estimate=pl.CostEstimate(
            flops=int(cost * 1e8), bytes_accessed=int(cost * 3e6), transcendentals=0
        ),
    )(*smem, *vmem)


def flip(x, axis, bit):
    return lax.ppermute(x, axis, [(i, i ^ bit) for i in range(lax.axis_size(axis))])


def shape(*dims, dtype=f32):
    return jax.ShapeDtypeStruct(dims, dtype)


def on_device(
    right_sides,
    points,
    basis,
    transfer,
    skeleton,
    near_list,
    near_count,
    inter_list,
    inter_count,
    upper_transfer,
    upper_skeleton,
    upper_list,
    upper_count,
):
    z = Sizes(
        lax.axis_size("group"),
        lax.axis_size("bulk"),
        basis.shape[0],
        basis.shape[1],
        basis.shape[2],
        right_sides.shape[0],
        near_list.shape[1],
        inter_list.shape[1],
    )
    part = functools.partial
    integers = part(shape, dtype=jnp.int32)
    halfs = part(shape, dtype=bf16)
    skeleton, upper_skeleton = skeleton.transpose(1, 0, 2), upper_skeleton.transpose(1, 0, 2)
    inter_list, inter_count, upper_list = inter_list.T, inter_count.reshape(1, -1), upper_list.T

    to_partner, to_other, own, term, where, *kept = call(
        part(up_kernel, z),
        [
            shape(z.rhs + 8, z.message_term),
            shape(z.rhs + 8, z.message_term),
            shape(z.rhs + 8, z.packed),
            shape(z.rhs, z.rank),
            integers(1),
            *[integers(*a.shape) for a in (near_list, near_count, upper_list, upper_count)],
            *[shape(*a.shape, dtype=a.dtype) for a in (right_sides, points, basis, transfer)],
            *[Vector(a) for a in (inter_list, inter_count)],
            shape(*upper_skeleton.shape),
            shape(z.shared + z.depth - 1 - z.top, z.rank, z.rank),
        ],
        [],
        [near_list, near_count, upper_list, upper_count, right_sides, points, basis, transfer, skeleton, inter_list, inter_count, upper_skeleton, upper_transfer],
        scratch=[
            pltpu.VMEM(skeleton.shape, f32),
            pltpu.SemaphoreType.DMA((13 + z.depth,)),
        ],
        cost=2.0,
        load=True,
    )
    lists, kept = kept[:4], kept[4:]
    right_sides, points, basis, transfer, inter_list, inter_count, upper_skeleton, matrices = kept
    their_term = flip(term, "bulk", 1)
    from_partner = flip(to_partner, "bulk", 1)
    sources = (2 * z.rhs, z.leaf)
    src, tgt, val, acc = call(
        part(own_kernel, z),
        [
            halfs(z.leaves, z.leaf, FEATURES),
            halfs(z.leaves, FEATURES, z.leaf),
            halfs(z.leaves, *sources),
            shape(z.leaves, z.rhs, z.leaf),
        ],
        [],
        [right_sides, points],
        cost=0.7,
    )
    items, halo_items, bounds, upper = call(
        part(lists_kernel, z),
        [
            integers(z.leaves * (z.near + 1) + 2 * STEP),
            integers(z.leaves * z.near + 2 * STEP),
            integers(3),
            integers(len(z.upper_levels) * z.slots),
        ],
        [where, *lists],
        [],
        cost=0.7,
    )
    terms = call(
        part(pair_kernel, z),
        shape(z.depth - z.top, z.rhs, z.rank),
        [where],
        [term, their_term, matrices],
        cost=0.3,
    )
    pairs = [(i, i + 1) for i in range(1, z.devices - 1, 2)]
    from_other = lax.ppermute(to_other, AXES, pairs + [(b, a) for a, b in pairs])

    whole_levels, partial = [], terms
    for bit in range(1, z.bulk.bit_length() - 1):
        whole_levels.append([partial[:1]])
        partial = partial[1:]
        sizes = [sum(p.shape[0] for p in level) for level in whole_levels]
        sent = jnp.concatenate([p for level in whole_levels for p in level] + [partial], axis=0)
        received = flip(sent, "bulk", 1 << bit)
        at = 0
        for level, size in zip(whole_levels, sizes):
            level.append(received[at : at + size])
            at += size
        partial = partial + received[at:]
    for bit in range(z.top):
        partial = jnp.concatenate([partial, flip(partial, "group", 1 << bit)], axis=0)
    tables = [jnp.concatenate(level, axis=0) for level in whole_levels] + [partial]

    def near(index, acc, more=()):
        arrays = [tgt, src, val, *more, acc]
        return call(
            part(near_kernel, z, index),
            shape(z.leaves, z.rhs, z.leaf),
            [items, halo_items, bounds],
            arrays,
            aliases={2 + len(arrays): 0},
            cost=2.0,
        )

    for index in range(len(NEAR_CUTS)):
        acc = near(index, acc)
    halo_tables = call(
        part(halo_kernel, z),
        [halfs(2 * z.half, z.leaf, FEATURES), halfs(2 * z.half, *sources)],
        [bounds],
        [from_partner, from_other],
        cost=0.5,
    )
    acc = near(len(NEAR_CUTS), acc, halo_tables)
    fields = call(
        part(local_kernel, z),
        shape(z.rhs, z.packed),
        [bounds],
        [inter_list, inter_count, own, from_partner, from_other],
        cost=1.5,
    )
    chain = call(
        part(top_kernel, z),
        [halfs(z.rank, upper_width(z))] * 2,
        [bounds, upper],
        [upper_skeleton, matrices],
        cost=0.6,
    )
    acc, weights = call(
        part(mid_kernel, z),
        [shape(z.leaves, z.rhs, z.leaf), halfs(2, z.leaves, z.rank, z.leaf)],
        [],
        [fields, basis, transfer, acc],
        aliases={3: 0},
        cost=1.0,
    )
    return call(
        part(final_kernel, z),
        shape(*right_sides.shape),
        [bounds, upper],
        [acc, weights, matrices, *tables, *chain],
        scratch=[
            pltpu.VMEM((z.leaves, z.rhs, z.leaf), f32),
            pltpu.SemaphoreType.DMA((z.leaves,)),
        ],
        cost=1.0,
        out_hbm=True,
    )


def solution(mesh):
    in_specs = (
        P(None, AXES),
        P(None, AXES),
        P(AXES, None, None),
        P(AXES, None, None),
        P(AXES, None, None),
        P(AXES, None),
        P(AXES),
        P(AXES, None),
        P(AXES),
        P(),
        P(),
        P(),
        P(),
    )
    return jax.shard_map(
        on_device, mesh=mesh, in_specs=in_specs, out_specs=P(None, AXES), check_vma=False
    )
```

time: 33.1 us -> 35.1 us (1.060)
  starting transfers between devices: 11.8 us -> 16.4 us
  Pallas kernels: 14.3 us -> 13 us
  waiting for transfers between devices: 6.62 us -> 5.32 us
    ppermute x5 -> x6, starting transfers between devices: 11.2 us -> 15.7 us  [flip(): lax.ppermute(x, axis, [(i, i ^ bit) for i in range(lax.axis_size(axis))])]
    ppermute x5 -> x6, waiting for transfers between devices: 6.62 us -> 5.32 us  [flip(): lax.ppermute(x, axis, [(i, i ^ bit) for i in range(lax.axis_size(axis))])]
    pallas_call x11 -> x13, Pallas kernels: 14.3 us -> 13 us  [call(): pl.pallas_call(body, out_shape=shapes if many else shapes[0], in_specs=[S...]
  transfers between devices with their start and end apart: 6 -> 7, of which waited for: 3 -> 4; matrix products, arithmetic and copies ran while one was open for 0% -> 0% of each run, Pallas kernels for 31% -> 16%
where the time goes in v4:
time: 35.1 us; the launch traced here: 34.9 us
  starting transfers between devices  16.4 us (47%)
  Pallas kernels  13 us (37%)
  waiting for transfers between devices  5.32 us (15%)
    ppermute x6, starting transfers between devices, flip(): lax.ppermute(x, axis, [(i, i ^ bit) for i in range(lax.axis_size(axis))])  15.7 us
    pallas_call x13, Pallas kernels, call(): pl.pallas_call(body, out_shape=shapes if many else shapes[0], in_specs=[S...  13 us
    ppermute x6, waiting for transfers between devices, flip(): lax.ppermute(x, axis, [(i, i ^ bit) for i in range(lax.axis_size(axis))])  5.32 us
  transfers between devices with their start and end apart: 7, of which 4 were waited for; matrix products, arithmetic and copies ran while one was open for 0% of the time, Pallas kernels for 16%

profile of v4, /device:TPU:0, one launch (start us, length us, event | category | flops | bytes accessed | tf_op | source)
XLA Modules:
  0.0 34.9 jit_solution(13228055343598145094)
XLA Ops:
  0.0 2.4 %shard_map.127 = (f32[40,1536]{1,0:T(8,128)S(1)}, f32[40,1536]{1,0:T(8,128)S(1)}, f32[40,1024]{1,0:T(8,128)S(1)}, f32[32,64]{1,0:T(8,128)S(1)}, s32[1]{0:T(128)S...) custom-call(s32[8,8]{1,0:T(8,128)} %near_list_in.1, ...), custom_call_target="tpu_custom_call" | custom-call | flops 200000000 | bytes 6000000 | tf_op jit(solution)/shard_map/pallas_call | solution.py:523
  2.4 0.6 %collective-permute-start = (f32[40,1536]{1,0:T(8,128)S(1)}, f32[40,1536]{1,0:T(8,128)S(1)}, u32[]{:S(2)}, u32[]{:S(2)}) collective-permute-start(f32[40,1536]{1,0:T(8,128)S(1)} %get-tuple-element.46), channel_id=1, source_target_pairs={{0,1},{1,0},{2,3},{3,2},{4,5},{5,4},{6,7},{7,6},{8,9},{9,8},{10,11... | collective-permute-start | bytes 737288 | tf_op jit(solution)/shard_map/ppermute | solution.py:538
  3.0 0.7 %collective-permute-start.1 = (f32[40,1536]{1,0:T(8,128)S(1)}, f32[40,1536]{1,0:T(8,128)S(1)}, u32[]{:S(2)}, u32[]{:S(2)}) collective-permute-start(f32[40,1536]{1,0:T(8,128)S(1)} %get-tuple-element.47), channel_id=1, source_target_pairs={{1,2},{3,4},{5,6},{7,8},{9,10},{11,12},{13,14},{15,16},{17,18},{19... | collective-permute-start | bytes 737288 | tf_op jit(solution)/shard_map/ppermute | solution.py:636
  3.6 4.0 %collective-permute-start.2 = (f32[32,64]{1,0:T(8,128)S(1)}, f32[32,64]{1,0:T(8,128)S(1)}, u32[]{:S(2)}, u32[]{:S(2)}) collective-permute-start(f32[32,64]{1,0:T(8,128)S(1)} %get-tuple-element.63.term_ref), channel_id=1, source_target_pairs={{0,1},{1,0},{2,3},{3,2},{4,5},{5,4},{6,7},{7,6},{8,9},{9,8},{10,11... | collective-permute-start | bytes 24584 | tf_op jit(solution)/shard_map/ppermute | solution.py:538
  7.6 0.3 shard_map.130
  8.0 0.4 %shard_map.128 = (s32[88]{0:T(128)S(4)}, s32[80]{0:T(128)S(4)}, s32[3]{0:T(128)S(4)}, s32[32]{0:T(128)S(4)}) custom-call(s32[1]{0:T(128)S(4)} %get-tuple-element.36.where_ref, s32[8,8]{1,0:T(8,128)S(4)} %get-tuple-element.37.near_list, s32[8]{0:T(128)S(4)} %get-tuple-element.38.near_count, s32[8,32]{1,0:T(8,128)S(4)} %get-tuple-element.39.upper_list, ...), custom_call_target="tpu_custom_call" | custom-call | flops 70000000 | bytes 2100000 | tf_op jit(solution)/shard_map/pallas_call | solution.py:523
  8.4 0.1 collective-permute-done.2.a_ref
  8.5 0.3 shard_map.137
  8.7 1.6 %collective-permute-start.3 = (f32[3,32,64]{2,1,0:T(8,128)S(1)}, f32[3,32,64]{2,1,0:T(8,128)S(1)}, u32[]{:S(2)}, u32[]{:S(2)}) collective-permute-start(f32[3,32,64]{2,1,0:T(8,128)S(1)} %shard_map.137), channel_id=1, source_target_pairs={{0,2},{1,3},{2,0},{3,1},{4,6},{5,7},{6,4},{7,5},{8,10},{9,11},{10,... | collective-permute-start | bytes 73736 | tf_op jit(solution)/shard_map/ppermute | solution.py:538
  10.3 0.9 %shard_map.138 = (bf16[64,512]{1,0:T(8,128)(2,1)S(1)}, bf16[64,512]{1,0:T(8,128)(2,1)S(1)}) custom-call(s32[3]{0:T(128)S(4)} %get-tuple-element.41.bounds_ref, s32[32]{0:T(128)S(4)} %get-tuple-element.42.upper_ref, f32[3,32,64]{2,1,0:T(8,128)S(1)} %get-tuple-element.64.skel_ref, f32[6,64,64]{2,1,0:T(8,128)S(1)} %get-tuple-element.62.matrix_ref), custom_call_target="tpu_custom_call" | custom-call | flops 60000000 | bytes 1800000 | tf_op jit(solution)/shard_map/pallas_call | solution.py:523
  11.2 1.0 %shard_map.132.rest_0_ = f32[8,32,256]{2,1,0:T(8,128)S(1)} custom-call(s32[88]{0:T(128)S(4)} %get-tuple-element.50.items_ref, s32[80]{0:T(128)S(4)} %get-tuple-element.51.halo_ref, s32[3]{0:T(128)S(4)} %get-tuple-element.41.bounds_ref, bf16[8,48,256]{2,1,0:T(8,128)(2,1)S(1)} %get-tuple-element.54.tgt, ...), custom_call_target="tpu_custom_call", output_to_operand_aliasing={{}: (6, {})} | custom-call | flops 200000000 | bytes 6000000 | tf_op jit(solution)/shard_map/pallas_call | solution.py:523
  12.2 1.6 %collective-permute-done.3 = f32[3,32,64]{2,1,0:T(8,128)S(1)} collective-permute-done((f32[3,32,64]{2,1,0:T(8,128)S(1)}, f32[3,32,64]{2,1,0:T(8,128)S(1)}, u32[]{:S(2)}, u32[]{:S(2)}) %collective-permute-start.3) | collective-permute-done | bytes 24608 | tf_op jit(solution)/shard_map/ppermute | solution.py:538
  13.8 4.7 %collective-permute-start.4 = (f32[4,32,64]{2,1,0:T(8,128)S(1)}, f32[4,32,64]{2,1,0:T(8,128)S(1)}, u32[]{:S(2)}, u32[]{:S(2)}) collective-permute-start(f32[4,32,64]{2,1,0:T(8,128)S(1)} %pad_maximum_fusion), channel_id=1, source_target_pairs={{0,4},{1,5},{2,6},{3,7},{4,0},{5,1},{6,2},{7,3},{8,12},{9,13},{10,... | collective-permute-start | bytes 98312 | tf_op jit(solution)/shard_map/ppermute | solution.py:538
  18.5 1.9 %shard_map.133.rest_0_ = f32[8,32,256]{2,1,0:T(8,128)S(1)} custom-call(s32[88]{0:T(128)S(4)} %get-tuple-element.50.items_ref, s32[80]{0:T(128)S(4)} %get-tuple-element.51.halo_ref, s32[3]{0:T(128)S(4)} %get-tuple-element.41.bounds_ref, bf16[8,48,256]{2,1,0:T(8,128)(2,1)S(1)} %get-tuple-element.54.tgt, ...), custom_call_target="tpu_custom_call", output_to_operand_aliasing={{}: (6, {})} | custom-call | flops 200000000 | bytes 6000000 | tf_op jit(solution)/shard_map/pallas_call | solution.py:523
  20.4 1.0 %shard_map.134.rest_2_ = f32[8,32,256]{2,1,0:T(8,128)S(1)} custom-call(s32[88]{0:T(128)S(4)} %get-tuple-element.50.items_ref, s32[80]{0:T(128)S(4)} %get-tuple-element.51.halo_ref, s32[3]{0:T(128)S(4)} %get-tuple-element.41.bounds_ref, bf16[8,48,256]{2,1,0:T(8,128)(2,1)S(1)} %get-tuple-element.54.tgt, ...), custom_call_target="tpu_custom_call", output_to_operand_aliasing={{}: (6, {})} | custom-call | flops 200000000 | bytes 6000000 | tf_op jit(solution)/shard_map/pallas_call | solution.py:523
  21.4 0.0 collective-permute-done.4
  21.4 2.3 %collective-permute-start.5 = (f32[1,32,64]{2,1,0:T(8,128)S(1)}, f32[1,32,64]{2,1,0:T(8,128)S(1)}, u32[]{:S(2)}, u32[]{:S(2)}) collective-permute-start(f32[1,32,64]{2,1,0:T(8,128)S(1)} %get-tuple-element.67), channel_id=1, source_target_pairs={{0,8},{8,0},{16,24},{24,16},{1,9},{9,1},{17,25},{25,17},{2,10},{10... | collective-permute-start | bytes 24584 | tf_op jit(solution)/shard_map/ppermute | solution.py:538
  23.8 1.7 %collective-permute-done.5 = f32[1,32,64]{2,1,0:T(8,128)S(1)} collective-permute-done((f32[1,32,64]{2,1,0:T(8,128)S(1)}, f32[1,32,64]{2,1,0:T(8,128)S(1)}, u32[]{:S(2)}, u32[]{:S(2)}) %collective-permute-start.5) | collective-permute-done | bytes 8224 | tf_op jit(solution)/shard_map/ppermute | solution.py:538
  25.5 2.6 %collective-permute-start.6 = (f32[2,32,64]{2,1,0:T(8,128)S(1)}, f32[2,32,64]{2,1,0:T(8,128)S(1)}, u32[]{:S(2)}, u32[]{:S(2)}) collective-permute-start(f32[2,32,64]{2,1,0:T(8,128)S(1)} %pad_maximum_fusion.5), channel_id=1, source_target_pairs={{0,16},{8,24},{16,0},{24,8},{1,17},{9,25},{17,1},{25,9},{2,18},{10... | collective-permute-start | bytes 49160 | tf_op jit(solution)/shard_map/ppermute | solution.py:538
  28.1 1.9 %collective-permute-done.6 = f32[2,32,64]{2,1,0:T(8,128)S(1)} collective-permute-done((f32[2,32,64]{2,1,0:T(8,128)S(1)}, f32[2,32,64]{2,1,0:T(8,128)S(1)}, u32[]{:S(2)}, u32[]{:S(2)}) %collective-permute-start.6) | collective-permute-done | bytes 16416 | tf_op jit(solution)/shard_map/ppermute | solution.py:538
  30.0 0.0 collective-permute-done.a_ref
  30.0 0.0 collective-permute-done.1.b_ref
  30.0 0.3 shard_map.131
  30.3 0.5 %shard_map.135.acc_in = f32[8,32,256]{2,1,0:T(8,128)S(1)} custom-call(s32[88]{0:T(128)S(4)} %get-tuple-element.50.items_ref, s32[80]{0:T(128)S(4)} %get-tuple-element.51.halo_ref, s32[3]{0:T(128)S(4)} %get-tuple-element.41.bounds_ref, bf16[8,48,256]{2,1,0:T(8,128)(2,1)S(1)} %get-tuple-element.54.tgt, ...), custom_call_target="tpu_custom_call", output_to_operand_aliasing={{}: (8, {})} | custom-call | flops 200000000 | bytes 6000000 | tf_op jit(solution)/shard_map/pallas_call | solution.py:523
  30.8 1.7 %shard_map.129.fields_ref = f32[32,1024]{1,0:T(8,128)S(1)} custom-call(s32[3]{0:T(128)S(4)} %get-tuple-element.41.bounds_ref, s32[8,15]{1,0:T(8,128)S(1)} %get-tuple-element.43.list_ref, s32[1,15]{1,0:T(1,128)S(1)} %get-tuple-element.44.count_ref, f32[40,1024]{1,0:T(8,128)S(1)} %get-tuple-element.45.own_ref, f32[40,1536]{1,0:T(8,128)S(1)} %collective-permute-done.a_ref, ...), custom_call_target="tpu_custom_call" | custom-call | flops 150000000 | bytes 4500000 | tf_op jit(solution)/shard_map/pallas_call | solution.py:523
  32.5 1.1 %shard_map.136 = (f32[8,32,256]{2,1,0:T(8,128)S(1)}, bf16[2,8,64,256]{3,2,1,0:T(8,128)(2,1)S(1)}) custom-call(f32[32,1024]{1,0:T(8,128)S(1)} %shard_map.129.fields_ref, f32[8,64,256]{2,1,0:T(8,128)S(1)} %get-tuple-element.48.basis_ref, f32[15,64,64]{2,1,0:T(8,128)S(1)} %get-tuple-element.49.transfer_ref, ...), custom_call_target="tpu_custom_call", output_to_operand_aliasing={{0}: (3, {})} | custom-call | flops 100000000 | bytes 3000000 | tf_op jit(solution)/shard_map/pallas_call | solution.py:523
  33.6 1.3 %shard_map.139 = f32[32,2048]{1,0:T(8,128)} custom-call(s32[3]{0:T(128)S(4)} %get-tuple-element.41.bounds_ref, s32[32]{0:T(128)S(4)} %get-tuple-element.42.upper_ref, f32[8,32,256]{2,1,0:T(8,128)S(1)} %get-tuple-element.60.acc, bf16[2,8,64,256]{3,2,1,0:T(8,128)(2,1)S(1)} %get-tuple-element.61.weights, f32[6,64,64]{2,1,0:T(8,128)S(1)} %get-tuple-element.62.matrix_ref, ...), custom_call_target="tpu_custom_call" | custom-call | flops 100000000 | bytes 3000000 | tf_op jit(solution)/shard_map/pallas_call | solution.py:523
  (10 shorter events, 0.1 us)
Async XLA Ops:
  2.4 27.6 %collective-permute-start = (f32[40,1536]{1,0:T(8,128)S(1)}, f32[40,1536]{1,0:T(8,128)S(1)}, u32[]{:S(2)}, u32[]{:S(2)}) collective-permute-start(f32[40,1536]{1,0:T(8,128)S(1)} %get-tuple-element.46), channel_id=1, source_target_pairs={{0,1},{1,0},{2,3},{3,2},{4,5},{5,4},{6,7},{7,6},{8,9},{9,8},{10,11... | collective-permute-start | bytes 737288 | tf_op jit(solution)/shard_map/ppermute | solution.py:538
  3.0 27.0 %collective-permute-start.1 = (f32[40,1536]{1,0:T(8,128)S(1)}, f32[40,1536]{1,0:T(8,128)S(1)}, u32[]{:S(2)}, u32[]{:S(2)}) collective-permute-start(f32[40,1536]{1,0:T(8,128)S(1)} %get-tuple-element.47), channel_id=1, source_target_pairs={{1,2},{3,4},{5,6},{7,8},{9,10},{11,12},{13,14},{15,16},{17,18},{19... | collective-permute-start | bytes 737288 | tf_op jit(solution)/shard_map/ppermute | solution.py:636
  3.6 4.8 %collective-permute-start.2 = (f32[32,64]{1,0:T(8,128)S(1)}, f32[32,64]{1,0:T(8,128)S(1)}, u32[]{:S(2)}, u32[]{:S(2)}) collective-permute-start(f32[32,64]{1,0:T(8,128)S(1)} %get-tuple-element.63.term_ref), channel_id=1, source_target_pairs={{0,1},{1,0},{2,3},{3,2},{4,5},{5,4},{6,7},{7,6},{8,9},{9,8},{10,11... | collective-permute-start | bytes 24584 | tf_op jit(solution)/shard_map/ppermute | solution.py:538
  8.7 5.1 %collective-permute-start.3 = (f32[3,32,64]{2,1,0:T(8,128)S(1)}, f32[3,32,64]{2,1,0:T(8,128)S(1)}, u32[]{:S(2)}, u32[]{:S(2)}) collective-permute-start(f32[3,32,64]{2,1,0:T(8,128)S(1)} %shard_map.137), channel_id=1, source_target_pairs={{0,2},{1,3},{2,0},{3,1},{4,6},{5,7},{6,4},{7,5},{8,10},{9,11},{10,... | collective-permute-start | bytes 73736 | tf_op jit(solution)/shard_map/ppermute | solution.py:538
  13.8 7.6 %collective-permute-start.4 = (f32[4,32,64]{2,1,0:T(8,128)S(1)}, f32[4,32,64]{2,1,0:T(8,128)S(1)}, u32[]{:S(2)}, u32[]{:S(2)}) collective-permute-start(f32[4,32,64]{2,1,0:T(8,128)S(1)} %pad_maximum_fusion), channel_id=1, source_target_pairs={{0,4},{1,5},{2,6},{3,7},{4,0},{5,1},{6,2},{7,3},{8,12},{9,13},{10,... | collective-permute-start | bytes 98312 | tf_op jit(solution)/shard_map/ppermute | solution.py:538
  21.4 4.0 %collective-permute-start.5 = (f32[1,32,64]{2,1,0:T(8,128)S(1)}, f32[1,32,64]{2,1,0:T(8,128)S(1)}, u32[]{:S(2)}, u32[]{:S(2)}) collective-permute-start(f32[1,32,64]{2,1,0:T(8,128)S(1)} %get-tuple-element.67), channel_id=1, source_target_pairs={{0,8},{8,0},{16,24},{24,16},{1,9},{9,1},{17,25},{25,17},{2,10},{10... | collective-permute-start | bytes 24584 | tf_op jit(solution)/shard_map/ppermute | solution.py:538
  25.5 4.5 %collective-permute-start.6 = (f32[2,32,64]{2,1,0:T(8,128)S(1)}, f32[2,32,64]{2,1,0:T(8,128)S(1)}, u32[]{:S(2)}, u32[]{:S(2)}) collective-permute-start(f32[2,32,64]{2,1,0:T(8,128)S(1)} %pad_maximum_fusion.5), channel_id=1, source_target_pairs={{0,16},{8,24},{16,0},{24,8},{1,17},{9,25},{17,1},{25,9},{2,18},{10... | collective-permute-start | bytes 49160 | tf_op jit(solution)/shard_map/ppermute | solution.py:538

commit v5 on v4

--- a/solution.py
+++ b/solution.py
@@ -111,7 +111,6 @@
             at += halves(count) * rank
         self.message_term = -(-at // 128) * 128
         self.packed = -(-self.nodes * rank // 128) * 128
-        self.ext_counts = [count + 2 * halves(count) for count in self.counts]
         self.upper_levels = list(range(1, self.depth))
 
     def level_size(self, level):
@@ -337,64 +336,70 @@
     return both[:rows] + both[rows:] + dot(high, kernel_low, 1, 1)
 
 
-def local_kernel(z, bounds_ref, list_ref, count_ref, own_ref, a_ref, b_ref, out_ref):
-    device = bounds_ref[2]
+def prepared(z, block):
+    high, low = split2(block[: z.rhs] * GAIN)
+    features = source_features(block[z.rhs :]).T.astype(bf16)
+    return features, jnp.concatenate([high, low], axis=0)
+
+
+def coupled(z, features, values, target, named, first):
+    nodes, lanes = features.shape[0] // z.rank, target.shape[1]
+    here = lax.broadcasted_iota(jnp.int32, (nodes, lanes), 0) + first
+    mask = jnp.zeros((nodes, lanes), f32)
+    for slot in range(z.slots):
+        mask = jnp.where(named[slot : slot + 1] == here, 1.0, mask)
+    matrix = kernel_of(dot(features, target, 1, 0))
+    matrix = matrix.reshape(nodes, z.rank, lanes) * mask[:, None]
+    high, low = split2(matrix.reshape(nodes * z.rank, lanes))
+    both = dot(values, high, 1, 0)
+    return both[: z.rhs] + both[z.rhs :] + dot(values[: z.rhs], low, 1, 0)
+
+
+def inner_kernel(z, where_ref, list_ref, count_ref, own_ref, out_ref, target_ref, named_ref):
+    device = where_ref[0]
+    rank = z.rank
+    features, values = prepared(z, own_ref[...])
+    target_ref[...] = target_features(own_ref[z.rhs :]).astype(bf16)
+    slot = lax.broadcasted_iota(jnp.int32, (z.slots, z.nodes), 0)
+    sources = jnp.where(slot < count_ref[...], list_ref[...], -1)
+    for node in range(z.nodes):
+        here = slice(node * rank, (node + 1) * rank)
+        named_ref[:, here] = jnp.broadcast_to(sources[:, node : node + 1], (z.slots, rank))
+    for level in range(z.levels):
+        count, half, first = z.counts[level], halves(z.counts[level]), z.offsets[level]
+        step = min(4, count)
+        for i in range(0, count, step):
+            low, high = max(0, i - half), min(count, i + step + half)
+            rows = slice((first + low) * rank, (first + high) * rank)
+            there = slice((first + i) * rank, (first + i + step) * rank)
+            if count == 1:
+                out_ref[:, there] = jnp.zeros((z.rhs, rank), f32)
+                continue
+            out_ref[:, there] = coupled(
+                z, features[rows], values[:, rows], target_ref[:, there], named_ref[:, there], device * count + low
+            )
+
+
+def outer_kernel(z, where_ref, a_ref, b_ref, target_ref, named_ref, fields_in, out_ref):
+    device = where_ref[0]
     parity = device % 2
     rank = z.rank
     start, width = z.message_c[0], z.message_term - z.message_c[0]
     a, b = a_ref[:, start : start + width], b_ref[:, start : start + width]
-    sides = [jnp.where(parity == 0, b, a), jnp.where(parity == 0, a, b)]
-    own = own_ref[...]
-
-    def prepared(block):
-        high, low = split2(block[: z.rhs] * GAIN)
-        return source_features(block[z.rhs :]), jnp.concatenate([high, low], axis=0)
-
-    left, right = [prepared(side) for side in sides]
-    middle = prepared(own)
-    target = target_features(own[z.rhs :]).astype(bf16)
-    slot = lax.broadcasted_iota(jnp.int32, (z.slots, z.nodes), 0)
-    sources = jnp.where(slot < count_ref[...], list_ref[...], -1)
+    left = prepared(z, jnp.where(parity == 0, b, a))
+    right = prepared(z, jnp.where(parity == 0, a, b))
     for level in range(z.levels):
         count, half, first = z.counts[level], halves(z.counts[level]), z.offsets[level]
         at = z.message_c[level] - start
-        features, values = [
-            jnp.concatenate(
-                [
-                    left[k][:, at : at + half * rank],
-                    middle[k][:, first * rank : (first + count) * rank],
-                    right[k][:, at : at + half * rank],
-                ],
-                axis=1,
+        rows = slice(at, at + half * rank)
+        for (features, values), low, source in (
+            (left, 0, device * count - half),
+            (right, count - half, (device + 1) * count),
+        ):
+            there = slice((first + low) * rank, (first + low + half) * rank)
+            out_ref[:, there] += coupled(
+                z, features[rows], values[:, rows], target_ref[:, there], named_ref[:, there], source
             )
-            for k in range(2)
-        ]
-        features = features.T.astype(bf16)
-        total = z.ext_counts[level]
-        named = jnp.concatenate(
-            [
-                jnp.broadcast_to(sources[:, first + i : first + i + 1], (z.slots, rank))
-                for i in range(count)
-            ],
-            axis=1,
-        )
-        here = lax.broadcasted_iota(jnp.int32, (total, count * rank), 0) + device * count - half
-        mask = jnp.zeros(here.shape, f32)
-        for k in range(z.slots):
-            mask = jnp.where(named[k : k + 1] == here, 1.0, mask)
-        step = min(4, count)
-        for i in range(0, count, step):
-            nodes = slice(i, i + step + 2 * half)
-            lanes = slice(i * rank, (i + step) * rank)
-            rows = slice(i * rank, (i + step + 2 * half) * rank)
-            there = slice((first + i) * rank, (first + i + step) * rank)
-            matrix = kernel_of(dot(features[rows], target[:, there], 1, 0))
-            matrix = matrix.reshape(step + 2 * half, rank, step * rank) * mask[nodes, None, lanes]
-            matrix_high, matrix_low = split2(matrix.reshape(-1, step * rank))
-            chosen = values[:, rows]
-            both = dot(chosen, matrix_high, 1, 0)
-            low = dot(chosen[: z.rhs], matrix_low, 1, 0)
-            out_ref[:, there] = both[: z.rhs] + both[z.rhs :] + low
 
 
 def upper_kernels(z, k, level, device, upper_ref, skel_ref):
@@ -432,29 +437,33 @@
     high_ref[...], low_ref[...] = split2(chain)
 
 
-def mid_kernel(z, fields_ref, basis_ref, transfer_ref, acc_in, acc, weights):
-    rank, rhs = z.rank, z.rhs
-    row = lax.broadcasted_iota(jnp.int32, (rhs + rank, rank), 0)
-    column = lax.broadcasted_iota(jnp.int32, (rhs + rank, rank), 1)
-    path = jnp.where(row - rhs == column, 1.0, 0.0)
-    none = jnp.zeros((rank, rank), f32)
-    path = matmul(path, transfer_ref[z.nodes - 1], 1, 1)
-    paths = [path + jnp.concatenate([fields_ref[:, (z.nodes - 1) * rank : z.nodes * rank], none], axis=0)]
-    none = jnp.zeros((rank, 2 * rank), f32)
+def weights_kernel(z, basis_ref, transfer_ref, weights):
+    rank = z.rank
+    paths = [jnp.transpose(transfer_ref[z.nodes - 1])]
     for level in range(z.levels - 2, -1, -1):
         below = []
         for i, path in enumerate(paths):
             node = z.offsets[level] + 2 * i
             both = matmul(path, transfer_ref[node : node + 2].reshape(2 * rank, rank), 1, 1)
-            both += jnp.concatenate([fields_ref[:, node * rank : (node + 2) * rank], none], axis=0)
             below += [both[:, :rank], both[:, rank:]]
         paths = below
     for leaf in range(z.leaves):
-        values = matmul(paths[leaf], basis_ref[leaf])
-        acc[leaf] += values[:rhs]
-        high, low = split2(values[rhs:])
-        weights[0, leaf] = high
-        weights[1, leaf] = low
+        weights[0, leaf], weights[1, leaf] = split2(matmul(paths[leaf], basis_ref[leaf]))
+
+
+def mid_kernel(z, fields_ref, basis_ref, transfer_ref, acc_in, acc):
+    rank = z.rank
+    paths = [fields_ref[:, (z.nodes - 1) * rank : z.nodes * rank]]
+    for level in range(z.levels - 2, -1, -1):
+        below = []
+        for i, path in enumerate(paths):
+            node = z.offsets[level] + 2 * i
+            both = matmul(path, transfer_ref[node : node + 2].reshape(2 * rank, rank), 1, 1)
+            both += fields_ref[:, node * rank : (node + 2) * rank]
+            below += [both[:, :rank], both[:, rank:]]
+        paths = below
+    for leaf in range(z.leaves):
+        acc[leaf] += matmul(paths[leaf], basis_ref[leaf])
 
 
 def final_kernel(z, bounds_ref, upper_ref, acc, weights, matrix_ref, *rest):
@@ -647,8 +656,12 @@
             level.append(received[at : at + size])
             at += size
         partial = partial + received[at:]
-    for bit in range(z.top):
+    order = [0]
+    for bit in reversed(range(z.top)):
         partial = jnp.concatenate([partial, flip(partial, "group", 1 << bit)], axis=0)
+        order += [place ^ 1 << bit for place in order]
+    places = [order.index(place) for place in range(z.group)]
+    partial = jnp.concatenate([partial[i : i + 1] for i in places], axis=0)
     tables = [jnp.concatenate(level, axis=0) for level in whole_levels] + [partial]
 
     def near(index, acc, more=()):
@@ -672,12 +685,20 @@
         cost=0.5,
     )
     acc = near(len(NEAR_CUTS), acc, halo_tables)
+    fields, target_rows, named = call(
+        part(inner_kernel, z),
+        [shape(z.rhs, z.packed), halfs(FEATURES, z.packed), Vector(integers(z.slots, z.packed))],
+        [where],
+        [inter_list, inter_count, own],
+        cost=1.0,
+    )
     fields = call(
-        part(local_kernel, z),
+        part(outer_kernel, z),
         shape(z.rhs, z.packed),
-        [bounds],
-        [inter_list, inter_count, own, from_partner, from_other],
-        cost=1.5,
+        [where],
+        [from_partner, from_other, target_rows, named, fields],
+        aliases={5: 0},
+        cost=0.8,
     )
     chain = call(
         part(top_kernel, z),
@@ -686,13 +707,16 @@
         [upper_skeleton, matrices],
         cost=0.6,
     )
-    acc, weights = call(
+    weights = call(
+        part(weights_kernel, z), halfs(2, z.leaves, z.rank, z.leaf), [], [basis, transfer], cost=0.8
+    )
+    acc = call(
         part(mid_kernel, z),
-        [shape(z.leaves, z.rhs, z.leaf), halfs(2, z.leaves, z.rank, z.leaf)],
+        shape(z.leaves, z.rhs, z.leaf),
         [],
         [fields, basis, transfer, acc],
         aliases={3: 0},
-        cost=1.0,
+        cost=0.6,
     )
     return call(
         part(final_kernel, z),

time: 35.1 us -> 35 us (level)
  Pallas kernels: 13 us -> 14.1 us
  starting transfers between devices: 16.4 us -> 15.7 us
  waiting for transfers between devices: 5.32 us -> 4.88 us
    pallas_call x13 -> x15, Pallas kernels: 13 us -> 14.1 us  [call(): pl.pallas_call(body, out_shape=shapes if many else shapes[0], in_specs=[S...]
    ppermute x6, starting transfers between devices: 15.7 us -> 15 us  [flip(): lax.ppermute(x, axis, [(i, i ^ bit) for i in range(lax.axis_size(axis))])]
    ppermute x6, waiting for transfers between devices: 5.32 us -> 4.88 us  [flip(): lax.ppermute(x, axis, [(i, i ^ bit) for i in range(lax.axis_size(axis))])]
  transfers between devices with their start and end apart: 7 -> 7, of which waited for: 4 -> 4; matrix products, arithmetic and copies ran while one was open for 0% -> 0% of each run, Pallas kernels for 16% -> 22%
where the time goes in v5:
time: 35 us; the launch traced here: 34.8 us
  starting transfers between devices  15.7 us (45%)
  Pallas kernels  14.1 us (40%)
  waiting for transfers between devices  4.88 us (14%)
    ppermute x6, starting transfers between devices, flip(): lax.ppermute(x, axis, [(i, i ^ bit) for i in range(lax.axis_size(axis))])  15 us
    pallas_call x15, Pallas kernels, call(): pl.pallas_call(body, out_shape=shapes if many else shapes[0], in_specs=[S...  14.1 us
    ppermute x6, waiting for transfers between devices, flip(): lax.ppermute(x, axis, [(i, i ^ bit) for i in range(lax.axis_size(axis))])  4.88 us
  transfers between devices with their start and end apart: 7, of which 4 were waited for; matrix products, arithmetic and copies ran while one was open for 0% of the time, Pallas kernels for 22%

profile of v5, /device:TPU:0, one launch (start us, length us, event | category | flops | bytes accessed | tf_op | source)
XLA Modules:
  0.0 34.8 jit_solution(17133482431779670110)
XLA Ops:
  0.0 2.4 %shard_map.127 = (f32[40,1536]{1,0:T(8,128)S(1)}, f32[40,1536]{1,0:T(8,128)S(1)}, f32[40,1024]{1,0:T(8,128)S(1)}, f32[32,64]{1,0:T(8,128)S(1)}, s32[1]{0:T(128)S...) custom-call(s32[8,8]{1,0:T(8,128)} %near_list_in.1, ...), custom_call_target="tpu_custom_call" | custom-call | flops 200000000 | bytes 6000000 | tf_op jit(solution)/shard_map/pallas_call | solution.py:532
  2.4 0.6 %collective-permute-start = (f32[40,1536]{1,0:T(8,128)S(1)}, f32[40,1536]{1,0:T(8,128)S(1)}, u32[]{:S(2)}, u32[]{:S(2)}) collective-permute-start(f32[40,1536]{1,0:T(8,128)S(1)} %get-tuple-element.44), channel_id=1, source_target_pairs={{0,1},{1,0},{2,3},{3,2},{4,5},{5,4},{6,7},{7,6},{8,9},{9,8},{10,11... | collective-permute-start | bytes 737288 | tf_op jit(solution)/shard_map/ppermute | solution.py:547
  3.0 0.7 %collective-permute-start.1 = (f32[40,1536]{1,0:T(8,128)S(1)}, f32[40,1536]{1,0:T(8,128)S(1)}, u32[]{:S(2)}, u32[]{:S(2)}) collective-permute-start(f32[40,1536]{1,0:T(8,128)S(1)} %get-tuple-element.45), channel_id=1, source_target_pairs={{1,2},{3,4},{5,6},{7,8},{9,10},{11,12},{13,14},{15,16},{17,18},{19... | collective-permute-start | bytes 737288 | tf_op jit(solution)/shard_map/ppermute | solution.py:645
  3.6 4.0 %collective-permute-start.2 = (f32[32,64]{1,0:T(8,128)S(1)}, f32[32,64]{1,0:T(8,128)S(1)}, u32[]{:S(2)}, u32[]{:S(2)}) collective-permute-start(f32[32,64]{1,0:T(8,128)S(1)} %get-tuple-element.65.term_ref), channel_id=1, source_target_pairs={{0,1},{1,0},{2,3},{3,2},{4,5},{5,4},{6,7},{7,6},{8,9},{9,8},{10,11... | collective-permute-start | bytes 24584 | tf_op jit(solution)/shard_map/ppermute | solution.py:547
  7.6 0.3 shard_map.131
  8.0 0.4 %shard_map.128 = (s32[88]{0:T(128)S(4)}, s32[80]{0:T(128)S(4)}, s32[3]{0:T(128)S(4)}, s32[32]{0:T(128)S(4)}) custom-call(s32[1]{0:T(128)S(4)} %get-tuple-element.37.where_ref, s32[8,8]{1,0:T(8,128)S(4)} %get-tuple-element.38.near_list, s32[8]{0:T(128)S(4)} %get-tuple-element.39.near_count, s32[8,32]{1,0:T(8,128)S(4)} %get-tuple-element.40.upper_list, ...), custom_call_target="tpu_custom_call" | custom-call | flops 70000000 | bytes 2100000 | tf_op jit(solution)/shard_map/pallas_call | solution.py:532
  8.4 1.0 %shard_map.133.rest_0_ = f32[8,32,256]{2,1,0:T(8,128)S(1)} custom-call(s32[88]{0:T(128)S(4)} %get-tuple-element.54.items_ref, s32[80]{0:T(128)S(4)} %get-tuple-element.55.halo_ref, s32[3]{0:T(128)S(4)} %get-tuple-element.42.bounds_ref, bf16[8,48,256]{2,1,0:T(8,128)(2,1)S(1)} %get-tuple-element.58.tgt, ...), custom_call_target="tpu_custom_call", output_to_operand_aliasing={{}: (6, {})} | custom-call | flops 200000000 | bytes 6000000 | tf_op jit(solution)/shard_map/pallas_call | solution.py:532
  9.4 0.0 collective-permute-done.2.a_ref
  9.4 0.3 shard_map.139
  9.6 1.6 %collective-permute-start.3 = (f32[3,32,64]{2,1,0:T(8,128)S(1)}, f32[3,32,64]{2,1,0:T(8,128)S(1)}, u32[]{:S(2)}, u32[]{:S(2)}) collective-permute-start(f32[3,32,64]{2,1,0:T(8,128)S(1)} %shard_map.139), channel_id=1, source_target_pairs={{0,2},{1,3},{2,0},{3,1},{4,6},{5,7},{6,4},{7,5},{8,10},{9,11},{10,... | collective-permute-start | bytes 73736 | tf_op jit(solution)/shard_map/ppermute | solution.py:547
  11.2 1.0 %shard_map.138.weights = bf16[2,8,64,256]{3,2,1,0:T(8,128)(2,1)S(1)} custom-call(f32[8,64,256]{2,1,0:T(8,128)S(1)} %get-tuple-element.52.basis_ref, f32[15,64,64]{2,1,0:T(8,128)S(1)} %get-tuple-element.53.transfer_ref), custom_call_target="tpu_custom_call" | custom-call | flops 80000000 | bytes 2400000 | tf_op jit(solution)/shard_map/pallas_call | solution.py:532
  12.2 2.0 %shard_map.134.rest_0_ = f32[8,32,256]{2,1,0:T(8,128)S(1)} custom-call(s32[88]{0:T(128)S(4)} %get-tuple-element.54.items_ref, s32[80]{0:T(128)S(4)} %get-tuple-element.55.halo_ref, s32[3]{0:T(128)S(4)} %get-tuple-element.42.bounds_ref, bf16[8,48,256]{2,1,0:T(8,128)(2,1)S(1)} %get-tuple-element.58.tgt, ...), custom_call_target="tpu_custom_call", output_to_operand_aliasing={{}: (6, {})} | custom-call | flops 200000000 | bytes 6000000 | tf_op jit(solution)/shard_map/pallas_call | solution.py:532
  14.2 0.2 collective-permute-done.3
  14.4 4.1 %collective-permute-start.4 = (f32[4,32,64]{2,1,0:T(8,128)S(1)}, f32[4,32,64]{2,1,0:T(8,128)S(1)}, u32[]{:S(2)}, u32[]{:S(2)}) collective-permute-start(f32[4,32,64]{2,1,0:T(8,128)S(1)} %pad_maximum_fusion), channel_id=1, source_target_pairs={{0,4},{1,5},{2,6},{3,7},{4,0},{5,1},{6,2},{7,3},{8,12},{9,13},{10,... | collective-permute-start | bytes 98312 | tf_op jit(solution)/shard_map/ppermute | solution.py:547
  18.5 0.8 %shard_map.140 = (bf16[64,512]{1,0:T(8,128)(2,1)S(1)}, bf16[64,512]{1,0:T(8,128)(2,1)S(1)}) custom-call(s32[3]{0:T(128)S(4)} %get-tuple-element.42.bounds_ref, s32[32]{0:T(128)S(4)} %get-tuple-element.43.upper_ref, f32[3,32,64]{2,1,0:T(8,128)S(1)} %get-tuple-element.66.skel_ref, f32[6,64,64]{2,1,0:T(8,128)S(1)} %get-tuple-element.64.matrix_ref), custom_call_target="tpu_custom_call" | custom-call | flops 60000000 | bytes 1800000 | tf_op jit(solution)/shard_map/pallas_call | solution.py:532
  19.3 0.9 %shard_map.129 = (f32[32,1024]{1,0:T(8,128)S(1)}, bf16[48,1024]{1,0:T(8,128)(2,1)S(1)}, s32[8,1024]{1,0:T(8,128)S(1)}) custom-call(s32[1]{0:T(128)S(4)} %get-tuple-element.37.where_ref, s32[8,15]{1,0:T(8,128)S(1)} %get-tuple-element.46.list_ref, s32[1,15]{1,0:T(1,128)S(1)} %get-tuple-element.47.count_ref, f32[40,1024]{1,0:T(8,128)S(1)} %get-tuple-element.48.own_ref), custom_call_target="tpu_custom_call" | custom-call | flops 100000000 | bytes 3000000 | tf_op jit(solution)/shard_map/pallas_call | solution.py:532
  20.2 1.0 %shard_map.135.rest_2_ = f32[8,32,256]{2,1,0:T(8,128)S(1)} custom-call(s32[88]{0:T(128)S(4)} %get-tuple-element.54.items_ref, s32[80]{0:T(128)S(4)} %get-tuple-element.55.halo_ref, s32[3]{0:T(128)S(4)} %get-tuple-element.42.bounds_ref, bf16[8,48,256]{2,1,0:T(8,128)(2,1)S(1)} %get-tuple-element.58.tgt, ...), custom_call_target="tpu_custom_call", output_to_operand_aliasing={{}: (6, {})} | custom-call | flops 200000000 | bytes 6000000 | tf_op jit(solution)/shard_map/pallas_call | solution.py:532
  21.2 0.2 collective-permute-done.4
  21.4 3.7 %collective-permute-start.5 = (f32[1,32,64]{2,1,0:T(8,128)S(1)}, f32[1,32,64]{2,1,0:T(8,128)S(1)}, u32[]{:S(2)}, u32[]{:S(2)}) collective-permute-start(f32[1,32,64]{2,1,0:T(8,128)S(1)} %get-tuple-element.69), channel_id=1, source_target_pairs={{0,16},{8,24},{16,0},{24,8},{1,17},{9,25},{17,1},{25,9},{2,18},{10... | collective-permute-start | bytes 24584 | tf_op jit(solution)/shard_map/ppermute | solution.py:547
  25.1 1.7 %collective-permute-done.5 = f32[1,32,64]{2,1,0:T(8,128)S(1)} collective-permute-done((f32[1,32,64]{2,1,0:T(8,128)S(1)}, f32[1,32,64]{2,1,0:T(8,128)S(1)}, u32[]{:S(2)}, u32[]{:S(2)}) %collective-permute-start.5) | collective-permute-done | bytes 8224 | tf_op jit(solution)/shard_map/ppermute | solution.py:547
  26.8 1.1 %collective-permute-start.6 = (f32[2,32,64]{2,1,0:T(8,128)S(1)}, f32[2,32,64]{2,1,0:T(8,128)S(1)}, u32[]{:S(2)}, u32[]{:S(2)}) collective-permute-start(f32[2,32,64]{2,1,0:T(8,128)S(1)} %pad_maximum_fusion.5), channel_id=1, source_target_pairs={{0,8},{8,0},{16,24},{24,16},{1,9},{9,1},{17,25},{25,17},{2,10},{10... | collective-permute-start | bytes 49160 | tf_op jit(solution)/shard_map/ppermute | solution.py:547
  27.9 2.8 %collective-permute-done.6 = f32[2,32,64]{2,1,0:T(8,128)S(1)} collective-permute-done((f32[2,32,64]{2,1,0:T(8,128)S(1)}, f32[2,32,64]{2,1,0:T(8,128)S(1)}, u32[]{:S(2)}, u32[]{:S(2)}) %collective-permute-start.6) | collective-permute-done | bytes 16416 | tf_op jit(solution)/shard_map/ppermute | solution.py:547
  30.7 0.0 collective-permute-done.a_ref
  30.7 0.0 collective-permute-done.1.b_ref
  30.8 0.3 shard_map.132
  31.1 0.5 %shard_map.136.acc_in = f32[8,32,256]{2,1,0:T(8,128)S(1)} custom-call(s32[88]{0:T(128)S(4)} %get-tuple-element.54.items_ref, s32[80]{0:T(128)S(4)} %get-tuple-element.55.halo_ref, s32[3]{0:T(128)S(4)} %get-tuple-element.42.bounds_ref, bf16[8,48,256]{2,1,0:T(8,128)(2,1)S(1)} %get-tuple-element.58.tgt, ...), custom_call_target="tpu_custom_call", output_to_operand_aliasing={{}: (8, {})} | custom-call | flops 200000000 | bytes 6000000 | tf_op jit(solution)/shard_map/pallas_call | solution.py:532
  31.6 1.1 %shard_map.130.fields_ref = f32[32,1024]{1,0:T(8,128)S(1)} custom-call(s32[1]{0:T(128)S(4)} %get-tuple-element.37.where_ref, f32[40,1536]{1,0:T(8,128)S(1)} %collective-permute-done.a_ref, f32[40,1536]{1,0:T(8,128)S(1)} %collective-permute-done.1.b_ref, bf16[48,1024]{1,0:T(8,128)(2,1)S(1)} %get-tuple-element.49.target_ref, ...), custom_call_target="tpu_custom_call", output_to_operand_aliasing={{}: (5, {})} | custom-call | flops 80000000 | bytes 2400000 | tf_op jit(solution)/shard_map/pallas_call | solution.py:532
  32.7 0.9 %shard_map.137.acc = f32[8,32,256]{2,1,0:T(8,128)S(1)} custom-call(f32[32,1024]{1,0:T(8,128)S(1)} %shard_map.130.fields_ref, f32[8,64,256]{2,1,0:T(8,128)S(1)} %get-tuple-element.52.basis_ref, f32[15,64,64]{2,1,0:T(8,128)S(1)} %get-tuple-element.53.transfer_ref, f32[8,32,256]{2,1,0:T(8,128)S(1)} %shard_map.136.acc_in), custom_call_target="tpu_custom_call", output_to_operand_aliasing={{}: (3, {})} | custom-call | flops 60000000 | bytes 1800000 | tf_op jit(solution)/shard_map/pallas_call | solution.py:532
  33.5 1.3 %shard_map.141 = f32[32,2048]{1,0:T(8,128)} custom-call(s32[3]{0:T(128)S(4)} %get-tuple-element.42.bounds_ref, s32[32]{0:T(128)S(4)} %get-tuple-element.43.upper_ref, f32[8,32,256]{2,1,0:T(8,128)S(1)} %shard_map.137.acc, bf16[2,8,64,256]{3,2,1,0:T(8,128)(2,1)S(1)} %shard_map.138.weights, f32[6,64,64]{2,1,0:T(8,128)S(1)} %get-tuple-element.64.matrix_ref, ...), custom_call_target="tpu_custom_call" | custom-call | flops 100000000 | bytes 3000000 | tf_op jit(solution)/shard_map/pallas_call | solution.py:532
  (11 shorter events, 0.1 us)
Async XLA Ops:
  2.4 28.3 %collective-permute-start = (f32[40,1536]{1,0:T(8,128)S(1)}, f32[40,1536]{1,0:T(8,128)S(1)}, u32[]{:S(2)}, u32[]{:S(2)}) collective-permute-start(f32[40,1536]{1,0:T(8,128)S(1)} %get-tuple-element.44), channel_id=1, source_target_pairs={{0,1},{1,0},{2,3},{3,2},{4,5},{5,4},{6,7},{7,6},{8,9},{9,8},{10,11... | collective-permute-start | bytes 737288 | tf_op jit(solution)/shard_map/ppermute | solution.py:547
  3.0 27.8 %collective-permute-start.1 = (f32[40,1536]{1,0:T(8,128)S(1)}, f32[40,1536]{1,0:T(8,128)S(1)}, u32[]{:S(2)}, u32[]{:S(2)}) collective-permute-start(f32[40,1536]{1,0:T(8,128)S(1)} %get-tuple-element.45), channel_id=1, source_target_pairs={{1,2},{3,4},{5,6},{7,8},{9,10},{11,12},{13,14},{15,16},{17,18},{19... | collective-permute-start | bytes 737288 | tf_op jit(solution)/shard_map/ppermute | solution.py:645
  3.6 5.7 %collective-permute-start.2 = (f32[32,64]{1,0:T(8,128)S(1)}, f32[32,64]{1,0:T(8,128)S(1)}, u32[]{:S(2)}, u32[]{:S(2)}) collective-permute-start(f32[32,64]{1,0:T(8,128)S(1)} %get-tuple-element.65.term_ref), channel_id=1, source_target_pairs={{0,1},{1,0},{2,3},{3,2},{4,5},{5,4},{6,7},{7,6},{8,9},{9,8},{10,11... | collective-permute-start | bytes 24584 | tf_op jit(solution)/shard_map/ppermute | solution.py:547
  9.6 4.7 %collective-permute-start.3 = (f32[3,32,64]{2,1,0:T(8,128)S(1)}, f32[3,32,64]{2,1,0:T(8,128)S(1)}, u32[]{:S(2)}, u32[]{:S(2)}) collective-permute-start(f32[3,32,64]{2,1,0:T(8,128)S(1)} %shard_map.139), channel_id=1, source_target_pairs={{0,2},{1,3},{2,0},{3,1},{4,6},{5,7},{6,4},{7,5},{8,10},{9,11},{10,... | collective-permute-start | bytes 73736 | tf_op jit(solution)/shard_map/ppermute | solution.py:547
  14.4 7.0 %collective-permute-start.4 = (f32[4,32,64]{2,1,0:T(8,128)S(1)}, f32[4,32,64]{2,1,0:T(8,128)S(1)}, u32[]{:S(2)}, u32[]{:S(2)}) collective-permute-start(f32[4,32,64]{2,1,0:T(8,128)S(1)} %pad_maximum_fusion), channel_id=1, source_target_pairs={{0,4},{1,5},{2,6},{3,7},{4,0},{5,1},{6,2},{7,3},{8,12},{9,13},{10,... | collective-permute-start | bytes 98312 | tf_op jit(solution)/shard_map/ppermute | solution.py:547
  21.4 5.4 %collective-permute-start.5 = (f32[1,32,64]{2,1,0:T(8,128)S(1)}, f32[1,32,64]{2,1,0:T(8,128)S(1)}, u32[]{:S(2)}, u32[]{:S(2)}) collective-permute-start(f32[1,32,64]{2,1,0:T(8,128)S(1)} %get-tuple-element.69), channel_id=1, source_target_pairs={{0,16},{8,24},{16,0},{24,8},{1,17},{9,25},{17,1},{25,9},{2,18},{10... | collective-permute-start | bytes 24584 | tf_op jit(solution)/shard_map/ppermute | solution.py:547
  26.8 3.9 %collective-permute-start.6 = (f32[2,32,64]{2,1,0:T(8,128)S(1)}, f32[2,32,64]{2,1,0:T(8,128)S(1)}, u32[]{:S(2)}, u32[]{:S(2)}) collective-permute-start(f32[2,32,64]{2,1,0:T(8,128)S(1)} %pad_maximum_fusion.5), channel_id=1, source_target_pairs={{0,8},{8,0},{16,24},{24,16},{1,9},{9,1},{17,25},{25,17},{2,10},{10... | collective-permute-start | bytes 49160 | tf_op jit(solution)/shard_map/ppermute | solution.py:547
